TPU v7x, 32 devices: a whole 2x2x4 slice. The times are simulated.
32 devices in a mesh: group: 1, expert: 16 (over z, y, x), dp: 2 (over core).
Axes of the slice: x: 2, y: 2, z: 4, core: 2. Of those that a mesh axis runs over, the one named last changes fastest.
Arguments:
- tokens: bfloat16 [2048, 4096], P(('group', 'expert', 'dp')), may hold values from -6 to 6
- queries: bfloat16 [2048, 4096], P(('group', 'expert', 'dp')), may hold values from -6 to 6
- keys_local: bfloat16 [2048, 256], P(('group', 'expert', 'dp')), may hold values from -6 to 6
- values_local: bfloat16 [2048, 256], P(('group', 'expert', 'dp')), may hold values from -6 to 6
- prompt_keys: bfloat16 [1024, 256], P('group'), may hold values from -6 to 6
- prompt_values: bfloat16 [1024, 256], P('group'), may hold values from -6 to 6
- norm_gain: float32 [4096], replicated, may hold values from 0.25 to 1.75
- expert_ids: int32 [2048, 8], P(('group', 'expert', 'dp')), may hold values from 0 to 15, all different within a row; in each aligned block of 64 rows (0 to 63, 64 to 127, ...) at most 42 rows name the same one
- route_weight: float32 [2048, 8], P(('group', 'expert', 'dp')), may hold values from 0.05 to 1
- stored_gate: bfloat16 [16, 4096, 768], P('expert', None, 'dp'), may hold values from -0.09375 to 0.09375
- stored_up: bfloat16 [16, 4096, 768], P('expert', None, 'dp'), may hold values from -0.09375 to 0.09375
- stored_down: bfloat16 [16, 768, 4096], P('expert', 'dp'), may hold values from -0.21875 to 0.21875
- holder: int32 [16], replicated, may hold values from 0 to 15, as said below
Outputs:
- layer_out: bfloat16 [2048, 4096], P(('group', 'expert', 'dp'))
Inputs may be any that keep to these rules, and one draw needn't show every extreme that they name: `expert_ids`: each row names 8 different experts. In the 64 rows of one device no expert is named more than 42 times, and in every draw some expert is named exactly 42 times in some device's rows. holder[s] is s or the slot 8 away (s + 16 / 2 modulo 16), holder[holder[s]] = s, and holder[0] = 8.
All inputs are finite; a program needn't handle non-finite values.
Results may differ from a plain program's by a relative error of at most 0.0055.
Values may be sent and summed in bfloat16 or wider, within the bound.
No kernel may reach another device: no remote copies, remote signals or barrier semaphores. Data moves between devices by JAX's collectives and lax.ppermute only.
A program may use at most 192 MiB of HBM per device.

v0:
```python
import functools

import jax
import jax.numpy as jnp
from jax import lax
from jax.experimental import pallas as pl
from jax.experimental.pallas import tpu as pltpu
from jax.sharding import PartitionSpec as P


HEADS = 32
KVH = 2
HD = 128
TOPK = 8
LANES = 128


def attend_kernel(heads, q_ref, keys_ref, values_ref, pkeys_ref, pvalues_ref, tokens_ref, out_ref):
    rows = q_ref.shape[0]
    dims = (((1,), (1,)), ((), ()))
    scale = HD ** (-0.5)
    stacked = jnp.concatenate([q_ref[:, h * HD : (h + 1) * HD] for h in range(heads)], 0)
    first = lax.dot_general(stacked, pkeys_ref[...], dims, preferred_element_type=jnp.float32)
    last = lax.dot_general(stacked, keys_ref[...], dims, preferred_element_type=jnp.float32)
    query = lax.broadcasted_iota(jnp.int32, (rows, rows), 0)
    key = lax.broadcasted_iota(jnp.int32, (rows, rows), 1)
    allowed = jnp.concatenate([key <= query] * heads, 0)
    first = first * scale
    last = jnp.where(allowed, last * scale, -jnp.inf)
    highest = jnp.maximum(
        jnp.max(first, axis=-1, keepdims=True), jnp.max(last, axis=-1, keepdims=True)
    )
    first, last = jnp.exp(first - highest), jnp.exp(last - highest)
    total = jnp.sum(first, axis=-1, keepdims=True) + jnp.sum(last, axis=-1, keepdims=True)
    inverse = 1.0 / total
    context = jnp.dot(
        (first * inverse).astype(jnp.bfloat16), pvalues_ref[...], preferred_element_type=jnp.float32
    ) + jnp.dot(
        (last * inverse).astype(jnp.bfloat16), values_ref[...], preferred_element_type=jnp.float32
    )
    for h in range(heads):
        at = slice(h * HD, (h + 1) * HD)
        out_ref[:, at] = tokens_ref[:, at].astype(jnp.float32) + context[h * rows : (h + 1) * rows]


def attend(tokens, queries, keys_local, values_local, prompt_keys, prompt_values, heads=4):
    rows, width = tokens.shape
    prefix = prompt_keys.shape[0]
    per_key = HEADS // KVH // heads
    wide = pl.BlockSpec((rows, heads * HD), lambda i: (0, i))
    own = pl.BlockSpec((rows, HD), lambda i: (0, i // per_key))
    shared = pl.BlockSpec((prefix, HD), lambda i: (0, i // per_key))
    return pl.pallas_call(
        functools.partial(attend_kernel, heads),
        grid=(HEADS // heads,),
        out_shape=jax.ShapeDtypeStruct((rows, width), jnp.float32),
        in_specs=[wide, own, own, shared, shared, wide],
        out_specs=wide,
        compiler_params=pltpu.CompilerParams(vmem_limit_bytes=VMEM_LIMIT),
        cost_estimate=pl.CostEstimate(
            flops=4 * rows * (prefix + rows) * width,
            bytes_accessed=8 * rows * width,
            transcendentals=rows * (prefix + rows) * HEADS,
        ),
        name="attend",
    )(queries, keys_local, values_local, prompt_keys, prompt_values, tokens)


def payload_kernel(experts, holder_ref, tokens_ref, gain_ref, ids_ref, route_ref, out_ref):
    rows, width = tokens_ref.shape
    wide = tokens_ref[...].astype(jnp.float32)
    scale = lax.rsqrt(jnp.mean(wide * wide, axis=-1, keepdims=True) + 1e-06)
    out_ref[:, :width] = (wide * scale * gain_ref[...]).astype(jnp.bfloat16)
    extra = out_ref.shape[1] - width
    part = lax.broadcasted_iota(jnp.int32, (extra, rows), 0)
    slot = part % experts
    held = jnp.zeros((extra, rows), jnp.int32)
    for i in range(experts):
        held = jnp.where(slot == i, holder_ref[i], held)
    route = route_ref[...]
    share = route / jnp.sum(route, axis=0, keepdims=True)
    per_slot = jnp.zeros((extra, rows), jnp.float32)
    for k in range(ids_ref.shape[0]):
        per_slot += jnp.where(ids_ref[k : k + 1] == held, share[k : k + 1], 0.0)
    high = per_slot.astype(jnp.bfloat16).astype(jnp.float32)
    both = jnp.where(part < experts, high, jnp.where(part < 2 * experts, per_slot - high, 0.0))
    same = lax.broadcasted_iota(jnp.int32, (rows, rows), 0) == lax.broadcasted_iota(
        jnp.int32, (rows, rows), 1
    )
    turned = lax.dot_general(
        same.astype(jnp.bfloat16),
        both.astype(jnp.bfloat16),
        (((1,), (1,)), ((), ())),
        preferred_element_type=jnp.float32,
    )
    out_ref[:, width:] = turned.astype(jnp.bfloat16)


def make_payload(tokens, norm_gain, expert_ids, route_weight, holder):
    rows, width = tokens.shape
    experts = holder.shape[0]
    extra = -(-2 * experts // LANES) * LANES
    vmem = pl.BlockSpec(memory_space=pltpu.VMEM)
    return pl.pallas_call(
        functools.partial(payload_kernel, experts),
        out_shape=jax.ShapeDtypeStruct((rows, width + extra), jnp.bfloat16),
        in_specs=[pl.BlockSpec(memory_space=pltpu.SMEM)] + [vmem] * 4,
        out_specs=vmem,
        name="payload",
    )(holder, tokens, norm_gain.reshape(1, -1), expert_ids.T, route_weight.T)


PLANE = 4
CHUNK = 1024
SLICE = 128
VMEM_LIMIT = 60 * 2**20


def capacity(tokens, owners):
    return min(tokens, max(2, tokens * TOPK * 4 // (3 * owners)))


def chunks(width):
    return [slice(at, min(at + CHUNK, width)) for at in range(0, width, CHUNK)]


def dispatch_kernel(slot_ref, base_ref, *outs):
    tokens, padded = base_ref.shape
    count = outs[0].shape[0]
    width = padded - padded % CHUNK
    extra = padded - width
    row = lax.broadcasted_iota(jnp.int32, (tokens, tokens), 0)
    column = lax.broadcasted_iota(jnp.int32, (tokens, tokens), 1)
    turned = lax.dot_general(
        base_ref[:, width:],
        (row == column).astype(jnp.bfloat16),
        (((0,), (0,)), ((), ())),
        preferred_element_type=jnp.float32,
    )
    part = lax.broadcasted_iota(jnp.int32, (extra, tokens), 0)
    routed = [
        jnp.sum(jnp.where(part == (slot_ref[0] ^ j), turned, 0.0), axis=0, keepdims=True) > 0.0
        for j in range(PLANE)
    ]
    ones = jnp.concatenate([r.astype(jnp.float32) for r in routed] * 2, 0).astype(jnp.bfloat16)
    place = jnp.dot(ones, (row < column).astype(jnp.bfloat16), preferred_element_type=jnp.float32)
    target = lax.broadcasted_iota(jnp.int32, (count, tokens), 0)
    chooser = jnp.concatenate(
        [
            jnp.where(
                (target == place[j : j + 1].astype(jnp.int32)) & routed[j], 1.0, 0.0
            ).astype(jnp.bfloat16)
            for j in range(PLANE)
        ],
        0,
    )
    for at in chunks(padded):
        rows = jnp.dot(chooser, base_ref[:, at], preferred_element_type=jnp.float32)
        rows = rows.astype(jnp.bfloat16)
        for j in range(PLANE):
            outs[j][:, at] = rows[j * count : (j + 1) * count]


def dispatch(slot, base, count):
    vmem = pl.BlockSpec(memory_space=pltpu.VMEM)
    tokens, padded = base.shape
    return pl.pallas_call(
        dispatch_kernel,
        out_shape=[jax.ShapeDtypeStruct((count, padded), jnp.bfloat16)] * PLANE,
        in_specs=[pl.BlockSpec(memory_space=pltpu.SMEM), vmem],
        out_specs=[vmem] * PLANE,
        cost_estimate=pl.CostEstimate(
            flops=2 * PLANE * count * tokens * padded,
            bytes_accessed=2 * (tokens + PLANE * count) * padded,
            transcendentals=0,
        ),
        name="dispatch",
    )(slot, base)


def combine_kernel(extras, slot_ref, meta_ref, *refs):
    results, terms, out_ref = refs[:PLANE], refs[PLANE : PLANE + extras], refs[-1]
    tokens, extra = meta_ref.shape
    count, width = results[0].shape
    row = lax.broadcasted_iota(jnp.int32, (tokens, tokens), 0)
    column = lax.broadcasted_iota(jnp.int32, (tokens, tokens), 1)
    lane = lax.broadcasted_iota(jnp.int32, (tokens, extra), 1)
    meta = meta_ref[...].astype(jnp.float32)
    before = (column < row).astype(jnp.bfloat16)
    target = lax.broadcasted_iota(jnp.int32, (tokens, count), 1)
    chooser = []
    for j in range(PLANE):
        routed = (
            jnp.sum(jnp.where(lane == (slot_ref[0] ^ j), meta, 0.0), axis=1, keepdims=True) > 0.0
        )
        ones = jnp.broadcast_to(jnp.where(routed, 1.0, 0.0), (tokens, count)).astype(jnp.bfloat16)
        place = jnp.dot(before, ones, preferred_element_type=jnp.float32)
        chooser.append(
            jnp.where((target == place.astype(jnp.int32)) & routed, 1.0, 0.0).astype(jnp.bfloat16)
        )
    chooser = jnp.concatenate(chooser, 1)
    for at in chunks(width):
        rows = jnp.concatenate([r[:, at] for r in results], 0)
        total = jnp.dot(chooser, rows, preferred_element_type=jnp.float32)
        for term in terms:
            total = total + term[:, at].astype(jnp.float32)
        out_ref[:, at] = total.astype(out_ref.dtype)


def combine(slot, base, results, terms, dtype):
    tokens, padded = base.shape
    count, width = results[0].shape
    extra = padded - width
    whole = lambda a: pl.BlockSpec(a.shape, lambda i: (0, 0))
    return pl.pallas_call(
        functools.partial(combine_kernel, len(terms)),
        grid=(1,),
        out_shape=jax.ShapeDtypeStruct((tokens, width), dtype),
        in_specs=[
            pl.BlockSpec(memory_space=pltpu.SMEM),
            pl.BlockSpec((tokens, extra), lambda i: (0, width // extra)),
        ]
        + [whole(a) for a in (*results, *terms)],
        out_specs=pl.BlockSpec((tokens, width), lambda i: (0, 0)),
        cost_estimate=pl.CostEstimate(
            flops=2 * PLANE * count * tokens * width,
            bytes_accessed=2 * (tokens + PLANE * count) * width,
            transcendentals=0,
        ),
        name="combine",
    )(slot, base, *results, *terms)


def ffn_kernel(counts, experts, slot_ref, *refs):
    n = len(counts)
    blocks, refs = refs[:n], refs[n:]
    weights, refs = refs[:6], refs[6:]
    outs, refs = refs[:n], refs[n:]
    rows_buf, gu_buf, down_buf, hid_buf, row_sem, gu_sem, down_sem = refs
    gate_m, up_m, down_m, gate_p, up_p, down_p = weights
    width, half = gate_m.shape
    parts = half // SLICE
    starts = [sum(counts[:i]) for i in range(n)]

    row_copies = [
        pltpu.make_async_copy(blocks[i], rows_buf.at[pl.ds(starts[i], counts[i])], row_sem.at[i])
        for i in range(n)
    ]
    gu_copies = []
    for side, pair in enumerate(((gate_m, up_m), (gate_p, up_p))):
        for s in range(parts):
            gu_copies.append(
                [
                    pltpu.make_async_copy(
                        ref.at[:, pl.ds(s * SLICE, SLICE)],
                        gu_buf.at[side * parts + s, :, pl.ds(j * SLICE, SLICE)],
                        gu_sem.at[side * parts + s, j],
                    )
                    for j, ref in enumerate(pair)
                ]
            )
    down_copies = [
        pltpu.make_async_copy(ref, down_buf.at[pl.ds(side * half, half)], down_sem.at[side])
        for side, ref in enumerate((down_m, down_p))
    ]
    for copy in row_copies:
        copy.start()
    for pair in gu_copies:
        for copy in pair:
            copy.start()
    for copy in down_copies:
        copy.start()
    for copy in row_copies:
        copy.wait()

    for s, pair in enumerate(gu_copies):
        for copy in pair:
            copy.wait()
        both = jnp.dot(rows_buf[:, :width], gu_buf[s], preferred_element_type=jnp.float32)
        gate, up = both[:, :SLICE], both[:, SLICE:]
        hid_buf[:, s * SLICE : (s + 1) * SLICE] = (
            gate / (1.0 + jnp.exp(-gate)) * up
        ).astype(jnp.bfloat16)

    extra = rows_buf.shape[1] - width
    lane = lax.broadcasted_iota(jnp.int32, (rows_buf.shape[0], extra), 1)
    mine = (lane == slot_ref[0]) | (lane == slot_ref[0] + experts)
    share = jnp.sum(
        jnp.where(mine, rows_buf[:, width:].astype(jnp.float32), 0.0), axis=-1, keepdims=True
    )
    for copy in down_copies:
        copy.wait()
    for at in chunks(width):
        result = jnp.dot(hid_buf[...], down_buf[:, at], preferred_element_type=jnp.float32)
        result = (result * share).astype(jnp.bfloat16)
        for i in range(n):
            outs[i][:, at] = result[starts[i] : starts[i] + counts[i]]


def run_ffn(slot, blocks, weights, experts):
    counts = tuple(b.shape[0] for b in blocks)
    rows, padded = sum(counts), blocks[0].shape[1]
    width, half = weights[0].shape
    anyspace = pl.BlockSpec(memory_space=pl.ANY)
    parts = 2 * half // SLICE
    return pl.pallas_call(
        functools.partial(ffn_kernel, counts, experts),
        out_shape=[jax.ShapeDtypeStruct((c, width), jnp.bfloat16) for c in counts],
        in_specs=[pl.BlockSpec(memory_space=pltpu.SMEM)] + [anyspace] * (len(blocks) + 6),
        out_specs=[pl.BlockSpec(memory_space=pltpu.VMEM)] * len(blocks),
        scratch_shapes=[
            pltpu.VMEM((rows, padded), jnp.bfloat16),
            pltpu.VMEM((parts, width, 2 * SLICE), jnp.bfloat16),
            pltpu.VMEM((2 * half, width), jnp.bfloat16),
            pltpu.VMEM((rows, 2 * half), jnp.bfloat16),
            pltpu.SemaphoreType.DMA((len(blocks),)),
            pltpu.SemaphoreType.DMA((parts, 2)),
            pltpu.SemaphoreType.DMA((2,)),
        ],
        compiler_params=pltpu.CompilerParams(vmem_limit_bytes=VMEM_LIMIT),
        cost_estimate=pl.CostEstimate(
            flops=2 * rows * width * half * 6,
            bytes_accessed=12 * width * half + 4 * rows * width,
            transcendentals=rows * half * 2,
        ),
        name="ffn",
    )(slot, *blocks, *weights)


def after(value, *others):
    return lax.optimization_barrier((value,) + others)[0]


def local(
    tokens,
    queries,
    keys_local,
    values_local,
    prompt_keys,
    prompt_values,
    norm_gain,
    expert_ids,
    route_weight,
    stored_gate,
    stored_up,
    stored_down,
    holder,
):
    owners = lax.axis_size("expert")
    experts = holder.shape[0]
    columns = owners // 4
    f32, bf16 = jnp.float32, jnp.bfloat16

    def swap(value, offset):
        return lax.ppermute(value, "expert", [(i, i ^ offset) for i in range(owners)])

    def partner(value):
        return lax.ppermute(value, "dp", [(0, 1), (1, 0)])

    own_weights = (stored_gate[0], stored_up[0], stored_down[0])
    weights = own_weights + tuple(partner(w) for w in own_weights)
    payload = make_payload(tokens, norm_gain, expert_ids, route_weight, holder)
    slot = lax.axis_index("expert").astype(jnp.int32).reshape(1)

    rows = -(-capacity(tokens.shape[0], owners) // 16) * 16
    bases, blocks, outs = {}, {}, {}

    def gather(k, base):
        bases[k] = base
        own, to_x, to_y, to_d = dispatch(slot, base, rows)
        blocks[k] = (own, swap(to_x, 1), swap(to_y, 2), swap(to_d, 3))

    def serve(k):
        own, to_x, to_y, to_d = run_ffn(slot, blocks[k], weights, experts)
        outs[k] = (own, swap(to_x, 1), swap(to_y, 2), swap(to_d, 3))

    def collect(k, terms=(), dtype=bf16):
        return combine(slot, bases[k], outs[k], terms, dtype)

    gather(0, payload)
    result = attend(tokens, queries, keys_local, values_local, prompt_keys, prompt_values)
    for first in range(0, columns, 4):
        if first == 0:
            gather(1, swap(payload, 4))
            gather(2, swap(after(payload, bases[1]), 8))
        else:
            gather(first, swap(payload, 4 * first))
            gather(first + 1, swap(payload, 4 * first + 4))
            gather(first + 2, swap(payload, 4 * first + 8))
        gather(first + 3, swap(bases[first + 2], 4))
    for k in range(columns):
        serve(k)
    sums = []
    for first in range(0, columns, 4):
        sums.append(swap(collect(first + 1), 4 * first + 4))
        passed = swap(collect(first + 3), 4)
        sums.append(swap(collect(first + 2, (passed,)), 4 * first + 8))
        if first:
            sums.append(swap(collect(first), 4 * first))
    result = collect(0, (result,), f32)
    for part in sums:
        result = result + part.astype(f32)
    return result.astype(bf16)


def solution(mesh):
    return jax.shard_map(
        local,
        mesh=mesh,
        in_specs=(
            P(("group", "expert", "dp"), None),
            P(("group", "expert", "dp"), None),
            P(("group", "expert", "dp"), None),
            P(("group", "expert", "dp"), None),
            P("group", None),
            P("group", None),
            P(),
            P(("group", "expert", "dp"), None),
            P(("group", "expert", "dp"), None),
            P("expert", None, "dp"),
            P("expert", None, "dp"),
            P("expert", "dp", None),
            P(),
        ),
        out_specs=P(("group", "expert", "dp"), None),
        check_vma=False,
    )
```

profile of v0, /device:TPU:14, one launch (start us, length us, event | category | flops | bytes accessed | tf_op | source)
XLA Modules:
  0.0 229.5 jit_solution(8707208983787810253)
XLA Ops:
  0.5 2.2 payload.1.base_ref.meta_ref
  3.1 14.6 %collective-permute-done.9.base_ref.meta_ref = bf16[64,4224]{1,0:T(8,128)(2,1)} collective-permute-done((bf16[64,4224]{1,0:T(8,128)(2,1)}, bf16[64,4224]{1,0:T(8,128)(2,1)}, u32[]{:S(2)}, u32[]{:S(2)}) %collective-permute-start.9) | collective-permute-done | bytes 540704 | tf_op jit(solution)/shard_map/ppermute | solution.py:355
  17.7 2.6 %collective-permute-start.17 = (bf16[64,4224]{1,0:T(8,128)(2,1)}, bf16[64,4224]{1,0:T(8,128)(2,1)}, u32[]{:S(2)}, u32[]{:S(2)}) collective-permute-start(bf16[64,4224]{1,0:T(8,128)(2,1)} %payload.1.base_ref.meta_ref), channel_id=1, source_target_pairs={{0,16},{2,18},{4,20},{6,22},{8,24},{10,26},{12,28},{14,30},{16,0},... | collective-permute-start | bytes 1622024 | tf_op jit(solution)/shard_map/ppermute | solution.py:355
  20.3 23.1 %collective-permute-done.17.base_ref.meta_ref = bf16[64,4224]{1,0:T(8,128)(2,1)} collective-permute-done((bf16[64,4224]{1,0:T(8,128)(2,1)}, bf16[64,4224]{1,0:T(8,128)(2,1)}, u32[]{:S(2)}, u32[]{:S(2)}) %collective-permute-start.17) | collective-permute-done | bytes 540704 | tf_op jit(solution)/shard_map/ppermute | solution.py:355
  43.4 1.4 collective-permute-start.24
  44.8 3.1 %dispatch.5 = (bf16[48,4224]{1,0:T(8,128)(2,1)}, bf16[48,4224]{1,0:T(8,128)(2,1)}, bf16[48,4224]{1,0:T(8,128)(2,1)}, bf16[48,4224]{1,0:T(8,128)(2,1)}) custom-call(s32[1]{0:T(128)} %bitcast.slot_ref, bf16[64,4224]{1,0:T(8,128)(2,1)} %collective-permute-done.9.base_ref.meta_ref), custom_call_target="tpu_custom_call" | custom-call | flops 103809024 | bytes 2162688 | tf_op jit(solution)/shard_map/dispatch/pallas_call | solution.py:167
  47.9 0.5 collective-permute-start.10
  48.4 9.5 %collective-permute-done.24.base_ref.meta_ref = bf16[64,4224]{1,0:T(8,128)(2,1)} collective-permute-done((bf16[64,4224]{1,0:T(8,128)(2,1)}, bf16[64,4224]{1,0:T(8,128)(2,1)}, u32[]{:S(2)}, u32[]{:S(2)}) %collective-permute-start.24) | collective-permute-done | bytes 540704 | tf_op jit(solution)/shard_map/ppermute | solution.py:355
  57.9 3.1 %dispatch.7 = (bf16[48,4224]{1,0:T(8,128)(2,1)}, bf16[48,4224]{1,0:T(8,128)(2,1)}, bf16[48,4224]{1,0:T(8,128)(2,1)}, bf16[48,4224]{1,0:T(8,128)(2,1)}) custom-call(s32[1]{0:T(128)} %bitcast.slot_ref, bf16[64,4224]{1,0:T(8,128)(2,1)} %collective-permute-done.24.base_ref.meta_ref), custom_call_target="tpu_custom_call" | custom-call | flops 103809024 | bytes 2162688 | tf_op jit(solution)/shard_map/dispatch/pallas_call | solution.py:167
  62.0 9.7 %collective-permute-done.25.refs_1_ = bf16[48,4224]{1,0:T(8,128)(2,1)} collective-permute-done((bf16[48,4224]{1,0:T(8,128)(2,1)}, bf16[48,4224]{1,0:T(8,128)(2,1)}, u32[]{:S(2)}, u32[]{:S(2)}) %collective-permute-start.25) | collective-permute-done | bytes 405536 | tf_op jit(solution)/shard_map/ppermute | solution.py:355
  72.2 3.1 %dispatch.6 = (bf16[48,4224]{1,0:T(8,128)(2,1)}, bf16[48,4224]{1,0:T(8,128)(2,1)}, bf16[48,4224]{1,0:T(8,128)(2,1)}, bf16[48,4224]{1,0:T(8,128)(2,1)}) custom-call(s32[1]{0:T(128)} %bitcast.slot_ref, bf16[64,4224]{1,0:T(8,128)(2,1)} %collective-permute-done.17.base_ref.meta_ref), custom_call_target="tpu_custom_call" | custom-call | flops 103809024 | bytes 2162688 | tf_op jit(solution)/shard_map/dispatch/pallas_call | solution.py:167
  75.3 1.5 collective-permute-start.11
  76.8 5.8 %collective-permute-done.27.refs_3_ = bf16[48,4224]{1,0:T(8,128)(2,1)} collective-permute-done((bf16[48,4224]{1,0:T(8,128)(2,1)}, bf16[48,4224]{1,0:T(8,128)(2,1)}, u32[]{:S(2)}, u32[]{:S(2)}) %collective-permute-start.27) | collective-permute-done | bytes 405536 | tf_op jit(solution)/shard_map/ppermute | solution.py:355
  83.1 1.5 collective-permute-start.18
  84.6 1.5 collective-permute-start.19
  86.6 14.2 %ffn.7 = (bf16[48,4096]{1,0:T(8,128)(2,1)}, bf16[48,4096]{1,0:T(8,128)(2,1)}, bf16[48,4096]{1,0:T(8,128)(2,1)}, bf16[48,4096]{1,0:T(8,128)(2,1)}) custom-call(s32[1]{0:T(128)} %bitcast.slot_ref, bf16[48,4224]{1,0:T(8,128)(2,1)} %get-tuple-element.63.refs_0_, bf16[48,4224]{1,0:T(8,128)(2,1)} %collective-permute-done.25.refs_1_, ...), custom_call_target="tpu_custom_call" | custom-call | flops 3623878656 | bytes 22020096 | tf_op jit(solution)/shard_map/ffn/pallas_call | solution.py:306
  100.8 1.5 collective-permute-done.11.refs_2_
  102.8 1.1 collective-permute-start.29
  103.9 1.9 collective-permute-start.30
  105.8 14.4 %ffn.5 = (bf16[48,4096]{1,0:T(8,128)(2,1)}, bf16[48,4096]{1,0:T(8,128)(2,1)}, bf16[48,4096]{1,0:T(8,128)(2,1)}, bf16[48,4096]{1,0:T(8,128)(2,1)}) custom-call(s32[1]{0:T(128)} %bitcast.slot_ref, bf16[48,4224]{1,0:T(8,128)(2,1)} %get-tuple-element.46.refs_0_, bf16[48,4224]{1,0:T(8,128)(2,1)} %copy-done.2, bf16[48,4224]{1,0:T(8,128)(2,1)} %collective-permute-done.11.refs_2_, ...), custom_call_target="tpu_custom_call" | custom-call | flops 3623878656 | bytes 22020096 | tf_op jit(solution)/shard_map/ffn/pallas_call | solution.py:306
  120.3 1.0 collective-permute-start.13
  121.3 0.7 collective-permute-start.14
  121.9 14.2 %ffn.6 = (bf16[48,4096]{1,0:T(8,128)(2,1)}, bf16[48,4096]{1,0:T(8,128)(2,1)}, bf16[48,4096]{1,0:T(8,128)(2,1)}, bf16[48,4096]{1,0:T(8,128)(2,1)}) custom-call(s32[1]{0:T(128)} %bitcast.slot_ref, bf16[48,4224]{1,0:T(8,128)(2,1)} %get-tuple-element.55.refs_0_, bf16[48,4224]{1,0:T(8,128)(2,1)} %copy-done.3, bf16[48,4224]{1,0:T(8,128)(2,1)} %collective-permute-done.19.refs_2_, ...), custom_call_target="tpu_custom_call" | custom-call | flops 3623878656 | bytes 22020096 | tf_op jit(solution)/shard_map/ffn/pallas_call | solution.py:306
  136.1 2.0 collective-permute-start.15
  138.1 0.9 collective-permute-start.21
  139.0 0.7 collective-permute-start.22
  139.8 2.9 %combine.6 = bf16[64,4096]{1,0:T(8,128)(2,1)} custom-call(s32[1]{0:T(128)} %bitcast.slot_ref, bf16[64,4224]{1,0:T(8,128)(2,1)} %collective-permute-done.24.base_ref.meta_ref, bf16[48,4096]{1,0:T(8,128)(2,1)} %get-tuple-element.67.refs_0_, bf16[48,4096]{1,0:T(8,128)(2,1)} %copy-done.13, bf16[48,4096]{1,0:T(8,128)(2,1)} %copy-done.16, bf16[48,4096]{1,0:T(8,128)(2,1)} %copy-done.17), custom_call_target="tpu_custom_call" | custom-call | flops 100663296 | bytes 2097152 | tf_op jit(solution)/shard_map/combine/pallas_call | solution.py:215
  142.7 3.2 %dispatch.4 = (bf16[48,4224]{1,0:T(8,128)(2,1)}, bf16[48,4224]{1,0:T(8,128)(2,1)}, bf16[48,4224]{1,0:T(8,128)(2,1)}, bf16[48,4224]{1,0:T(8,128)(2,1)}) custom-call(s32[1]{0:T(128)} %bitcast.slot_ref, bf16[64,4224]{1,0:T(8,128)(2,1)} %payload.1.base_ref.meta_ref), custom_call_target="tpu_custom_call" | custom-call | flops 103809024 | bytes 2162688 | tf_op jit(solution)/shard_map/dispatch/pallas_call | solution.py:167
  145.9 5.1 %collective-permute-done.14.refs_2_ = bf16[48,4096]{1,0:T(8,128)(2,1)S(1)} collective-permute-done((bf16[48,4096]{1,0:T(8,128)(2,1)}, bf16[48,4096]{1,0:T(8,128)(2,1)S(1)}, u32[]{:S(2)}, u32[]{:S(2)}) %collective-permute-start.14) | collective-permute-done | bytes 393248 | tf_op jit(solution)/shard_map/ppermute | solution.py:355
  151.5 0.8 copy-done.15
  152.8 3.5 %collective-permute-done.21.refs_1_ = bf16[48,4096]{1,0:T(8,128)(2,1)S(1)} collective-permute-done((bf16[48,4096]{1,0:T(8,128)(2,1)}, bf16[48,4096]{1,0:T(8,128)(2,1)S(1)}, u32[]{:S(2)}, u32[]{:S(2)}) %collective-permute-start.21) | collective-permute-done | bytes 393248 | tf_op jit(solution)/shard_map/ppermute | solution.py:355
  156.3 2.3 %collective-permute-start.2 = (bf16[48,4224]{1,0:T(8,128)(2,1)}, bf16[48,4224]{1,0:T(8,128)(2,1)S(1)}, u32[]{:S(2)}, u32[]{:S(2)}) collective-permute-start(bf16[48,4224]{1,0:T(8,128)(2,1)} %get-tuple-element.41), channel_id=1, source_target_pairs={{0,6},{2,4},{4,2},{6,0},{8,14},{10,12},{12,10},{14,8},{16,22},{18,... | collective-permute-start | bytes 1216520 | tf_op jit(solution)/shard_map/ppermute | solution.py:355
  158.6 0.8 collective-permute-done.22.refs_2_
  159.9 2.9 %combine.5 = bf16[64,4096]{1,0:T(8,128)(2,1)} custom-call(s32[1]{0:T(128)} %bitcast.slot_ref, bf16[64,4224]{1,0:T(8,128)(2,1)} %collective-permute-done.9.base_ref.meta_ref, bf16[48,4096]{1,0:T(8,128)(2,1)} %get-tuple-element.50.refs_0_, bf16[48,4096]{1,0:T(8,128)(2,1)} %copy-done.10, bf16[48,4096]{1,0:T(8,128)(2,1)} %copy-done.11, bf16[48,4096]{1,0:T(8,128)(2,1)} %copy-done.15), custom_call_target="tpu_custom_call" | custom-call | flops 100663296 | bytes 2097152 | tf_op jit(solution)/shard_map/combine/pallas_call | solution.py:215
  162.8 18.3 %collective-permute-done.23.refs_3_ = bf16[48,4096]{1,0:T(8,128)(2,1)} collective-permute-done((bf16[48,4096]{1,0:T(8,128)(2,1)}, bf16[48,4096]{1,0:T(8,128)(2,1)}, u32[]{:S(2)}, u32[]{:S(2)}) %collective-permute-start.23) | collective-permute-done | bytes 393248 | tf_op jit(solution)/shard_map/ppermute | solution.py:355
  181.3 0.8 copy-done.1
  182.1 3.0 %combine.7 = bf16[64,4096]{1,0:T(8,128)(2,1)} custom-call(s32[1]{0:T(128)} %bitcast.slot_ref, bf16[64,4224]{1,0:T(8,128)(2,1)} %collective-permute-done.17.base_ref.meta_ref, bf16[48,4096]{1,0:T(8,128)(2,1)} %get-tuple-element.59.refs_0_, bf16[48,4096]{1,0:T(8,128)(2,1)} %copy-done.12, bf16[48,4096]{1,0:T(8,128)(2,1)} %copy-done.14, ...), custom_call_target="tpu_custom_call" | custom-call | flops 100663296 | bytes 2097152 | tf_op jit(solution)/shard_map/combine/pallas_call | solution.py:215
  185.1 3.3 %collective-permute-start.32 = (bf16[64,4096]{1,0:T(8,128)(2,1)}, bf16[64,4096]{1,0:T(8,128)(2,1)S(1)}, u32[]{:S(2)}, u32[]{:S(2)}) collective-permute-start(bf16[64,4096]{1,0:T(8,128)(2,1)} %combine.7), channel_id=1, source_target_pairs={{0,16},{2,18},{4,20},{6,22},{8,24},{10,26},{12,28},{14,30},{16,0},... | collective-permute-start | bytes 1572872 | tf_op jit(solution)/shard_map/ppermute | solution.py:355
  188.5 0.7 copy-done.4
  189.5 14.2 %ffn.4 = (bf16[48,4096]{1,0:T(8,128)(2,1)}, bf16[48,4096]{1,0:T(8,128)(2,1)}, bf16[48,4096]{1,0:T(8,128)(2,1)}, bf16[48,4096]{1,0:T(8,128)(2,1)}) custom-call(s32[1]{0:T(128)} %bitcast.slot_ref, bf16[48,4224]{1,0:T(8,128)(2,1)} %get-tuple-element.38.refs_0_, bf16[48,4224]{1,0:T(8,128)(2,1)} %copy-done.4, bf16[48,4224]{1,0:T(8,128)(2,1)} %copy-done.5, ...), custom_call_target="tpu_custom_call" | custom-call | flops 3623878656 | bytes 22020096 | tf_op jit(solution)/shard_map/ffn/pallas_call | solution.py:306
  203.7 1.6 collective-permute-start.6
  205.2 1.5 collective-permute-start.7
  207.2 9.8 %attend.1.refs_4_ = f32[64,4096]{1,0:T(8,128)} custom-call(bf16[64,4096]{1,0:T(8,128)(2,1)} %q_ref.1, bf16[64,256]{1,0:T(8,128)(2,1)} %keys_ref.1, bf16[64,256]{1,0:T(8,128)(2,1)} %values_ref.1, bf16[1024,256]{1,0:T(8,128)(2,1)} %pkeys_ref.1, bf16[1024,256]{1,0:T(8,128)(2,1)} %pvalues_ref.1, bf16[64,4096]{1,0:T(8,128)(2,1)} %tokens_ref.3), custom_call_target="tpu_custom_call" | custom-call | flops 1140850688 | bytes 2097152 | tf_op jit(solution)/shard_map/attend/pallas_call | solution.py:53
  217.0 4.6 %collective-permute-done.7.refs_2_ = bf16[48,4096]{1,0:T(8,128)(2,1)S(1)} collective-permute-done((bf16[48,4096]{1,0:T(8,128)(2,1)}, bf16[48,4096]{1,0:T(8,128)(2,1)S(1)}, u32[]{:S(2)}, u32[]{:S(2)}) %collective-permute-start.7) | collective-permute-done | bytes 393248 | tf_op jit(solution)/shard_map/ppermute | solution.py:355
  221.6 1.5 collective-permute-done.8.refs_3_
  223.1 0.8 copy-done.9
  223.9 3.4 %combine.4 = f32[64,4096]{1,0:T(8,128)} custom-call(s32[1]{0:T(128)} %bitcast.slot_ref, bf16[64,4224]{1,0:T(8,128)(2,1)} %payload.1.base_ref.meta_ref, bf16[48,4096]{1,0:T(8,128)(2,1)} %get-tuple-element.42.refs_0_, bf16[48,4096]{1,0:T(8,128)(2,1)} %copy-done.7, bf16[48,4096]{1,0:T(8,128)(2,1)} %copy-done.8, bf16[48,4096]{1,0:T(8,128)(2,1)} %copy-done.9, ...), custom_call_target="tpu_custom_call" | custom-call | flops 100663296 | bytes 2097152 | tf_op jit(solution)/shard_map/combine/pallas_call | solution.py:215
  227.3 2.2 add_convert_fusion
  (69 shorter events, 6.8 us)
Async XLA Ops:
  0.0 83.1 %collective-permute-start.3 = (bf16[4096,384]{1,0:T(8,128)(2,1)}, bf16[4096,384]{1,0:T(8,128)(2,1)S(1)}, u32[]{:S(2)}, u32[]{:S(2)}) collective-permute-start(bf16[4096,384]{1,0:T(8,128)(2,1)} %bitcast.7), channel_id=1, source_target_pairs={{0,1},{1,0},{2,3},{3,2},{4,5},{5,4},{6,7},{7,6},{8,9},{9,8},{10,11... | collective-permute-start | bytes 9437192 | tf_op jit(solution)/shard_map/ppermute | solution.py:358
  0.0 84.6 %collective-permute-start.4 = (bf16[4096,384]{1,0:T(8,128)(2,1)}, bf16[4096,384]{1,0:T(8,128)(2,1)}, u32[]{:S(2)}, u32[]{:S(2)}) collective-permute-start(bf16[4096,384]{1,0:T(8,128)(2,1)} %bitcast.12), channel_id=1, source_target_pairs={{0,1},{1,0},{2,3},{3,2},{4,5},{5,4},{6,7},{7,6},{8,9},{9,8},{10,11... | collective-permute-start | bytes 9437192 | tf_op jit(solution)/shard_map/ppermute | solution.py:358
  0.5 85.7 %collective-permute-start.5 = (bf16[384,4096]{1,0:T(8,128)(2,1)}, bf16[384,4096]{1,0:T(8,128)(2,1)}, u32[]{:S(2)}, u32[]{:S(2)}) collective-permute-start(bf16[384,4096]{1,0:T(8,128)(2,1)} %bitcast.17), channel_id=1, source_target_pairs={{0,1},{1,0},{2,3},{3,2},{4,5},{5,4},{6,7},{7,6},{8,9},{9,8},{10,11... | collective-permute-start | bytes 9437192 | tf_op jit(solution)/shard_map/ppermute | solution.py:358
  2.7 15.0 %collective-permute-start.9 = (bf16[64,4224]{1,0:T(8,128)(2,1)}, bf16[64,4224]{1,0:T(8,128)(2,1)}, u32[]{:S(2)}, u32[]{:S(2)}) collective-permute-start(bf16[64,4224]{1,0:T(8,128)(2,1)} %payload.1.base_ref.meta_ref), channel_id=1, source_target_pairs={{0,8},{2,10},{4,12},{6,14},{8,0},{10,2},{12,4},{14,6},{16,24},{18,... | collective-permute-start | bytes 1622024 | tf_op jit(solution)/shard_map/ppermute | solution.py:355
  17.7 25.7 %collective-permute-start.17 = (bf16[64,4224]{1,0:T(8,128)(2,1)}, bf16[64,4224]{1,0:T(8,128)(2,1)}, u32[]{:S(2)}, u32[]{:S(2)}) collective-permute-start(bf16[64,4224]{1,0:T(8,128)(2,1)} %payload.1.base_ref.meta_ref), channel_id=1, source_target_pairs={{0,16},{2,18},{4,20},{6,22},{8,24},{10,26},{12,28},{14,30},{16,0},... | collective-permute-start | bytes 1622024 | tf_op jit(solution)/shard_map/ppermute | solution.py:355
  43.4 14.5 %collective-permute-start.24 = (bf16[64,4224]{1,0:T(8,128)(2,1)}, bf16[64,4224]{1,0:T(8,128)(2,1)}, u32[]{:S(2)}, u32[]{:S(2)}) collective-permute-start(bf16[64,4224]{1,0:T(8,128)(2,1)} %collective-permute-done.17.base_ref.meta_ref), channel_id=1, source_target_pairs={{0,8},{2,10},{4,12},{6,14},{8,0},{10,2},{12,4},{14,6},{16,24},{18,... | collective-permute-start | bytes 1622024 | tf_op jit(solution)/shard_map/ppermute | solution.py:355
  47.9 13.7 %collective-permute-start.10 = (bf16[48,4224]{1,0:T(8,128)(2,1)}, bf16[48,4224]{1,0:T(8,128)(2,1)S(1)}, u32[]{:S(2)}, u32[]{:S(2)}) collective-permute-start(bf16[48,4224]{1,0:T(8,128)(2,1)} %get-tuple-element.47), channel_id=1, source_target_pairs={{0,2},{2,0},{4,6},{6,4},{8,10},{10,8},{12,14},{14,12},{16,18},{18,... | collective-permute-start | bytes 1216520 | tf_op jit(solution)/shard_map/ppermute | solution.py:355
  61.0 10.8 %collective-permute-start.25 = (bf16[48,4224]{1,0:T(8,128)(2,1)}, bf16[48,4224]{1,0:T(8,128)(2,1)}, u32[]{:S(2)}, u32[]{:S(2)}) collective-permute-start(bf16[48,4224]{1,0:T(8,128)(2,1)} %get-tuple-element.64), channel_id=1, source_target_pairs={{0,2},{2,0},{4,6},{6,4},{8,10},{10,8},{12,14},{14,12},{16,18},{18,... | collective-permute-start | bytes 1216520 | tf_op jit(solution)/shard_map/ppermute | solution.py:355
  61.5 39.3 %copy-start.2 = (bf16[48,4224]{1,0:T(8,128)(2,1)}, bf16[48,4224]{1,0:T(8,128)(2,1)S(1)}, u32[]{:S(2)}) copy-start(bf16[48,4224]{1,0:T(8,128)(2,1)S(1)} %collective-permute-done.10.refs_1_) | copy-start | bytes 1216516
  61.5 13.8 %collective-permute-start.26 = (bf16[48,4224]{1,0:T(8,128)(2,1)}, bf16[48,4224]{1,0:T(8,128)(2,1)}, u32[]{:S(2)}, u32[]{:S(2)}) collective-permute-start(bf16[48,4224]{1,0:T(8,128)(2,1)} %get-tuple-element.65), channel_id=1, source_target_pairs={{0,4},{2,6},{4,0},{6,2},{8,12},{10,14},{12,8},{14,10},{16,20},{18,... | collective-permute-start | bytes 1216520 | tf_op jit(solution)/shard_map/ppermute | solution.py:355
  71.8 10.9 %collective-permute-start.27 = (bf16[48,4224]{1,0:T(8,128)(2,1)}, bf16[48,4224]{1,0:T(8,128)(2,1)}, u32[]{:S(2)}, u32[]{:S(2)}) collective-permute-start(bf16[48,4224]{1,0:T(8,128)(2,1)} %get-tuple-element.66), channel_id=1, source_target_pairs={{0,6},{2,4},{4,2},{6,0},{8,14},{10,12},{12,10},{14,8},{16,22},{18,... | collective-permute-start | bytes 1216520 | tf_op jit(solution)/shard_map/ppermute | solution.py:355
  75.3 27.0 %collective-permute-start.11 = (bf16[48,4224]{1,0:T(8,128)(2,1)}, bf16[48,4224]{1,0:T(8,128)(2,1)}, u32[]{:S(2)}, u32[]{:S(2)}) collective-permute-start(bf16[48,4224]{1,0:T(8,128)(2,1)} %get-tuple-element.48), channel_id=1, source_target_pairs={{0,4},{2,6},{4,0},{6,2},{8,12},{10,14},{12,8},{14,10},{16,20},{18,... | collective-permute-start | bytes 1216520 | tf_op jit(solution)/shard_map/ppermute | solution.py:355
  82.7 20.2 %collective-permute-start.12 = (bf16[48,4224]{1,0:T(8,128)(2,1)}, bf16[48,4224]{1,0:T(8,128)(2,1)}, u32[]{:S(2)}, u32[]{:S(2)}) collective-permute-start(bf16[48,4224]{1,0:T(8,128)(2,1)} %get-tuple-element.49), channel_id=1, source_target_pairs={{0,6},{2,4},{4,2},{6,0},{8,14},{10,12},{12,10},{14,8},{16,22},{18,... | collective-permute-start | bytes 1216520 | tf_op jit(solution)/shard_map/ppermute | solution.py:355
  83.1 3.5 %copy-start = (bf16[4096,384]{1,0:T(8,128)(2,1)}, bf16[4096,384]{1,0:T(8,128)(2,1)S(1)}, u32[]{:S(2)}) copy-start(bf16[4096,384]{1,0:T(8,128)(2,1)S(1)} %collective-permute-done.3.refs_7_) | copy-start | bytes 9437188
  83.1 20.8 %collective-permute-start.18 = (bf16[48,4224]{1,0:T(8,128)(2,1)}, bf16[48,4224]{1,0:T(8,128)(2,1)S(1)}, u32[]{:S(2)}, u32[]{:S(2)}) collective-permute-start(bf16[48,4224]{1,0:T(8,128)(2,1)} %get-tuple-element.56), channel_id=1, source_target_pairs={{0,2},{2,0},{4,6},{6,4},{8,10},{10,8},{12,14},{14,12},{16,18},{18,... | collective-permute-start | bytes 1216520 | tf_op jit(solution)/shard_map/ppermute | solution.py:355
  84.6 35.6 %collective-permute-start.19 = (bf16[48,4224]{1,0:T(8,128)(2,1)}, bf16[48,4224]{1,0:T(8,128)(2,1)}, u32[]{:S(2)}, u32[]{:S(2)}) collective-permute-start(bf16[48,4224]{1,0:T(8,128)(2,1)} %get-tuple-element.57), channel_id=1, source_target_pairs={{0,4},{2,6},{4,0},{6,2},{8,12},{10,14},{12,8},{14,10},{16,20},{18,... | collective-permute-start | bytes 1216520 | tf_op jit(solution)/shard_map/ppermute | solution.py:355
  86.2 35.1 %collective-permute-start.20 = (bf16[48,4224]{1,0:T(8,128)(2,1)}, bf16[48,4224]{1,0:T(8,128)(2,1)}, u32[]{:S(2)}, u32[]{:S(2)}) collective-permute-start(bf16[48,4224]{1,0:T(8,128)(2,1)} %get-tuple-element.58), channel_id=1, source_target_pairs={{0,6},{2,4},{4,2},{6,0},{8,14},{10,12},{12,10},{14,8},{16,22},{18,... | collective-permute-start | bytes 1216520 | tf_op jit(solution)/shard_map/ppermute | solution.py:355
  102.3 33.8 %collective-permute-start.28 = (bf16[48,4096]{1,0:T(8,128)(2,1)}, bf16[48,4096]{1,0:T(8,128)(2,1)S(1)}, u32[]{:S(2)}, u32[]{:S(2)}) collective-permute-start(bf16[48,4096]{1,0:T(8,128)(2,1)} %get-tuple-element.68), channel_id=1, source_target_pairs={{0,2},{2,0},{4,6},{6,4},{8,10},{10,8},{12,14},{14,12},{16,18},{18,... | collective-permute-start | bytes 1179656 | tf_op jit(solution)/shard_map/ppermute | solution.py:355
  102.8 35.2 %collective-permute-start.29 = (bf16[48,4096]{1,0:T(8,128)(2,1)}, bf16[48,4096]{1,0:T(8,128)(2,1)S(1)}, u32[]{:S(2)}, u32[]{:S(2)}) collective-permute-start(bf16[48,4096]{1,0:T(8,128)(2,1)} %get-tuple-element.69), channel_id=1, source_target_pairs={{0,4},{2,6},{4,0},{6,2},{8,12},{10,14},{12,8},{14,10},{16,20},{18,... | collective-permute-start | bytes 1179656 | tf_op jit(solution)/shard_map/ppermute | solution.py:355
  103.9 16.3 %copy-start.3 = (bf16[48,4224]{1,0:T(8,128)(2,1)}, bf16[48,4224]{1,0:T(8,128)(2,1)S(1)}, u32[]{:S(2)}) copy-start(bf16[48,4224]{1,0:T(8,128)(2,1)S(1)} %collective-permute-done.18.refs_1_) | copy-start | bytes 1216516
  103.9 35.1 %collective-permute-start.30 = (bf16[48,4096]{1,0:T(8,128)(2,1)}, bf16[48,4096]{1,0:T(8,128)(2,1)S(1)}, u32[]{:S(2)}, u32[]{:S(2)}) collective-permute-start(bf16[48,4096]{1,0:T(8,128)(2,1)} %get-tuple-element.70), channel_id=1, source_target_pairs={{0,6},{2,4},{4,2},{6,0},{8,14},{10,12},{12,10},{14,8},{16,22},{18,... | collective-permute-start | bytes 1179656 | tf_op jit(solution)/shard_map/ppermute | solution.py:355
  120.3 22.4 %collective-permute-start.13 = (bf16[48,4096]{1,0:T(8,128)(2,1)}, bf16[48,4096]{1,0:T(8,128)(2,1)S(1)}, u32[]{:S(2)}, u32[]{:S(2)}) collective-permute-start(bf16[48,4096]{1,0:T(8,128)(2,1)} %get-tuple-element.51), channel_id=1, source_target_pairs={{0,2},{2,0},{4,6},{6,4},{8,10},{10,8},{12,14},{14,12},{16,18},{18,... | collective-permute-start | bytes 1179656 | tf_op jit(solution)/shard_map/ppermute | solution.py:355
  121.3 29.8 %collective-permute-start.14 = (bf16[48,4096]{1,0:T(8,128)(2,1)}, bf16[48,4096]{1,0:T(8,128)(2,1)S(1)}, u32[]{:S(2)}, u32[]{:S(2)}) collective-permute-start(bf16[48,4096]{1,0:T(8,128)(2,1)} %get-tuple-element.52), channel_id=1, source_target_pairs={{0,4},{2,6},{4,0},{6,2},{8,12},{10,14},{12,8},{14,10},{16,20},{18,... | collective-permute-start | bytes 1179656 | tf_op jit(solution)/shard_map/ppermute | solution.py:355
  136.1 3.6 %copy-start.13 = (bf16[48,4096]{1,0:T(8,128)(2,1)}, bf16[48,4096]{1,0:T(8,128)(2,1)S(1)}, u32[]{:S(2)}) copy-start(bf16[48,4096]{1,0:T(8,128)(2,1)S(1)} %collective-permute-done.28.refs_1_) | copy-start | bytes 1179652
  136.1 15.4 %collective-permute-start.15 = (bf16[48,4096]{1,0:T(8,128)(2,1)}, bf16[48,4096]{1,0:T(8,128)(2,1)S(1)}, u32[]{:S(2)}, u32[]{:S(2)}) collective-permute-start(bf16[48,4096]{1,0:T(8,128)(2,1)} %get-tuple-element.53), channel_id=1, source_target_pairs={{0,6},{2,4},{4,2},{6,0},{8,14},{10,12},{12,10},{14,8},{16,22},{18,... | collective-permute-start | bytes 1179656 | tf_op jit(solution)/shard_map/ppermute | solution.py:355
  138.1 1.6 copy-start.16
  138.1 18.3 %collective-permute-start.21 = (bf16[48,4096]{1,0:T(8,128)(2,1)}, bf16[48,4096]{1,0:T(8,128)(2,1)S(1)}, u32[]{:S(2)}, u32[]{:S(2)}) collective-permute-start(bf16[48,4096]{1,0:T(8,128)(2,1)} %get-tuple-element.60), channel_id=1, source_target_pairs={{0,2},{2,0},{4,6},{6,4},{8,10},{10,8},{12,14},{14,12},{16,18},{18,... | collective-permute-start | bytes 1179656 | tf_op jit(solution)/shard_map/ppermute | solution.py:355
  139.0 0.8 copy-start.17
  139.0 20.4 %collective-permute-start.22 = (bf16[48,4096]{1,0:T(8,128)(2,1)}, bf16[48,4096]{1,0:T(8,128)(2,1)S(1)}, u32[]{:S(2)}, u32[]{:S(2)}) collective-permute-start(bf16[48,4096]{1,0:T(8,128)(2,1)} %get-tuple-element.61), channel_id=1, source_target_pairs={{0,4},{2,6},{4,0},{6,2},{8,12},{10,14},{12,8},{14,10},{16,20},{18,... | collective-permute-start | bytes 1179656 | tf_op jit(solution)/shard_map/ppermute | solution.py:355
  142.6 17.3 %copy-start.10 = (bf16[48,4096]{1,0:T(8,128)(2,1)}, bf16[48,4096]{1,0:T(8,128)(2,1)S(1)}, u32[]{:S(2)}) copy-start(bf16[48,4096]{1,0:T(8,128)(2,1)S(1)} %collective-permute-done.13.refs_1_) | copy-start | bytes 1179652
  142.6 38.7 %collective-permute-start.31 = (bf16[64,4096]{1,0:T(8,128)(2,1)}, bf16[64,4096]{1,0:T(8,128)(2,1)S(1)}, u32[]{:S(2)}, u32[]{:S(2)}) collective-permute-start(bf16[64,4096]{1,0:T(8,128)(2,1)} %combine.6), channel_id=1, source_target_pairs={{0,8},{2,10},{4,12},{6,14},{8,0},{10,2},{12,4},{14,6},{16,24},{18,... | collective-permute-start | bytes 1572872 | tf_op jit(solution)/shard_map/ppermute | solution.py:355
  151.0 8.9 %copy-start.11 = (bf16[48,4096]{1,0:T(8,128)(2,1)}, bf16[48,4096]{1,0:T(8,128)(2,1)S(1)}, u32[]{:S(2)}) copy-start(bf16[48,4096]{1,0:T(8,128)(2,1)S(1)} %collective-permute-done.14.refs_2_) | copy-start | bytes 1179652
  151.0 37.5 %collective-permute-start = (bf16[48,4224]{1,0:T(8,128)(2,1)}, bf16[48,4224]{1,0:T(8,128)(2,1)S(1)}, u32[]{:S(2)}, u32[]{:S(2)}) collective-permute-start(bf16[48,4224]{1,0:T(8,128)(2,1)} %get-tuple-element.39), channel_id=1, source_target_pairs={{0,2},{2,0},{4,6},{6,4},{8,10},{10,8},{12,14},{14,12},{16,18},{18,... | collective-permute-start | bytes 1216520 | tf_op jit(solution)/shard_map/ppermute | solution.py:355
  152.3 36.2 %collective-permute-start.1 = (bf16[48,4224]{1,0:T(8,128)(2,1)}, bf16[48,4224]{1,0:T(8,128)(2,1)S(1)}, u32[]{:S(2)}, u32[]{:S(2)}) collective-permute-start(bf16[48,4224]{1,0:T(8,128)(2,1)} %get-tuple-element.40), channel_id=1, source_target_pairs={{0,4},{2,6},{4,0},{6,2},{8,12},{10,14},{12,8},{14,10},{16,20},{18,... | collective-permute-start | bytes 1216520 | tf_op jit(solution)/shard_map/ppermute | solution.py:355
  156.3 25.0 %copy-start.12 = (bf16[48,4096]{1,0:T(8,128)(2,1)}, bf16[48,4096]{1,0:T(8,128)(2,1)S(1)}, u32[]{:S(2)}) copy-start(bf16[48,4096]{1,0:T(8,128)(2,1)S(1)} %collective-permute-done.21.refs_1_) | copy-start | bytes 1179652
  156.3 32.2 %collective-permute-start.2 = (bf16[48,4224]{1,0:T(8,128)(2,1)}, bf16[48,4224]{1,0:T(8,128)(2,1)S(1)}, u32[]{:S(2)}, u32[]{:S(2)}) collective-permute-start(bf16[48,4224]{1,0:T(8,128)(2,1)} %get-tuple-element.41), channel_id=1, source_target_pairs={{0,6},{2,4},{4,2},{6,0},{8,14},{10,12},{12,10},{14,8},{16,22},{18,... | collective-permute-start | bytes 1216520 | tf_op jit(solution)/shard_map/ppermute | solution.py:355
  159.4 21.9 %copy-start.14 = (bf16[48,4096]{1,0:T(8,128)(2,1)}, bf16[48,4096]{1,0:T(8,128)(2,1)S(1)}, u32[]{:S(2)}) copy-start(bf16[48,4096]{1,0:T(8,128)(2,1)S(1)} %collective-permute-done.22.refs_2_) | copy-start | bytes 1179652
  159.4 21.6 %collective-permute-start.23 = (bf16[48,4096]{1,0:T(8,128)(2,1)}, bf16[48,4096]{1,0:T(8,128)(2,1)}, u32[]{:S(2)}, u32[]{:S(2)}) collective-permute-start(bf16[48,4096]{1,0:T(8,128)(2,1)} %get-tuple-element.62), channel_id=1, source_target_pairs={{0,6},{2,4},{4,2},{6,0},{8,14},{10,12},{12,10},{14,8},{16,22},{18,... | collective-permute-start | bytes 1179656 | tf_op jit(solution)/shard_map/ppermute | solution.py:355
  181.0 46.2 %collective-permute-start.16 = (bf16[64,4096]{1,0:T(8,128)(2,1)}, bf16[64,4096]{1,0:T(8,128)(2,1)S(1)}, u32[]{:S(2)}, u32[]{:S(2)}) collective-permute-start(bf16[64,4096]{1,0:T(8,128)(2,1)} %combine.5), channel_id=1, source_target_pairs={{0,8},{2,10},{4,12},{6,14},{8,0},{10,2},{12,4},{14,6},{16,24},{18,... | collective-permute-start | bytes 1572872 | tf_op jit(solution)/shard_map/ppermute | solution.py:355
  181.3 0.8 copy-start.1
  185.1 42.2 %collective-permute-start.32 = (bf16[64,4096]{1,0:T(8,128)(2,1)}, bf16[64,4096]{1,0:T(8,128)(2,1)S(1)}, u32[]{:S(2)}, u32[]{:S(2)}) collective-permute-start(bf16[64,4096]{1,0:T(8,128)(2,1)} %combine.7), channel_id=1, source_target_pairs={{0,16},{2,18},{4,20},{6,22},{8,24},{10,26},{12,28},{14,30},{16,0},... | collective-permute-start | bytes 1572872 | tf_op jit(solution)/shard_map/ppermute | solution.py:355
  188.5 0.9 copy-start.5
  188.5 1.0 copy-start.6
  203.7 13.3 %collective-permute-start.6 = (bf16[48,4096]{1,0:T(8,128)(2,1)}, bf16[48,4096]{1,0:T(8,128)(2,1)S(1)}, u32[]{:S(2)}, u32[]{:S(2)}) collective-permute-start(bf16[48,4096]{1,0:T(8,128)(2,1)} %get-tuple-element.43), channel_id=1, source_target_pairs={{0,2},{2,0},{4,6},{6,4},{8,10},{10,8},{12,14},{14,12},{16,18},{18,... | collective-permute-start | bytes 1179656 | tf_op jit(solution)/shard_map/ppermute | solution.py:355
  205.2 16.4 %collective-permute-start.7 = (bf16[48,4096]{1,0:T(8,128)(2,1)}, bf16[48,4096]{1,0:T(8,128)(2,1)S(1)}, u32[]{:S(2)}, u32[]{:S(2)}) collective-permute-start(bf16[48,4096]{1,0:T(8,128)(2,1)} %get-tuple-element.44), channel_id=1, source_target_pairs={{0,4},{2,6},{4,0},{6,2},{8,12},{10,14},{12,8},{14,10},{16,20},{18,... | collective-permute-start | bytes 1179656 | tf_op jit(solution)/shard_map/ppermute | solution.py:355
  206.8 16.4 %collective-permute-start.8 = (bf16[48,4096]{1,0:T(8,128)(2,1)}, bf16[48,4096]{1,0:T(8,128)(2,1)S(1)}, u32[]{:S(2)}, u32[]{:S(2)}) collective-permute-start(bf16[48,4096]{1,0:T(8,128)(2,1)} %get-tuple-element.45), channel_id=1, source_target_pairs={{0,6},{2,4},{4,2},{6,0},{8,14},{10,12},{12,10},{14,8},{16,22},{18,... | collective-permute-start | bytes 1179656 | tf_op jit(solution)/shard_map/ppermute | solution.py:355
  217.0 6.1 %copy-start.7 = (bf16[48,4096]{1,0:T(8,128)(2,1)}, bf16[48,4096]{1,0:T(8,128)(2,1)S(1)}, u32[]{:S(2)}) copy-start(bf16[48,4096]{1,0:T(8,128)(2,1)S(1)} %collective-permute-done.6.refs_1_) | copy-start | bytes 1179652
  221.6 1.5 copy-start.8
  (3 other events, 2.3 us)
where the time goes:
time: 234 us; the launch traced here: 229 us
  waiting for transfers between devices  98 us (42%)
  Pallas kernels  93.4 us (40%)
  starting transfers between devices  32.2 us (14%)
  local copies, waits for them, and re-layouts  3.47 us (1%)
    ppermute x30, waiting for transfers between devices, swap(): lax.ppermute(value, 'expert', [(i, i ^ offset) for i in range(owners)])  98 us
    pallas_call x4, Pallas kernels, run_ffn(): pl.pallas_call(functools.partial(ffn_kernel, counts, experts), out_shape=...  56.9 us
    ppermute x30, starting transfers between devices, swap(): lax.ppermute(value, 'expert', [(i, i ^ offset) for i in range(owners)])  31.7 us
    pallas_call x4, Pallas kernels, dispatch(): pl.pallas_call(dispatch_kernel, out_shape=[jax.ShapeDtypeStruct((count, p...  12.5 us
    pallas_call x4, Pallas kernels, combine(): pl.pallas_call(functools.partial(combine_kernel, len(terms)), grid=(1,),...  12.1 us
    pallas_call x1, Pallas kernels, attend(): pl.pallas_call(functools.partial(attend_kernel, heads), grid=(HEADS // he...  9.79 us
  transfers between devices with their start and end apart: 33, of which 12 were waited for; matrix products, arithmetic and copies ran while one was open for 0% of the time, Pallas kernels for 41%

commit v1 on v0

v1 whole, which is shorter than its diff:
```python
import functools

import jax
import jax.numpy as jnp
from jax import lax
from jax.experimental import pallas as pl
from jax.experimental.pallas import tpu as pltpu
from jax.sharding import PartitionSpec as P


HEADS = 32
KVH = 2
HD = 128
TOPK = 8
LANES = 128


def attend_kernel(heads, q_ref, keys_ref, values_ref, pkeys_ref, pvalues_ref, tokens_ref, out_ref):
    rows = q_ref.shape[0]
    dims = (((1,), (1,)), ((), ()))
    scale = HD ** (-0.5)
    stacked = jnp.concatenate([q_ref[:, h * HD : (h + 1) * HD] for h in range(heads)], 0)
    first = lax.dot_general(stacked, pkeys_ref[...], dims, preferred_element_type=jnp.float32)
    last = lax.dot_general(stacked, keys_ref[...], dims, preferred_element_type=jnp.float32)
    query = lax.broadcasted_iota(jnp.int32, (rows, rows), 0)
    key = lax.broadcasted_iota(jnp.int32, (rows, rows), 1)
    allowed = jnp.concatenate([key <= query] * heads, 0)
    first = first * scale
    last = jnp.where(allowed, last * scale, -jnp.inf)
    highest = jnp.maximum(
        jnp.max(first, axis=-1, keepdims=True), jnp.max(last, axis=-1, keepdims=True)
    )
    first, last = jnp.exp(first - highest), jnp.exp(last - highest)
    total = jnp.sum(first, axis=-1, keepdims=True) + jnp.sum(last, axis=-1, keepdims=True)
    inverse = 1.0 / total
    context = jnp.dot(
        (first * inverse).astype(jnp.bfloat16), pvalues_ref[...], preferred_element_type=jnp.float32
    ) + jnp.dot(
        (last * inverse).astype(jnp.bfloat16), values_ref[...], preferred_element_type=jnp.float32
    )
    for h in range(heads):
        at = slice(h * HD, (h + 1) * HD)
        out_ref[:, at] = tokens_ref[:, at].astype(jnp.float32) + context[h * rows : (h + 1) * rows]


def attend(tokens, queries, keys_local, values_local, prompt_keys, prompt_values, heads=4):
    rows, width = tokens.shape
    prefix = prompt_keys.shape[0]
    per_key = HEADS // KVH // heads
    wide = pl.BlockSpec((rows, heads * HD), lambda i: (0, i))
    own = pl.BlockSpec((rows, HD), lambda i: (0, i // per_key))
    shared = pl.BlockSpec((prefix, HD), lambda i: (0, i // per_key))
    return pl.pallas_call(
        functools.partial(attend_kernel, heads),
        grid=(HEADS // heads,),
        out_shape=jax.ShapeDtypeStruct((rows, width), jnp.float32),
        in_specs=[wide, own, own, shared, shared, wide],
        out_specs=wide,
        compiler_params=pltpu.CompilerParams(vmem_limit_bytes=24 * 2**20),
        cost_estimate=pl.CostEstimate(
            flops=4 * rows * (prefix + rows) * width,
            bytes_accessed=8 * rows * width,
            transcendentals=rows * (prefix + rows) * HEADS,
        ),
        name="attend",
    )(queries, keys_local, values_local, prompt_keys, prompt_values, tokens)


PLANE = 4
CHUNK = 1024
SUB = 8
SMALL = 16 * 2**20
LARGE = 60 * 2**20


def capacity(tokens, owners):
    return min(tokens, max(2, tokens * TOPK * 4 // (3 * owners)))


def packing(count, width):
    full = count // SUB * SUB
    left = count - full
    pieces = left * (width // CHUNK)
    columns = -(-pieces // (full // SUB)) * LANES
    return full, left, columns


def place_of(piece, full, width):
    high, wide = divmod(piece, full // SUB)
    return slice(wide * SUB, wide * SUB + SUB), slice(width + high * LANES, width + (high + 1) * LANES)


def chunks(width):
    return [slice(at, at + CHUNK) for at in range(0, width, CHUNK)]


def pack(out_ref, rows, at, count, width):
    full, left, _ = packing(count, width)
    out_ref[:, at] = rows[:full].astype(jnp.bfloat16)
    for q in range(left):
        line = rows[full + q : full + q + 1]
        tile = jnp.concatenate([line[:, c : c + LANES] for c in range(0, CHUNK, LANES)], 0)
        piece = q * (width // CHUNK) + at.start // CHUNK
        sub, lane = place_of(piece, full, width)
        out_ref[sub, lane] = tile.astype(jnp.bfloat16)


def unpack(ref, at, count, width):
    full, left, _ = packing(count, width)
    rows = ref[:, at].astype(jnp.float32)
    if not left:
        return rows
    lines = [rows]
    for q in range(left):
        piece = q * (width // CHUNK) + at.start // CHUNK
        sub, lane = place_of(piece, full, width)
        tile = ref[sub, lane].astype(jnp.float32)
        lines.append(jnp.concatenate([tile[c : c + 1] for c in range(SUB)], 1))
    lines.append(jnp.zeros((SUB - left, CHUNK), jnp.float32))
    return jnp.concatenate(lines, 0)


def padded_rows(count):
    return -(-count // SUB) * SUB


def choose(count, slot_ref, base_ref, outs):
    tokens, padded = base_ref.shape
    width = padded // CHUNK * CHUNK
    extra = padded - width
    size = padded_rows(count)
    row = lax.broadcasted_iota(jnp.int32, (tokens, tokens), 0)
    column = lax.broadcasted_iota(jnp.int32, (tokens, tokens), 1)
    turned = lax.dot_general(
        base_ref[:, width:],
        (row == column).astype(jnp.bfloat16),
        (((0,), (0,)), ((), ())),
        preferred_element_type=jnp.float32,
    )
    part = lax.broadcasted_iota(jnp.int32, (extra, tokens), 0)
    routed = [
        jnp.sum(jnp.where(part == (slot_ref[0] ^ j), turned, 0.0), axis=0, keepdims=True) > 0.0
        for j in range(PLANE)
    ]
    ones = jnp.concatenate([r.astype(jnp.float32) for r in routed] * 2, 0).astype(jnp.bfloat16)
    place = jnp.dot(ones, (row < column).astype(jnp.bfloat16), preferred_element_type=jnp.float32)
    target = lax.broadcasted_iota(jnp.int32, (size, tokens), 0)
    chooser = jnp.concatenate(
        [
            jnp.where(
                (target == place[j : j + 1].astype(jnp.int32)) & routed[j], 1.0, 0.0
            ).astype(jnp.bfloat16)
            for j in range(PLANE)
        ],
        0,
    )
    for at in chunks(width):
        rows = jnp.dot(chooser, base_ref[:, at], preferred_element_type=jnp.float32)
        for j in range(PLANE):
            pack(outs[j], rows[j * size : (j + 1) * size], at, count, width)


def clear(outs, count, width):
    full, left, columns = packing(count, width)
    pieces = left * (width // CHUNK)
    for piece in range(pieces, columns // LANES * (full // SUB)):
        sub, lane = place_of(piece, full, width)
        for out in outs:
            out[sub, lane] = jnp.zeros((SUB, LANES), jnp.bfloat16)


def payload_kernel(
    experts, count, slot_ref, holder_ref, tokens_ref, gain_ref, ids_ref, route_ref, out_ref, *outs
):
    rows, width = tokens_ref.shape
    wide = tokens_ref[...].astype(jnp.float32)
    scale = lax.rsqrt(jnp.mean(wide * wide, axis=-1, keepdims=True) + 1e-06)
    out_ref[:, :width] = (wide * scale * gain_ref[...]).astype(jnp.bfloat16)
    extra = out_ref.shape[1] - width
    part = lax.broadcasted_iota(jnp.int32, (extra, rows), 0)
    slot = part % experts
    held = jnp.zeros((extra, rows), jnp.int32)
    for i in range(experts):
        held = jnp.where(slot == i, holder_ref[i], held)
    route = route_ref[...]
    share = route / jnp.sum(route, axis=0, keepdims=True)
    per_slot = jnp.zeros((extra, rows), jnp.float32)
    for k in range(ids_ref.shape[0]):
        per_slot += jnp.where(ids_ref[k : k + 1] == held, share[k : k + 1], 0.0)
    high = per_slot.astype(jnp.bfloat16).astype(jnp.float32)
    both = jnp.where(part < experts, high, jnp.where(part < 2 * experts, per_slot - high, 0.0))
    same = lax.broadcasted_iota(jnp.int32, (rows, rows), 0) == lax.broadcasted_iota(
        jnp.int32, (rows, rows), 1
    )
    turned = lax.dot_general(
        same.astype(jnp.bfloat16),
        both.astype(jnp.bfloat16),
        (((1,), (1,)), ((), ())),
        preferred_element_type=jnp.float32,
    )
    out_ref[:, width:] = turned.astype(jnp.bfloat16)
    choose(count, slot_ref, out_ref, outs)
    clear(outs, count, width)


def packed_shape(count, width):
    full, _, columns = packing(count, width)
    return jax.ShapeDtypeStruct((full, width + columns), jnp.bfloat16)


def make_payload(slot, tokens, norm_gain, expert_ids, route_weight, holder, count):
    rows, width = tokens.shape
    experts = holder.shape[0]
    extra = -(-2 * experts // LANES) * LANES
    vmem = pl.BlockSpec(memory_space=pltpu.VMEM)
    outs = pl.pallas_call(
        functools.partial(payload_kernel, experts, count),
        out_shape=[jax.ShapeDtypeStruct((rows, width + extra), jnp.bfloat16)]
        + [packed_shape(count, width)] * PLANE,
        in_specs=[pl.BlockSpec(memory_space=pltpu.SMEM)] * 2 + [vmem] * 4,
        out_specs=[vmem] * (PLANE + 1),
        compiler_params=pltpu.CompilerParams(vmem_limit_bytes=LARGE),
        name="payload",
    )(slot, holder, tokens, norm_gain.reshape(1, -1), expert_ids.T, route_weight.T)
    return outs[0], outs[1:]


def dispatch_kernel(count, slot_ref, base_ref, *outs):
    choose(count, slot_ref, base_ref, outs)
    clear(outs, count, base_ref.shape[1] // CHUNK * CHUNK)


def dispatch(slot, base, count, width):
    vmem = pl.BlockSpec(memory_space=pltpu.VMEM)
    tokens, padded = base.shape
    return pl.pallas_call(
        functools.partial(dispatch_kernel, count),
        out_shape=[packed_shape(count, width)] * PLANE,
        in_specs=[pl.BlockSpec(memory_space=pltpu.SMEM), vmem],
        out_specs=[vmem] * PLANE,
        cost_estimate=pl.CostEstimate(
            flops=2 * PLANE * count * tokens * padded,
            bytes_accessed=2 * (tokens + PLANE * count) * padded,
            transcendentals=0,
        ),
        compiler_params=pltpu.CompilerParams(vmem_limit_bytes=SMALL),
        name="dispatch",
    )(slot, base)


def combine_kernel(extras, experts, count, slot_ref, meta_ref, *refs):
    results, terms, out_ref = refs[:PLANE], refs[PLANE : PLANE + extras], refs[-1]
    tokens, extra = meta_ref.shape
    width = out_ref.shape[1]
    size = padded_rows(count)
    row = lax.broadcasted_iota(jnp.int32, (tokens, tokens), 0)
    column = lax.broadcasted_iota(jnp.int32, (tokens, tokens), 1)
    lane = lax.broadcasted_iota(jnp.int32, (tokens, extra), 1)
    meta = meta_ref[...].astype(jnp.float32)
    before = (column < row).astype(jnp.bfloat16)
    target = lax.broadcasted_iota(jnp.int32, (tokens, size), 1)
    chooser, shares = [], []
    for j in range(PLANE):
        at_slot = lane == (slot_ref[0] ^ j)
        high = jnp.sum(jnp.where(at_slot, meta, 0.0), axis=1, keepdims=True)
        routed = high > 0.0
        ones = jnp.broadcast_to(jnp.where(routed, 1.0, 0.0), (tokens, size)).astype(jnp.bfloat16)
        place = jnp.dot(before, ones, preferred_element_type=jnp.float32)
        mine = jnp.where((target == place.astype(jnp.int32)) & routed, 1.0, 0.0)
        mine = mine.astype(jnp.bfloat16)
        both = jnp.where(at_slot | (lane == (slot_ref[0] ^ j) + experts), meta, 0.0)
        per_row = lax.dot_general(
            mine,
            both.astype(jnp.bfloat16),
            (((0,), (0,)), ((), ())),
            preferred_element_type=jnp.float32,
        )
        shares.append(jnp.sum(per_row, axis=1, keepdims=True))
        chooser.append(mine)
    chooser = jnp.concatenate(chooser, 1)
    shares = jnp.concatenate(shares, 0)
    for at in chunks(width):
        rows = jnp.concatenate([unpack(r, at, count, width) for r in results], 0)
        rows = (rows * shares).astype(jnp.bfloat16)
        total = jnp.dot(chooser, rows, preferred_element_type=jnp.float32)
        for term in terms:
            total = total + term[:, at].astype(jnp.float32)
        out_ref[:, at] = total.astype(out_ref.dtype)


def combine(slot, base, results, terms, dtype, experts, count, width):
    tokens, padded = base.shape
    extra = padded - width
    whole = lambda a: pl.BlockSpec(a.shape, lambda i: (0, 0))
    return pl.pallas_call(
        functools.partial(combine_kernel, len(terms), experts, count),
        grid=(1,),
        out_shape=jax.ShapeDtypeStruct((tokens, width), dtype),
        in_specs=[
            pl.BlockSpec(memory_space=pltpu.SMEM),
            pl.BlockSpec((tokens, extra), lambda i: (0, width // extra)),
        ]
        + [whole(a) for a in (*results, *terms)],
        out_specs=pl.BlockSpec((tokens, width), lambda i: (0, 0)),
        cost_estimate=pl.CostEstimate(
            flops=2 * PLANE * count * tokens * width,
            bytes_accessed=2 * (tokens + PLANE * count) * width,
            transcendentals=0,
        ),
        compiler_params=pltpu.CompilerParams(vmem_limit_bytes=SMALL),
        name="combine",
    )(slot, base, *results, *terms)


def ffn_kernel(count, *refs):
    blocks, refs = refs[:PLANE], refs[PLANE:]
    gate_m, up_m, down_m, gate_p, up_p, down_p = refs[:6]
    outs, (rows_buf, hid_buf) = refs[6 : 6 + PLANE], refs[6 + PLANE :]
    width, half = gate_m.shape
    size = padded_rows(count)
    for at in chunks(width):
        for i, block in enumerate(blocks):
            rows = unpack(block, at, count, width)
            rows_buf[i * size : (i + 1) * size, at] = rows.astype(jnp.bfloat16)
    for side, (gate_w, up_w) in enumerate(((gate_m, up_m), (gate_p, up_p))):
        gate = jnp.dot(rows_buf[...], gate_w[...], preferred_element_type=jnp.float32)
        up = jnp.dot(rows_buf[...], up_w[...], preferred_element_type=jnp.float32)
        hid_buf[:, side * half : (side + 1) * half] = (
            gate / (1.0 + jnp.exp(-gate)) * up
        ).astype(jnp.bfloat16)
    for at in chunks(width):
        result = jnp.dot(hid_buf[:, :half], down_m[:, at], preferred_element_type=jnp.float32)
        result += jnp.dot(hid_buf[:, half:], down_p[:, at], preferred_element_type=jnp.float32)
        for i in range(PLANE):
            pack(outs[i], result[i * size : (i + 1) * size], at, count, width)
    clear(outs, count, width)


def run_ffn(blocks, weights, count):
    rows = PLANE * padded_rows(count)
    width, half = weights[0].shape
    vmem = pl.BlockSpec(memory_space=pltpu.VMEM)
    return pl.pallas_call(
        functools.partial(ffn_kernel, count),
        out_shape=[packed_shape(count, width)] * PLANE,
        in_specs=[vmem] * (PLANE + 6),
        out_specs=[vmem] * PLANE,
        scratch_shapes=[
            pltpu.VMEM((rows, width), jnp.bfloat16),
            pltpu.VMEM((rows, 2 * half), jnp.bfloat16),
        ],
        compiler_params=pltpu.CompilerParams(vmem_limit_bytes=SMALL),
        cost_estimate=pl.CostEstimate(
            flops=2 * rows * width * half * 6,
            bytes_accessed=12 * width * half + 4 * rows * width,
            transcendentals=rows * half * 2,
        ),
        name="ffn",
    )(*blocks, *weights)


def after(value, *others):
    return lax.optimization_barrier((value,) + others)[0]


def local(
    tokens,
    queries,
    keys_local,
    values_local,
    prompt_keys,
    prompt_values,
    norm_gain,
    expert_ids,
    route_weight,
    stored_gate,
    stored_up,
    stored_down,
    holder,
):
    owners = lax.axis_size("expert")
    experts = holder.shape[0]
    columns = owners // 4
    f32, bf16 = jnp.float32, jnp.bfloat16

    def swap(value, offset):
        return lax.ppermute(value, "expert", [(i, i ^ offset) for i in range(owners)])

    def partner(value):
        return lax.ppermute(value, "dp", [(0, 1), (1, 0)])

    own_weights = (stored_gate[0], stored_up[0], stored_down[0])
    weights = own_weights + tuple(partner(w) for w in own_weights)
    slot = lax.axis_index("expert").astype(jnp.int32).reshape(1)
    width = tokens.shape[1]
    count = capacity(tokens.shape[0], owners)
    payload, chosen = make_payload(slot, tokens, norm_gain, expert_ids, route_weight, holder, count)
    bases, blocks, outs = {}, {}, {}

    def gather(k, base, ready=None):
        bases[k] = base
        if ready is None:
            ready = dispatch(slot, base, count, width)
        own, to_x, to_y, to_d = ready
        blocks[k] = (own, swap(to_x, 1), swap(to_y, 2), swap(to_d, 3))

    def serve(k):
        own, to_x, to_y, to_d = run_ffn(blocks[k], weights, count)
        outs[k] = (own, swap(to_x, 1), swap(to_y, 2), swap(to_d, 3))

    def collect(k, terms=(), dtype=bf16):
        return combine(slot, bases[k], outs[k], terms, dtype, experts, count, width)

    gather(0, payload, chosen)
    result = attend(tokens, queries, keys_local, values_local, prompt_keys, prompt_values)
    for first in range(0, columns, 4):
        if first == 0:
            gather(1, swap(payload, 4))
            gather(2, swap(after(payload, bases[1]), 8))
        else:
            gather(first, swap(payload, 4 * first))
            gather(first + 1, swap(payload, 4 * first + 4))
            gather(first + 2, swap(payload, 4 * first + 8))
        gather(first + 3, swap(bases[first + 2], 4))
    for k in range(columns):
        serve(k)
    sums = []
    for k in range(1, columns):
        sums.append(swap(collect(k), 4 * k))
    result = collect(0, (result,), f32)
    for part in sums:
        result = result + part.astype(f32)
    return result.astype(bf16)


def solution(mesh):
    return jax.shard_map(
        local,
        mesh=mesh,
        in_specs=(
            P(("group", "expert", "dp"), None),
            P(("group", "expert", "dp"), None),
            P(("group", "expert", "dp"), None),
            P(("group", "expert", "dp"), None),
            P("group", None),
            P("group", None),
            P(),
            P(("group", "expert", "dp"), None),
            P(("group", "expert", "dp"), None),
            P("expert", None, "dp"),
            P("expert", None, "dp"),
            P("expert", "dp", None),
            P(),
        ),
        out_specs=P(("group", "expert", "dp"), None),
        check_vma=False,
    )
```

time: 234 us -> 194 us (0.83); the launches traced: 229 us -> 192 us
  Pallas kernels: 93.4 us -> 51.8 us
  starting transfers between devices: 32.2 us -> 35.8 us
    pallas_call x13 -> x12, Pallas kernels: 83.7 us -> 43.6 us  [the longest x4 32.6 us: run_ffn(): pl.pallas_call(functools.partial(ffn_kernel, count), out_shape=[packed_sh...]
    ppermute x30, starting transfers between devices: 31.7 us -> 35.3 us  [swap(): lax.ppermute(value, 'expert', [(i, i ^ offset) for i in range(owners)])]
    unnamed x36 -> x24, local copies, waits for them, and re-layouts: 3.47 us -> 5.71 us
  transfers between devices with their start and end apart: 33 -> 33, of which waited for: 12 -> 17; matrix products, arithmetic and copies ran while one was open for 0% -> 0% of each run, Pallas kernels for 41% -> 27%
where the time goes in v1:
time: 194 us; the launch traced here: 192 us
  waiting for transfers between devices  97.4 us (50%)
  Pallas kernels  51.8 us (27%)
  starting transfers between devices  35.8 us (18%)
  local copies, waits for them, and re-layouts  5.71 us (3%)
    ppermute x30, waiting for transfers between devices, swap(): lax.ppermute(value, 'expert', [(i, i ^ offset) for i in range(owners)])  97.4 us
    ppermute x30, starting transfers between devices, swap(): lax.ppermute(value, 'expert', [(i, i ^ offset) for i in range(owners)])  35.3 us
    pallas_call x4, Pallas kernels, run_ffn(): pl.pallas_call(functools.partial(ffn_kernel, count), out_shape=[packed_sh...  32.6 us
    pallas_call x1, Pallas kernels, attend(): pl.pallas_call(functools.partial(attend_kernel, heads), grid=(HEADS // he...  8.19 us
    unnamed x24, local copies, waits for them, and re-layouts  5.71 us
    pallas_call x4, Pallas kernels, combine(): pl.pallas_call(functools.partial(combine_kernel, len(terms), experts, cou...  5.13 us
  transfers between devices with their start and end apart: 33, of which 17 were waited for; matrix products, arithmetic and copies ran while one was open for 0% of the time, Pallas kernels for 27%

profile of v1, /device:TPU:14, one launch (start us, length us, event | category | flops | bytes accessed | tf_op | source)
XLA Modules:
  0.0 191.9 jit_solution(3656183676950772692)
XLA Ops:
  0.5 3.2 %payload.1 = (bf16[64,4224]{1,0:T(8,128)(2,1)}, bf16[40,4352]{1,0:T(8,128)(2,1)}, bf16[40,4352]{1,0:T(8,128)(2,1)}, bf16[40,4352]{1,0:T(8,128)(2,1)}, bf16[40,4352]{1,0:T(8,128)(2,1)}) custom-call(s32[1]{0:T(128)} %bitcast.slot_ref, s32[16]{0:T(128)} %holder_ref.1, bf16[64,4096]{1,0:T(8,128)(2,1)} %tokens_ref.3, f32[1,4096]{1,0:T(1,128)} %bitcast.22, ...), custom_call_target="tpu_custom_call" | custom-call | tf_op jit(solution)/shard_map/payload/pallas_call | solution.py:216
  4.7 13.9 %collective-permute-done.9.base_ref.meta_ref = bf16[64,4224]{1,0:T(8,128)(2,1)S(1)} collective-permute-done((bf16[64,4224]{1,0:T(8,128)(2,1)}, bf16[64,4224]{1,0:T(8,128)(2,1)S(1)}, u32[]{:S(2)}, u32[]{:S(2)}) %collective-permute-start.9) | collective-permute-done | bytes 540704 | tf_op jit(solution)/shard_map/ppermute | solution.py:387
  18.7 2.6 %collective-permute-start.17 = (bf16[64,4224]{1,0:T(8,128)(2,1)}, bf16[64,4224]{1,0:T(8,128)(2,1)S(1)}, u32[]{:S(2)}, u32[]{:S(2)}) collective-permute-start(bf16[64,4224]{1,0:T(8,128)(2,1)} %get-tuple-element.56.meta_ref), channel_id=1, source_target_pairs={{0,16},{2,18},{4,20},{6,22},{8,24},{10,26},{12,28},{14,30},{16,0},... | collective-permute-start | bytes 1622024 | tf_op jit(solution)/shard_map/ppermute | solution.py:387
  21.3 0.9 dispatch.3
  22.2 0.6 collective-permute-start.10
  22.7 8.9 %collective-permute-done.10.refs_1_ = bf16[40,4352]{1,0:T(8,128)(2,1)S(1)} collective-permute-done((bf16[40,4352]{1,0:T(8,128)(2,1)S(1)}, bf16[40,4352]{1,0:T(8,128)(2,1)S(1)}, u32[]{:S(2)}, u32[]{:S(2)}) %collective-permute-start.10) | collective-permute-done | bytes 348192 | tf_op jit(solution)/shard_map/ppermute | solution.py:387
  32.1 12.2 %collective-permute-done.17.base_ref.meta_ref = bf16[64,4224]{1,0:T(8,128)(2,1)S(1)} collective-permute-done((bf16[64,4224]{1,0:T(8,128)(2,1)}, bf16[64,4224]{1,0:T(8,128)(2,1)S(1)}, u32[]{:S(2)}, u32[]{:S(2)}) %collective-permute-start.17) | collective-permute-done | bytes 540704 | tf_op jit(solution)/shard_map/ppermute | solution.py:387
  44.9 0.9 dispatch.4
  45.8 1.6 collective-permute-start.18
  47.3 9.0 %collective-permute-done.12.refs_3_ = bf16[40,4352]{1,0:T(8,128)(2,1)S(1)} collective-permute-done((bf16[40,4352]{1,0:T(8,128)(2,1)S(1)}, bf16[40,4352]{1,0:T(8,128)(2,1)S(1)}, u32[]{:S(2)}, u32[]{:S(2)}) %collective-permute-start.12) | collective-permute-done | bytes 348192 | tf_op jit(solution)/shard_map/ppermute | solution.py:387
  56.3 1.3 collective-permute-start.25
  57.6 4.3 %collective-permute-done.18.refs_1_ = bf16[40,4352]{1,0:T(8,128)(2,1)S(1)} collective-permute-done((bf16[40,4352]{1,0:T(8,128)(2,1)S(1)}, bf16[40,4352]{1,0:T(8,128)(2,1)S(1)}, u32[]{:S(2)}, u32[]{:S(2)}) %collective-permute-start.18) | collective-permute-done | bytes 348192 | tf_op jit(solution)/shard_map/ppermute | solution.py:387
  61.9 1.5 collective-permute-start.19
  63.4 5.3 %collective-permute-done.25.base_ref.meta_ref = bf16[64,4224]{1,0:T(8,128)(2,1)S(1)} collective-permute-done((bf16[64,4224]{1,0:T(8,128)(2,1)S(1)}, bf16[64,4224]{1,0:T(8,128)(2,1)S(1)}, u32[]{:S(2)}, u32[]{:S(2)}) %collective-permute-start.25) | collective-permute-done | bytes 540704 | tf_op jit(solution)/shard_map/ppermute | solution.py:387
  69.2 0.9 dispatch.5
  70.1 8.5 %collective-permute-done.19.refs_2_ = bf16[40,4352]{1,0:T(8,128)(2,1)S(1)} collective-permute-done((bf16[40,4352]{1,0:T(8,128)(2,1)S(1)}, bf16[40,4352]{1,0:T(8,128)(2,1)S(1)}, u32[]{:S(2)}, u32[]{:S(2)}) %collective-permute-start.19) | collective-permute-done | bytes 348192 | tf_op jit(solution)/shard_map/ppermute | solution.py:387
  78.5 1.5 collective-permute-start.1
  80.5 1.5 collective-permute-start.26
  82.0 1.5 collective-permute-start.27
  83.6 1.9 copy-done
  85.5 1.9 copy-done.2
  87.3 1.9 copy-done.3
  89.2 8.1 %ffn.5 = (bf16[40,4352]{1,0:T(8,128)(2,1)S(1)}, bf16[40,4352]{1,0:T(8,128)(2,1)S(1)}, bf16[40,4352]{1,0:T(8,128)(2,1)S(1)}, bf16[40,4352]{1,0:T(8,128)(2,1)S(1)}) custom-call(bf16[40,4352]{1,0:T(8,128)(2,1)S(1)} %get-tuple-element.48.refs_0_, bf16[40,4352]{1,0:T(8,128)(2,1)S(1)} %collective-permute-done.10.refs_1_, ...), custom_call_target="tpu_custom_call" | custom-call | flops 3623878656 | bytes 22020096 | tf_op jit(solution)/shard_map/ffn/pallas_call | solution.py:343
  97.8 8.4 %ffn.6 = (bf16[40,4352]{1,0:T(8,128)(2,1)S(1)}, bf16[40,4352]{1,0:T(8,128)(2,1)S(1)}, bf16[40,4352]{1,0:T(8,128)(2,1)S(1)}, bf16[40,4352]{1,0:T(8,128)(2,1)S(1)}) custom-call(bf16[40,4352]{1,0:T(8,128)(2,1)S(1)} %get-tuple-element.57.refs_0_, bf16[40,4352]{1,0:T(8,128)(2,1)S(1)} %collective-permute-done.18.refs_1_, ...), custom_call_target="tpu_custom_call" | custom-call | flops 3623878656 | bytes 22020096 | tf_op jit(solution)/shard_map/ffn/pallas_call | solution.py:343
  106.2 1.6 collective-permute-start.13
  107.8 1.5 collective-permute-start.14
  109.8 3.5 %collective-permute-done.27.refs_2_ = bf16[40,4352]{1,0:T(8,128)(2,1)S(1)} collective-permute-done((bf16[40,4352]{1,0:T(8,128)(2,1)S(1)}, bf16[40,4352]{1,0:T(8,128)(2,1)S(1)}, u32[]{:S(2)}, u32[]{:S(2)}) %collective-permute-start.27) | collective-permute-done | bytes 348192 | tf_op jit(solution)/shard_map/ppermute | solution.py:387
  113.6 8.1 %ffn.7 = (bf16[40,4352]{1,0:T(8,128)(2,1)S(1)}, bf16[40,4352]{1,0:T(8,128)(2,1)S(1)}, bf16[40,4352]{1,0:T(8,128)(2,1)S(1)}, bf16[40,4352]{1,0:T(8,128)(2,1)S(1)}) custom-call(bf16[40,4352]{1,0:T(8,128)(2,1)S(1)} %get-tuple-element.65.refs_0_, bf16[40,4352]{1,0:T(8,128)(2,1)S(1)} %collective-permute-done.26.refs_1_, ...), custom_call_target="tpu_custom_call" | custom-call | flops 3623878656 | bytes 22020096 | tf_op jit(solution)/shard_map/ffn/pallas_call | solution.py:343
  121.7 3.2 %collective-permute-start.23 = (bf16[40,4352]{1,0:T(8,128)(2,1)S(1)}, bf16[40,4352]{1,0:T(8,128)(2,1)S(1)}, u32[]{:S(2)}, u32[]{:S(2)}) collective-permute-start(bf16[40,4352]{1,0:T(8,128)(2,1)S(1)} %get-tuple-element.64), channel_id=1, source_target_pairs={{0,6},{2,4},{4,2},{6,0},{8,14},{10,12},{12,10},{14,8},{16,22},{18,... | collective-permute-start | bytes 1044488 | tf_op jit(solution)/shard_map/ppermute | solution.py:387
  125.0 3.2 %collective-permute-done.14.refs_2_ = bf16[40,4352]{1,0:T(8,128)(2,1)S(1)} collective-permute-done((bf16[40,4352]{1,0:T(8,128)(2,1)S(1)}, bf16[40,4352]{1,0:T(8,128)(2,1)S(1)}, u32[]{:S(2)}, u32[]{:S(2)}) %collective-permute-start.14) | collective-permute-done | bytes 348192 | tf_op jit(solution)/shard_map/ppermute | solution.py:387
  128.5 3.7 %collective-permute-done.21.refs_1_ = bf16[40,4352]{1,0:T(8,128)(2,1)S(1)} collective-permute-done((bf16[40,4352]{1,0:T(8,128)(2,1)S(1)}, bf16[40,4352]{1,0:T(8,128)(2,1)S(1)}, u32[]{:S(2)}, u32[]{:S(2)}) %collective-permute-start.21) | collective-permute-done | bytes 348192 | tf_op jit(solution)/shard_map/ppermute | solution.py:387
  132.3 2.5 %collective-permute-start.31 = (bf16[40,4352]{1,0:T(8,128)(2,1)S(1)}, bf16[40,4352]{1,0:T(8,128)(2,1)S(1)}, u32[]{:S(2)}, u32[]{:S(2)}) collective-permute-start(bf16[40,4352]{1,0:T(8,128)(2,1)S(1)} %get-tuple-element.72), channel_id=1, source_target_pairs={{0,6},{2,4},{4,2},{6,0},{8,14},{10,12},{12,10},{14,8},{16,22},{18,... | collective-permute-start | bytes 1044488 | tf_op jit(solution)/shard_map/ppermute | solution.py:387
  134.7 8.0 %ffn.4 = (bf16[40,4352]{1,0:T(8,128)(2,1)S(1)}, bf16[40,4352]{1,0:T(8,128)(2,1)S(1)}, bf16[40,4352]{1,0:T(8,128)(2,1)S(1)}, bf16[40,4352]{1,0:T(8,128)(2,1)S(1)}) custom-call(bf16[40,4352]{1,0:T(8,128)(2,1)S(1)} %copy-done.6, bf16[40,4352]{1,0:T(8,128)(2,1)S(1)} %collective-permute-done.refs_1_, bf16[40,4352]{1,0:T(8,128)(2,1)S(1)} %collective-permute-done.1.refs_2_, ...), custom_call_target="tpu_custom_call" | custom-call | flops 3623878656 | bytes 22020096 | tf_op jit(solution)/shard_map/ffn/pallas_call | solution.py:343
  143.4 1.4 combine.5
  144.9 5.2 %collective-permute-start.16 = (bf16[64,4096]{1,0:T(8,128)(2,1)S(1)}, bf16[64,4096]{1,0:T(8,128)(2,1)S(1)}, u32[]{:S(2)}, u32[]{:S(2)}) collective-permute-start(bf16[64,4096]{1,0:T(8,128)(2,1)S(1)} %combine.5), channel_id=1, source_target_pairs={{0,8},{2,10},{4,12},{6,14},{8,0},{10,2},{12,4},{14,6},{16,24},{18,... | collective-permute-start | bytes 1572872 | tf_op jit(solution)/shard_map/ppermute | solution.py:387
  150.0 1.2 combine.6
  151.4 1.5 collective-permute-done.30.refs_2_
  152.8 2.4 %collective-permute-done.31.refs_3_ = bf16[40,4352]{1,0:T(8,128)(2,1)S(1)} collective-permute-done((bf16[40,4352]{1,0:T(8,128)(2,1)S(1)}, bf16[40,4352]{1,0:T(8,128)(2,1)S(1)}, u32[]{:S(2)}, u32[]{:S(2)}) %collective-permute-start.31) | collective-permute-done | bytes 348192 | tf_op jit(solution)/shard_map/ppermute | solution.py:387
  155.3 1.2 combine.7
  156.6 0.6 collective-permute-start.7
  157.2 0.7 collective-permute-done.6.refs_1_
  157.9 3.8 %collective-permute-start.8 = (bf16[40,4352]{1,0:T(8,128)(2,1)S(1)}, bf16[40,4352]{1,0:T(8,128)(2,1)S(1)}, u32[]{:S(2)}, u32[]{:S(2)}) collective-permute-start(bf16[40,4352]{1,0:T(8,128)(2,1)S(1)} %get-tuple-element.47), channel_id=1, source_target_pairs={{0,6},{2,4},{4,2},{6,0},{8,14},{10,12},{12,10},{14,8},{16,22},{18,... | collective-permute-start | bytes 1044488 | tf_op jit(solution)/shard_map/ppermute | solution.py:387
  161.7 8.2 %attend.1.refs_4_ = f32[64,4096]{1,0:T(8,128)S(1)} custom-call(bf16[64,4096]{1,0:T(8,128)(2,1)S(1)} %copy-done.7, bf16[64,256]{1,0:T(8,128)(2,1)S(1)} %copy-done.10, bf16[64,256]{1,0:T(8,128)(2,1)S(1)} %copy-done.11, bf16[1024,256]{1,0:T(8,128)(2,1)S(1)} %copy-done.8, bf16[1024,256]{1,0:T(8,128)(2,1)S(1)} %copy-done.9, bf16[64,4096]{1,0:T(8,128)(2,1)S(1)} %copy-done.5), custom_call_target="tpu_custom_call" | custom-call | flops 1140850688 | bytes 2097152 | tf_op jit(solution)/shard_map/attend/pallas_call | solution.py:53
  169.9 2.6 %collective-permute-done.7.refs_2_ = bf16[40,4352]{1,0:T(8,128)(2,1)S(1)} collective-permute-done((bf16[40,4352]{1,0:T(8,128)(2,1)S(1)}, bf16[40,4352]{1,0:T(8,128)(2,1)S(1)}, u32[]{:S(2)}, u32[]{:S(2)}) %collective-permute-start.7) | collective-permute-done | bytes 348192 | tf_op jit(solution)/shard_map/ppermute | solution.py:387
  172.6 1.2 combine.4
  173.8 6.7 %collective-permute-done.24 = bf16[64,4096]{1,0:T(8,128)(2,1)S(1)} collective-permute-done((bf16[64,4096]{1,0:T(8,128)(2,1)S(1)}, bf16[64,4096]{1,0:T(8,128)(2,1)S(1)}, u32[]{:S(2)}, u32[]{:S(2)}) %collective-permute-start.24) | collective-permute-done | bytes 524320 | tf_op jit(solution)/shard_map/ppermute | solution.py:387
  180.5 10.3 %collective-permute-done.32 = bf16[64,4096]{1,0:T(8,128)(2,1)S(1)} collective-permute-done((bf16[64,4096]{1,0:T(8,128)(2,1)S(1)}, bf16[64,4096]{1,0:T(8,128)(2,1)S(1)}, u32[]{:S(2)}, u32[]{:S(2)}) %collective-permute-start.32) | collective-permute-done | bytes 524320 | tf_op jit(solution)/shard_map/ppermute | solution.py:387
  190.9 1.1 add_convert_fusion
  (56 shorter events, 5.9 us)
Async XLA Ops:
  0.0 80.1 %collective-permute-start.3 = (bf16[4096,384]{1,0:T(8,128)(2,1)}, bf16[4096,384]{1,0:T(8,128)(2,1)S(1)}, u32[]{:S(2)}, u32[]{:S(2)}) collective-permute-start(bf16[4096,384]{1,0:T(8,128)(2,1)} %bitcast.7), channel_id=1, source_target_pairs={{0,1},{1,0},{2,3},{3,2},{4,5},{5,4},{6,7},{7,6},{8,9},{9,8},{10,11... | collective-permute-start | bytes 9437192 | tf_op jit(solution)/shard_map/ppermute | solution.py:390
  0.0 80.5 %collective-permute-start.4 = (bf16[4096,384]{1,0:T(8,128)(2,1)}, bf16[4096,384]{1,0:T(8,128)(2,1)}, u32[]{:S(2)}, u32[]{:S(2)}) collective-permute-start(bf16[4096,384]{1,0:T(8,128)(2,1)} %bitcast.12), channel_id=1, source_target_pairs={{0,1},{1,0},{2,3},{3,2},{4,5},{5,4},{6,7},{7,6},{8,9},{9,8},{10,11... | collective-permute-start | bytes 9437192 | tf_op jit(solution)/shard_map/ppermute | solution.py:390
  0.5 81.5 %collective-permute-start.5 = (bf16[384,4096]{1,0:T(8,128)(2,1)}, bf16[384,4096]{1,0:T(8,128)(2,1)}, u32[]{:S(2)}, u32[]{:S(2)}) collective-permute-start(bf16[384,4096]{1,0:T(8,128)(2,1)} %bitcast.17), channel_id=1, source_target_pairs={{0,1},{1,0},{2,3},{3,2},{4,5},{5,4},{6,7},{7,6},{8,9},{9,8},{10,11... | collective-permute-start | bytes 9437192 | tf_op jit(solution)/shard_map/ppermute | solution.py:390
  3.8 14.9 %collective-permute-start.9 = (bf16[64,4224]{1,0:T(8,128)(2,1)}, bf16[64,4224]{1,0:T(8,128)(2,1)S(1)}, u32[]{:S(2)}, u32[]{:S(2)}) collective-permute-start(bf16[64,4224]{1,0:T(8,128)(2,1)} %get-tuple-element.56.meta_ref), channel_id=1, source_target_pairs={{0,8},{2,10},{4,12},{6,14},{8,0},{10,2},{12,4},{14,6},{16,24},{18,... | collective-permute-start | bytes 1622024 | tf_op jit(solution)/shard_map/ppermute | solution.py:387
  4.2 17.9 %collective-permute-start = (bf16[40,4352]{1,0:T(8,128)(2,1)}, bf16[40,4352]{1,0:T(8,128)(2,1)S(1)}, u32[]{:S(2)}, u32[]{:S(2)}) collective-permute-start(bf16[40,4352]{1,0:T(8,128)(2,1)} %get-tuple-element.41), channel_id=1, source_target_pairs={{0,2},{2,0},{4,6},{6,4},{8,10},{10,8},{12,14},{14,12},{16,18},{18,... | collective-permute-start | bytes 1044488 | tf_op jit(solution)/shard_map/ppermute | solution.py:387
  18.7 25.7 %collective-permute-start.17 = (bf16[64,4224]{1,0:T(8,128)(2,1)}, bf16[64,4224]{1,0:T(8,128)(2,1)S(1)}, u32[]{:S(2)}, u32[]{:S(2)}) collective-permute-start(bf16[64,4224]{1,0:T(8,128)(2,1)} %get-tuple-element.56.meta_ref), channel_id=1, source_target_pairs={{0,16},{2,18},{4,20},{6,22},{8,24},{10,26},{12,28},{14,30},{16,0},... | collective-permute-start | bytes 1622024 | tf_op jit(solution)/shard_map/ppermute | solution.py:387
  22.2 9.5 %collective-permute-start.10 = (bf16[40,4352]{1,0:T(8,128)(2,1)S(1)}, bf16[40,4352]{1,0:T(8,128)(2,1)S(1)}, u32[]{:S(2)}, u32[]{:S(2)}) collective-permute-start(bf16[40,4352]{1,0:T(8,128)(2,1)S(1)} %get-tuple-element.49), channel_id=1, source_target_pairs={{0,2},{2,0},{4,6},{6,4},{8,10},{10,8},{12,14},{14,12},{16,18},{18,... | collective-permute-start | bytes 1044488 | tf_op jit(solution)/shard_map/ppermute | solution.py:387
  31.6 14.1 %collective-permute-start.11 = (bf16[40,4352]{1,0:T(8,128)(2,1)S(1)}, bf16[40,4352]{1,0:T(8,128)(2,1)S(1)}, u32[]{:S(2)}, u32[]{:S(2)}) collective-permute-start(bf16[40,4352]{1,0:T(8,128)(2,1)S(1)} %get-tuple-element.50), channel_id=1, source_target_pairs={{0,4},{2,6},{4,0},{6,2},{8,12},{10,14},{12,8},{14,10},{16,20},{18,... | collective-permute-start | bytes 1044488 | tf_op jit(solution)/shard_map/ppermute | solution.py:387
  44.4 11.9 %collective-permute-start.12 = (bf16[40,4352]{1,0:T(8,128)(2,1)S(1)}, bf16[40,4352]{1,0:T(8,128)(2,1)S(1)}, u32[]{:S(2)}, u32[]{:S(2)}) collective-permute-start(bf16[40,4352]{1,0:T(8,128)(2,1)S(1)} %get-tuple-element.51), channel_id=1, source_target_pairs={{0,6},{2,4},{4,2},{6,0},{8,14},{10,12},{12,10},{14,8},{16,22},{18,... | collective-permute-start | bytes 1044488 | tf_op jit(solution)/shard_map/ppermute | solution.py:387
  45.8 16.1 %collective-permute-start.18 = (bf16[40,4352]{1,0:T(8,128)(2,1)S(1)}, bf16[40,4352]{1,0:T(8,128)(2,1)S(1)}, u32[]{:S(2)}, u32[]{:S(2)}) collective-permute-start(bf16[40,4352]{1,0:T(8,128)(2,1)S(1)} %get-tuple-element.58), channel_id=1, source_target_pairs={{0,2},{2,0},{4,6},{6,4},{8,10},{10,8},{12,14},{14,12},{16,18},{18,... | collective-permute-start | bytes 1044488 | tf_op jit(solution)/shard_map/ppermute | solution.py:387
  56.3 12.4 %collective-permute-start.25 = (bf16[64,4224]{1,0:T(8,128)(2,1)S(1)}, bf16[64,4224]{1,0:T(8,128)(2,1)S(1)}, u32[]{:S(2)}, u32[]{:S(2)}) collective-permute-start(bf16[64,4224]{1,0:T(8,128)(2,1)S(1)} %collective-permute-done.17.base_ref.meta_ref), channel_id=1, source_target_pairs={{0,8},{2,10},{4,12},{6,14},{8,0},{10,2},{12,4},{14,6},{16,24},{18,... | collective-permute-start | bytes 1622024 | tf_op jit(solution)/shard_map/ppermute | solution.py:387
  61.9 16.7 %collective-permute-start.19 = (bf16[40,4352]{1,0:T(8,128)(2,1)S(1)}, bf16[40,4352]{1,0:T(8,128)(2,1)S(1)}, u32[]{:S(2)}, u32[]{:S(2)}) collective-permute-start(bf16[40,4352]{1,0:T(8,128)(2,1)S(1)} %get-tuple-element.59), channel_id=1, source_target_pairs={{0,4},{2,6},{4,0},{6,2},{8,12},{10,14},{12,8},{14,10},{16,20},{18,... | collective-permute-start | bytes 1044488 | tf_op jit(solution)/shard_map/ppermute | solution.py:387
  68.7 28.6 %collective-permute-start.20 = (bf16[40,4352]{1,0:T(8,128)(2,1)S(1)}, bf16[40,4352]{1,0:T(8,128)(2,1)S(1)}, u32[]{:S(2)}, u32[]{:S(2)}) collective-permute-start(bf16[40,4352]{1,0:T(8,128)(2,1)S(1)} %get-tuple-element.60), channel_id=1, source_target_pairs={{0,6},{2,4},{4,2},{6,0},{8,14},{10,12},{12,10},{14,8},{16,22},{18,... | collective-permute-start | bytes 1044488 | tf_op jit(solution)/shard_map/ppermute | solution.py:387
  78.5 27.7 %collective-permute-start.1 = (bf16[40,4352]{1,0:T(8,128)(2,1)}, bf16[40,4352]{1,0:T(8,128)(2,1)S(1)}, u32[]{:S(2)}, u32[]{:S(2)}) collective-permute-start(bf16[40,4352]{1,0:T(8,128)(2,1)} %get-tuple-element.42), channel_id=1, source_target_pairs={{0,4},{2,6},{4,0},{6,2},{8,12},{10,14},{12,8},{14,10},{16,20},{18,... | collective-permute-start | bytes 1044488 | tf_op jit(solution)/shard_map/ppermute | solution.py:387
  80.1 27.7 %collective-permute-start.2 = (bf16[40,4352]{1,0:T(8,128)(2,1)}, bf16[40,4352]{1,0:T(8,128)(2,1)S(1)}, u32[]{:S(2)}, u32[]{:S(2)}) collective-permute-start(bf16[40,4352]{1,0:T(8,128)(2,1)} %get-tuple-element.43), channel_id=1, source_target_pairs={{0,6},{2,4},{4,2},{6,0},{8,14},{10,12},{12,10},{14,8},{16,22},{18,... | collective-permute-start | bytes 1044488 | tf_op jit(solution)/shard_map/ppermute | solution.py:387
  80.5 28.8 %collective-permute-start.26 = (bf16[40,4352]{1,0:T(8,128)(2,1)S(1)}, bf16[40,4352]{1,0:T(8,128)(2,1)S(1)}, u32[]{:S(2)}, u32[]{:S(2)}) collective-permute-start(bf16[40,4352]{1,0:T(8,128)(2,1)S(1)} %get-tuple-element.66), channel_id=1, source_target_pairs={{0,2},{2,0},{4,6},{6,4},{8,10},{10,8},{12,14},{14,12},{16,18},{18,... | collective-permute-start | bytes 1044488 | tf_op jit(solution)/shard_map/ppermute | solution.py:387
  82.0 31.3 %collective-permute-start.27 = (bf16[40,4352]{1,0:T(8,128)(2,1)S(1)}, bf16[40,4352]{1,0:T(8,128)(2,1)S(1)}, u32[]{:S(2)}, u32[]{:S(2)}) collective-permute-start(bf16[40,4352]{1,0:T(8,128)(2,1)S(1)} %get-tuple-element.67), channel_id=1, source_target_pairs={{0,4},{2,6},{4,0},{6,2},{8,12},{10,14},{12,8},{14,10},{16,20},{18,... | collective-permute-start | bytes 1044488 | tf_op jit(solution)/shard_map/ppermute | solution.py:387
  83.6 1.9 copy-start
  85.5 1.9 copy-start.2
  87.3 1.9 copy-start.3
  97.3 16.0 %collective-permute-start.28 = (bf16[40,4352]{1,0:T(8,128)(2,1)S(1)}, bf16[40,4352]{1,0:T(8,128)(2,1)S(1)}, u32[]{:S(2)}, u32[]{:S(2)}) collective-permute-start(bf16[40,4352]{1,0:T(8,128)(2,1)S(1)} %get-tuple-element.68), channel_id=1, source_target_pairs={{0,6},{2,4},{4,2},{6,0},{8,14},{10,12},{12,10},{14,8},{16,22},{18,... | collective-permute-start | bytes 1044488 | tf_op jit(solution)/shard_map/ppermute | solution.py:387
  97.8 15.8 %copy-start.1 = (bf16[1,4096,384]{2,1,0:T(8,128)(2,1)S(1)}, bf16[1,4096,384]{2,1,0:T(8,128)(2,1)}, u32[]{:S(2)}) copy-start(bf16[1,4096,384]{2,1,0:T(8,128)(2,1)} %param.22) | copy-start | bytes 9437188
  106.2 15.5 %collective-permute-start.13 = (bf16[40,4352]{1,0:T(8,128)(2,1)S(1)}, bf16[40,4352]{1,0:T(8,128)(2,1)S(1)}, u32[]{:S(2)}, u32[]{:S(2)}) collective-permute-start(bf16[40,4352]{1,0:T(8,128)(2,1)S(1)} %get-tuple-element.53), channel_id=1, source_target_pairs={{0,2},{2,0},{4,6},{6,4},{8,10},{10,8},{12,14},{14,12},{16,18},{18,... | collective-permute-start | bytes 1044488 | tf_op jit(solution)/shard_map/ppermute | solution.py:387
  107.8 20.4 %collective-permute-start.14 = (bf16[40,4352]{1,0:T(8,128)(2,1)S(1)}, bf16[40,4352]{1,0:T(8,128)(2,1)S(1)}, u32[]{:S(2)}, u32[]{:S(2)}) collective-permute-start(bf16[40,4352]{1,0:T(8,128)(2,1)S(1)} %get-tuple-element.54), channel_id=1, source_target_pairs={{0,4},{2,6},{4,0},{6,2},{8,12},{10,14},{12,8},{14,10},{16,20},{18,... | collective-permute-start | bytes 1044488 | tf_op jit(solution)/shard_map/ppermute | solution.py:387
  109.3 18.9 %collective-permute-start.15 = (bf16[40,4352]{1,0:T(8,128)(2,1)S(1)}, bf16[40,4352]{1,0:T(8,128)(2,1)S(1)}, u32[]{:S(2)}, u32[]{:S(2)}) collective-permute-start(bf16[40,4352]{1,0:T(8,128)(2,1)S(1)} %get-tuple-element.55), channel_id=1, source_target_pairs={{0,6},{2,4},{4,2},{6,0},{8,14},{10,12},{12,10},{14,8},{16,22},{18,... | collective-permute-start | bytes 1044488 | tf_op jit(solution)/shard_map/ppermute | solution.py:387
  113.3 18.9 %collective-permute-start.21 = (bf16[40,4352]{1,0:T(8,128)(2,1)S(1)}, bf16[40,4352]{1,0:T(8,128)(2,1)S(1)}, u32[]{:S(2)}, u32[]{:S(2)}) collective-permute-start(bf16[40,4352]{1,0:T(8,128)(2,1)S(1)} %get-tuple-element.62), channel_id=1, source_target_pairs={{0,2},{2,0},{4,6},{6,4},{8,10},{10,8},{12,14},{14,12},{16,18},{18,... | collective-permute-start | bytes 1044488 | tf_op jit(solution)/shard_map/ppermute | solution.py:387
  113.3 29.8 %collective-permute-start.22 = (bf16[40,4352]{1,0:T(8,128)(2,1)S(1)}, bf16[40,4352]{1,0:T(8,128)(2,1)S(1)}, u32[]{:S(2)}, u32[]{:S(2)}) collective-permute-start(bf16[40,4352]{1,0:T(8,128)(2,1)S(1)} %get-tuple-element.63), channel_id=1, source_target_pairs={{0,4},{2,6},{4,0},{6,2},{8,12},{10,14},{12,8},{14,10},{16,20},{18,... | collective-permute-start | bytes 1044488 | tf_op jit(solution)/shard_map/ppermute | solution.py:387
  113.6 21.1 %copy-start.6 = (bf16[40,4352]{1,0:T(8,128)(2,1)S(1)}, bf16[40,4352]{1,0:T(8,128)(2,1)}, u32[]{:S(2)}) copy-start(bf16[40,4352]{1,0:T(8,128)(2,1)} %get-tuple-element.40.refs_0_) | copy-start | bytes 1044484
  121.7 23.1 %collective-permute-start.23 = (bf16[40,4352]{1,0:T(8,128)(2,1)S(1)}, bf16[40,4352]{1,0:T(8,128)(2,1)S(1)}, u32[]{:S(2)}, u32[]{:S(2)}) collective-permute-start(bf16[40,4352]{1,0:T(8,128)(2,1)S(1)} %get-tuple-element.64), channel_id=1, source_target_pairs={{0,6},{2,4},{4,2},{6,0},{8,14},{10,12},{12,10},{14,8},{16,22},{18,... | collective-permute-start | bytes 1044488 | tf_op jit(solution)/shard_map/ppermute | solution.py:387
  128.2 23.0 %collective-permute-start.29 = (bf16[40,4352]{1,0:T(8,128)(2,1)S(1)}, bf16[40,4352]{1,0:T(8,128)(2,1)S(1)}, u32[]{:S(2)}, u32[]{:S(2)}) collective-permute-start(bf16[40,4352]{1,0:T(8,128)(2,1)S(1)} %get-tuple-element.70), channel_id=1, source_target_pairs={{0,2},{2,0},{4,6},{6,4},{8,10},{10,8},{12,14},{14,12},{16,18},{18,... | collective-permute-start | bytes 1044488 | tf_op jit(solution)/shard_map/ppermute | solution.py:387
  128.2 24.6 %collective-permute-start.30 = (bf16[40,4352]{1,0:T(8,128)(2,1)S(1)}, bf16[40,4352]{1,0:T(8,128)(2,1)S(1)}, u32[]{:S(2)}, u32[]{:S(2)}) collective-permute-start(bf16[40,4352]{1,0:T(8,128)(2,1)S(1)} %get-tuple-element.71), channel_id=1, source_target_pairs={{0,4},{2,6},{4,0},{6,2},{8,12},{10,14},{12,8},{14,10},{16,20},{18,... | collective-permute-start | bytes 1044488 | tf_op jit(solution)/shard_map/ppermute | solution.py:387
  132.3 23.0 %collective-permute-start.31 = (bf16[40,4352]{1,0:T(8,128)(2,1)S(1)}, bf16[40,4352]{1,0:T(8,128)(2,1)S(1)}, u32[]{:S(2)}, u32[]{:S(2)}) collective-permute-start(bf16[40,4352]{1,0:T(8,128)(2,1)S(1)} %get-tuple-element.72), channel_id=1, source_target_pairs={{0,6},{2,4},{4,2},{6,0},{8,14},{10,12},{12,10},{14,8},{16,22},{18,... | collective-permute-start | bytes 1044488 | tf_op jit(solution)/shard_map/ppermute | solution.py:387
  143.2 14.8 %collective-permute-start.6 = (bf16[40,4352]{1,0:T(8,128)(2,1)S(1)}, bf16[40,4352]{1,0:T(8,128)(2,1)S(1)}, u32[]{:S(2)}, u32[]{:S(2)}) collective-permute-start(bf16[40,4352]{1,0:T(8,128)(2,1)S(1)} %get-tuple-element.45), channel_id=1, source_target_pairs={{0,2},{2,0},{4,6},{6,4},{8,10},{10,8},{12,14},{14,12},{16,18},{18,... | collective-permute-start | bytes 1044488 | tf_op jit(solution)/shard_map/ppermute | solution.py:387
  143.4 18.3 %copy-start.5 = (bf16[64,4096]{1,0:T(8,128)(2,1)S(1)}, bf16[64,4096]{1,0:T(8,128)(2,1)}, u32[]{:S(2)}) copy-start(bf16[64,4096]{1,0:T(8,128)(2,1)} %tokens_ref.3) | copy-start | bytes 1572868
  143.4 18.3 %copy-start.7 = (bf16[64,4096]{1,0:T(8,128)(2,1)S(1)}, bf16[64,4096]{1,0:T(8,128)(2,1)}, u32[]{:S(2)}) copy-start(bf16[64,4096]{1,0:T(8,128)(2,1)} %q_ref.1) | copy-start | bytes 1572868
  143.4 18.3 %copy-start.8 = (bf16[1024,256]{1,0:T(8,128)(2,1)S(1)}, bf16[1024,256]{1,0:T(8,128)(2,1)}, u32[]{:S(2)}) copy-start(bf16[1024,256]{1,0:T(8,128)(2,1)} %pkeys_ref.1) | copy-start | bytes 1572868
  143.4 18.3 %copy-start.9 = (bf16[1024,256]{1,0:T(8,128)(2,1)S(1)}, bf16[1024,256]{1,0:T(8,128)(2,1)}, u32[]{:S(2)}) copy-start(bf16[1024,256]{1,0:T(8,128)(2,1)} %pvalues_ref.1) | copy-start | bytes 1572868
  143.4 18.3 %copy-start.10 = (bf16[64,256]{1,0:T(8,128)(2,1)S(1)}, bf16[64,256]{1,0:T(8,128)(2,1)}, u32[]{:S(2)}) copy-start(bf16[64,256]{1,0:T(8,128)(2,1)} %keys_ref.1) | copy-start | bytes 98308
  143.4 18.3 %copy-start.11 = (bf16[64,256]{1,0:T(8,128)(2,1)S(1)}, bf16[64,256]{1,0:T(8,128)(2,1)}, u32[]{:S(2)}) copy-start(bf16[64,256]{1,0:T(8,128)(2,1)} %values_ref.1) | copy-start | bytes 98308
  144.9 28.9 %collective-permute-start.16 = (bf16[64,4096]{1,0:T(8,128)(2,1)S(1)}, bf16[64,4096]{1,0:T(8,128)(2,1)S(1)}, u32[]{:S(2)}, u32[]{:S(2)}) collective-permute-start(bf16[64,4096]{1,0:T(8,128)(2,1)S(1)} %combine.5), channel_id=1, source_target_pairs={{0,8},{2,10},{4,12},{6,14},{8,0},{10,2},{12,4},{14,6},{16,24},{18,... | collective-permute-start | bytes 1572872 | tf_op jit(solution)/shard_map/ppermute | solution.py:387
  151.3 29.2 %collective-permute-start.24 = (bf16[64,4096]{1,0:T(8,128)(2,1)S(1)}, bf16[64,4096]{1,0:T(8,128)(2,1)S(1)}, u32[]{:S(2)}, u32[]{:S(2)}) collective-permute-start(bf16[64,4096]{1,0:T(8,128)(2,1)S(1)} %combine.6), channel_id=1, source_target_pairs={{0,16},{2,18},{4,20},{6,22},{8,24},{10,26},{12,28},{14,30},{16,0},... | collective-permute-start | bytes 1572872 | tf_op jit(solution)/shard_map/ppermute | solution.py:387
  155.3 17.3 %copy-start.4 = (bf16[64,4224]{1,0:T(8,128)(2,1)S(1)}, bf16[64,4224]{1,0:T(8,128)(2,1)}, u32[]{:S(2)}) copy-start(bf16[64,4224]{1,0:T(8,128)(2,1)} %get-tuple-element.56.meta_ref) | copy-start | bytes 1622020
  156.5 34.4 %collective-permute-start.32 = (bf16[64,4096]{1,0:T(8,128)(2,1)S(1)}, bf16[64,4096]{1,0:T(8,128)(2,1)S(1)}, u32[]{:S(2)}, u32[]{:S(2)}) collective-permute-start(bf16[64,4096]{1,0:T(8,128)(2,1)S(1)} %combine.7), channel_id=1, source_target_pairs={{0,24},{2,26},{4,28},{6,30},{8,16},{10,18},{12,20},{14,22},{16,8},... | collective-permute-start | bytes 1572872 | tf_op jit(solution)/shard_map/ppermute | solution.py:387
  156.6 16.0 %collective-permute-start.7 = (bf16[40,4352]{1,0:T(8,128)(2,1)S(1)}, bf16[40,4352]{1,0:T(8,128)(2,1)S(1)}, u32[]{:S(2)}, u32[]{:S(2)}) collective-permute-start(bf16[40,4352]{1,0:T(8,128)(2,1)S(1)} %get-tuple-element.46), channel_id=1, source_target_pairs={{0,4},{2,6},{4,0},{6,2},{8,12},{10,14},{12,8},{14,10},{16,20},{18,... | collective-permute-start | bytes 1044488 | tf_op jit(solution)/shard_map/ppermute | solution.py:387
  157.9 14.7 %collective-permute-start.8 = (bf16[40,4352]{1,0:T(8,128)(2,1)S(1)}, bf16[40,4352]{1,0:T(8,128)(2,1)S(1)}, u32[]{:S(2)}, u32[]{:S(2)}) collective-permute-start(bf16[40,4352]{1,0:T(8,128)(2,1)S(1)} %get-tuple-element.47), channel_id=1, source_target_pairs={{0,6},{2,4},{4,2},{6,0},{8,14},{10,12},{12,10},{14,8},{16,22},{18,... | collective-permute-start | bytes 1044488 | tf_op jit(solution)/shard_map/ppermute | solution.py:387

commit v2 on v1

--- a/solution.py
+++ b/solution.py
@@ -43,27 +43,30 @@
         out_ref[:, at] = tokens_ref[:, at].astype(jnp.float32) + context[h * rows : (h + 1) * rows]
 
 
-def attend(tokens, queries, keys_local, values_local, prompt_keys, prompt_values, heads=4):
-    rows, width = tokens.shape
+def attend(part, tokens, queries, keys_local, values_local, prompt_keys, prompt_values, heads=4):
+    rows, width = tokens.shape[0], tokens.shape[1] // KVH
     prefix = prompt_keys.shape[0]
-    per_key = HEADS // KVH // heads
-    wide = pl.BlockSpec((rows, heads * HD), lambda i: (0, i))
-    own = pl.BlockSpec((rows, HD), lambda i: (0, i // per_key))
-    shared = pl.BlockSpec((prefix, HD), lambda i: (0, i // per_key))
+    steps = HEADS // KVH // heads
+    wide = pl.BlockSpec((rows, heads * HD), lambda i: (0, part * steps + i))
+    own = pl.BlockSpec((rows, HD), lambda i: (0, part))
+    shared = pl.BlockSpec((prefix, HD), lambda i: (0, part))
     return pl.pallas_call(
         functools.partial(attend_kernel, heads),
-        grid=(HEADS // heads,),
+        grid=(steps,),
         out_shape=jax.ShapeDtypeStruct((rows, width), jnp.float32),
         in_specs=[wide, own, own, shared, shared, wide],
-        out_specs=wide,
+        out_specs=pl.BlockSpec((rows, heads * HD), lambda i: (0, i)),
         compiler_params=pltpu.CompilerParams(vmem_limit_bytes=24 * 2**20),
         cost_estimate=pl.CostEstimate(
             flops=4 * rows * (prefix + rows) * width,
             bytes_accessed=8 * rows * width,
-            transcendentals=rows * (prefix + rows) * HEADS,
+            transcendentals=rows * (prefix + rows) * HEADS // KVH,
         ),
         name="attend",
-    )(queries, keys_local, values_local, prompt_keys, prompt_values, tokens)
+    )(*[
+        pltpu.with_memory_space_constraint(a, pltpu.HBM)
+        for a in (queries, keys_local, values_local, prompt_keys, prompt_values, tokens)
+    ])
 
 
 PLANE = 4
@@ -124,15 +127,20 @@
     return -(-count // SUB) * SUB
 
 
-def choose(count, slot_ref, base_ref, outs):
-    tokens, padded = base_ref.shape
-    width = padded // CHUNK * CHUNK
-    extra = padded - width
+def normed(tokens_ref, gain_ref):
+    wide = tokens_ref[...].astype(jnp.float32)
+    scale = lax.rsqrt(jnp.mean(wide * wide, axis=-1, keepdims=True) + 1e-06)
+    return (wide * scale * gain_ref[...]).astype(jnp.bfloat16)
+
+
+def choose(count, slot_ref, base_ref, meta, outs):
+    tokens, extra = meta.shape
+    width = base_ref.shape[1] // CHUNK * CHUNK
     size = padded_rows(count)
     row = lax.broadcasted_iota(jnp.int32, (tokens, tokens), 0)
     column = lax.broadcasted_iota(jnp.int32, (tokens, tokens), 1)
     turned = lax.dot_general(
-        base_ref[:, width:],
+        meta,
         (row == column).astype(jnp.bfloat16),
         (((0,), (0,)), ((), ())),
         preferred_element_type=jnp.float32,
@@ -170,12 +178,20 @@
 
 
 def payload_kernel(
-    experts, count, slot_ref, holder_ref, tokens_ref, gain_ref, ids_ref, route_ref, out_ref, *outs
+    experts,
+    count,
+    slot_ref,
+    holder_ref,
+    tokens_ref,
+    gain_ref,
+    ids_ref,
+    route_ref,
+    out_ref,
+    meta_ref,
+    *outs,
 ):
     rows, width = tokens_ref.shape
-    wide = tokens_ref[...].astype(jnp.float32)
-    scale = lax.rsqrt(jnp.mean(wide * wide, axis=-1, keepdims=True) + 1e-06)
-    out_ref[:, :width] = (wide * scale * gain_ref[...]).astype(jnp.bfloat16)
+    out_ref[:, :width] = normed(tokens_ref, gain_ref)
     extra = out_ref.shape[1] - width
     part = lax.broadcasted_iota(jnp.int32, (extra, rows), 0)
     slot = part % experts
@@ -198,8 +214,10 @@
         (((1,), (1,)), ((), ())),
         preferred_element_type=jnp.float32,
     )
-    out_ref[:, width:] = turned.astype(jnp.bfloat16)
-    choose(count, slot_ref, out_ref, outs)
+    meta = turned.astype(jnp.bfloat16)
+    out_ref[:, width:] = meta
+    meta_ref[...] = meta
+    choose(count, slot_ref, out_ref, meta, outs)
     clear(outs, count, width)
 
 
@@ -215,37 +233,51 @@
     vmem = pl.BlockSpec(memory_space=pltpu.VMEM)
     outs = pl.pallas_call(
         functools.partial(payload_kernel, experts, count),
-        out_shape=[jax.ShapeDtypeStruct((rows, width + extra), jnp.bfloat16)]
+        out_shape=[
+            jax.ShapeDtypeStruct((rows, width + extra), jnp.bfloat16),
+            jax.ShapeDtypeStruct((rows, extra), jnp.bfloat16),
+        ]
         + [packed_shape(count, width)] * PLANE,
         in_specs=[pl.BlockSpec(memory_space=pltpu.SMEM)] * 2 + [vmem] * 4,
-        out_specs=[vmem] * (PLANE + 1),
+        out_specs=[vmem] * (PLANE + 2),
         compiler_params=pltpu.CompilerParams(vmem_limit_bytes=LARGE),
         name="payload",
     )(slot, holder, tokens, norm_gain.reshape(1, -1), expert_ids.T, route_weight.T)
-    return outs[0], outs[1:]
+    return outs[0], outs[1], outs[2:]
 
 
 def dispatch_kernel(count, slot_ref, base_ref, *outs):
-    choose(count, slot_ref, base_ref, outs)
-    clear(outs, count, base_ref.shape[1] // CHUNK * CHUNK)
+    width = base_ref.shape[1] // CHUNK * CHUNK
+    choose(count, slot_ref, base_ref, base_ref[:, width:], outs)
+    clear(outs, count, width)
+
+
+def raw_dispatch_kernel(count, slot_ref, tokens_ref, meta_ref, gain_ref, *refs):
+    outs, rows_buf = refs[:PLANE], refs[PLANE]
+    rows_buf[...] = normed(tokens_ref, gain_ref)
+    choose(count, slot_ref, rows_buf, meta_ref[...], outs)
+    clear(outs, count, tokens_ref.shape[1])
 
 
 def dispatch(slot, base, count, width):
     vmem = pl.BlockSpec(memory_space=pltpu.VMEM)
-    tokens, padded = base.shape
+    raw = isinstance(base, tuple)
+    operands = base if raw else (base,)
+    tokens = operands[0].shape[0]
     return pl.pallas_call(
-        functools.partial(dispatch_kernel, count),
+        functools.partial(raw_dispatch_kernel if raw else dispatch_kernel, count),
         out_shape=[packed_shape(count, width)] * PLANE,
-        in_specs=[pl.BlockSpec(memory_space=pltpu.SMEM), vmem],
+        in_specs=[pl.BlockSpec(memory_space=pltpu.SMEM)] + [vmem] * len(operands),
         out_specs=[vmem] * PLANE,
+        scratch_shapes=[pltpu.VMEM((tokens, width), jnp.bfloat16)] if raw else [],
         cost_estimate=pl.CostEstimate(
-            flops=2 * PLANE * count * tokens * padded,
-            bytes_accessed=2 * (tokens + PLANE * count) * padded,
+            flops=2 * PLANE * count * tokens * width,
+            bytes_accessed=2 * (tokens + PLANE * count) * width,
             transcendentals=0,
         ),
         compiler_params=pltpu.CompilerParams(vmem_limit_bytes=SMALL),
         name="dispatch",
-    )(slot, base)
+    )(slot, *operands)
 
 
 def combine_kernel(extras, experts, count, slot_ref, meta_ref, *refs):
@@ -283,14 +315,15 @@
         rows = jnp.concatenate([unpack(r, at, count, width) for r in results], 0)
         rows = (rows * shares).astype(jnp.bfloat16)
         total = jnp.dot(chooser, rows, preferred_element_type=jnp.float32)
-        for term in terms:
-            total = total + term[:, at].astype(jnp.float32)
+        if terms:
+            part, start = divmod(at.start, width // len(terms))
+            total = total + terms[part][:, start : start + CHUNK].astype(jnp.float32)
         out_ref[:, at] = total.astype(out_ref.dtype)
 
 
 def combine(slot, base, results, terms, dtype, experts, count, width):
     tokens, padded = base.shape
-    extra = padded - width
+    extra = padded % CHUNK
     whole = lambda a: pl.BlockSpec(a.shape, lambda i: (0, 0))
     return pl.pallas_call(
         functools.partial(combine_kernel, len(terms), experts, count),
@@ -298,7 +331,7 @@
         out_shape=jax.ShapeDtypeStruct((tokens, width), dtype),
         in_specs=[
             pl.BlockSpec(memory_space=pltpu.SMEM),
-            pl.BlockSpec((tokens, extra), lambda i: (0, width // extra)),
+            pl.BlockSpec((tokens, extra), lambda i: (0, padded // extra - 1)),
         ]
         + [whole(a) for a in (*results, *terms)],
         out_specs=pl.BlockSpec((tokens, width), lambda i: (0, 0)),
@@ -359,10 +392,6 @@
     )(*blocks, *weights)
 
 
-def after(value, *others):
-    return lax.optimization_barrier((value,) + others)[0]
-
-
 def local(
     tokens,
     queries,
@@ -394,7 +423,9 @@
     slot = lax.axis_index("expert").astype(jnp.int32).reshape(1)
     width = tokens.shape[1]
     count = capacity(tokens.shape[0], owners)
-    payload, chosen = make_payload(slot, tokens, norm_gain, expert_ids, route_weight, holder, count)
+    payload, meta, chosen = make_payload(
+        slot, tokens, norm_gain, expert_ids, route_weight, holder, count
+    )
     bases, blocks, outs = {}, {}, {}
 
     def gather(k, base, ready=None):
@@ -412,11 +443,19 @@
         return combine(slot, bases[k], outs[k], terms, dtype, experts, count, width)
 
     gather(0, payload, chosen)
-    result = attend(tokens, queries, keys_local, values_local, prompt_keys, prompt_values)
+    result = []
+    for part in range(KVH):
+        result.append(
+            attend(
+                part, tokens, queries, keys_local, values_local, prompt_keys, prompt_values
+            )
+        )
     for first in range(0, columns, 4):
         if first == 0:
-            gather(1, swap(payload, 4))
-            gather(2, swap(after(payload, bases[1]), 8))
+            lanes = swap(meta, 4)
+            gather(1, (swap(tokens, 4), lanes, norm_gain.reshape(1, -1)))
+            bases[1] = lanes
+            gather(2, swap(payload, 8))
         else:
             gather(first, swap(payload, 4 * first))
             gather(first + 1, swap(payload, 4 * first + 4))
@@ -427,7 +466,7 @@
     sums = []
     for k in range(1, columns):
         sums.append(swap(collect(k), 4 * k))
-    result = collect(0, (result,), f32)
+    result = collect(0, result, f32)
     for part in sums:
         result = result + part.astype(f32)
     return result.astype(bf16)

time: 194 us -> 198 us (1.021)
  Pallas kernels: 51.8 us -> 54.9 us
    pallas_call x4 -> x5, Pallas kernels: 10.8 us -> 13.9 us  [the longest x2 10.1 us: attend(): pl.pallas_call(functools.partial(attend_kernel, heads), grid=(steps,), ou...]
    ppermute x30 -> x31, starting transfers between devices: 35.3 us -> 36.1 us  [swap(): lax.ppermute(value, 'expert', [(i, i ^ offset) for i in range(owners)])]
    unnamed x24 -> x14, local copies, waits for them, and re-layouts: 5.71 us -> 6.4 us
    ppermute x30 -> x31, waiting for transfers between devices: 97.4 us -> 96.8 us  [swap(): lax.ppermute(value, 'expert', [(i, i ^ offset) for i in range(owners)])]
  transfers between devices with their start and end apart: 33 -> 34, of which waited for: 17 -> 13; matrix products, arithmetic and copies ran while one was open for 0% -> 0% of each run, Pallas kernels for 27% -> 28%
where the time goes in v2:
time: 198 us; the launch traced here: 196 us
  waiting for transfers between devices  96.8 us (49%)
  Pallas kernels  54.9 us (28%)
  starting transfers between devices  36.6 us (18%)
  local copies, waits for them, and re-layouts  6.4 us (3%)
    ppermute x31, waiting for transfers between devices, swap(): lax.ppermute(value, 'expert', [(i, i ^ offset) for i in range(owners)])  96.8 us
    ppermute x31, starting transfers between devices, swap(): lax.ppermute(value, 'expert', [(i, i ^ offset) for i in range(owners)])  36.1 us
    pallas_call x4, Pallas kernels, run_ffn(): pl.pallas_call(functools.partial(ffn_kernel, count), out_shape=[packed_sh...  32.6 us
    pallas_call x2, Pallas kernels, attend(): pl.pallas_call(functools.partial(attend_kernel, heads), grid=(steps,), ou...  10.1 us
    unnamed x14, local copies, waits for them, and re-layouts  6.4 us
    pallas_call x4, Pallas kernels, combine(): pl.pallas_call(functools.partial(combine_kernel, len(terms), experts, cou...  5.12 us
  transfers between devices with their start and end apart: 34, of which 13 were waited for; matrix products, arithmetic and copies ran while one was open for 0% of the time, Pallas kernels for 28%

profile of v2, /device:TPU:14, one launch (start us, length us, event | category | flops | bytes accessed | tf_op | source)
XLA Modules:
  0.0 196.0 jit_solution(16254943650671794567)
XLA Ops:
  1.0 3.3 %payload.1 = (bf16[64,4224]{1,0:T(8,128)(2,1)}, bf16[64,128]{1,0:T(8,128)(2,1)}, bf16[40,4352]{1,0:T(8,128)(2,1)}, bf16[40,4352]{1,0:T(8,128)(2,1)}, bf16[40,4352]{1,0:T(8,128)(2,1)}, /*index=5*/bf16[40,4352]{1,0:T(8,128)(2,1)}) custom-call(s32[1]{0:T(128)} %bitcast.slot_ref, s32[16]{0:T(128)} %holder_ref.1, bf16[64,4096]{1,0:T(8,128)(2,1)} %tokens_ref.5, ...), custom_call_target="tpu_custom_call" | custom-call | tf_op jit(solution)/shard_map/payload/pallas_call | solution.py:234
  4.2 1.6 collective-permute-start.9
  5.8 9.6 %collective-permute-done.9.meta_ref = bf16[64,128]{1,0:T(8,128)(2,1)S(1)} collective-permute-done((bf16[64,128]{1,0:T(8,128)(2,1)}, bf16[64,128]{1,0:T(8,128)(2,1)S(1)}, u32[]{:S(2)}, u32[]{:S(2)}) %collective-permute-start.9) | collective-permute-done | bytes 16416 | tf_op jit(solution)/shard_map/ppermute | solution.py:416
  16.0 2.6 %collective-permute-start.18 = (bf16[64,4224]{1,0:T(8,128)(2,1)}, bf16[64,4224]{1,0:T(8,128)(2,1)S(1)}, u32[]{:S(2)}, u32[]{:S(2)}) collective-permute-start(bf16[64,4224]{1,0:T(8,128)(2,1)} %get-tuple-element.39.meta_ref), channel_id=1, source_target_pairs={{0,16},{2,18},{4,20},{6,22},{8,24},{10,26},{12,28},{14,30},{16,0},... | collective-permute-start | bytes 1622024 | tf_op jit(solution)/shard_map/ppermute | solution.py:416
  18.5 0.7 copy-done.6
  19.3 2.0 %dispatch.3 = (bf16[40,4352]{1,0:T(8,128)(2,1)S(1)}, bf16[40,4352]{1,0:T(8,128)(2,1)S(1)}, bf16[40,4352]{1,0:T(8,128)(2,1)S(1)}, bf16[40,4352]{1,0:T(8,128)(2,1)S(1)}) custom-call(s32[1]{0:T(128)} %bitcast.slot_ref, bf16[64,4096]{1,0:T(8,128)(2,1)} %collective-permute-done.10.tokens_ref, bf16[64,128]{1,0:T(8,128)(2,1)S(1)} %collective-permute-done.9.meta_ref, ...), custom_call_target="tpu_custom_call" | custom-call | flops 88080384 | bytes 1900544 | tf_op jit(solution)/shard_map/dispatch/pallas_call | solution.py:267
  21.2 4.2 %collective-permute-done.refs_1_ = bf16[40,4352]{1,0:T(8,128)(2,1)S(1)} collective-permute-done((bf16[40,4352]{1,0:T(8,128)(2,1)}, bf16[40,4352]{1,0:T(8,128)(2,1)S(1)}, u32[]{:S(2)}, u32[]{:S(2)}) %collective-permute-start) | collective-permute-done | bytes 348192 | tf_op jit(solution)/shard_map/ppermute | solution.py:416
  26.0 15.5 %collective-permute-done.18.base_ref.meta_ref = bf16[64,4224]{1,0:T(8,128)(2,1)S(1)} collective-permute-done((bf16[64,4224]{1,0:T(8,128)(2,1)}, bf16[64,4224]{1,0:T(8,128)(2,1)S(1)}, u32[]{:S(2)}, u32[]{:S(2)}) %collective-permute-start.18) | collective-permute-done | bytes 540704 | tf_op jit(solution)/shard_map/ppermute | solution.py:416
  42.0 2.4 %collective-permute-start.13 = (bf16[40,4352]{1,0:T(8,128)(2,1)S(1)}, bf16[40,4352]{1,0:T(8,128)(2,1)S(1)}, u32[]{:S(2)}, u32[]{:S(2)}) collective-permute-start(bf16[40,4352]{1,0:T(8,128)(2,1)S(1)} %get-tuple-element.52), channel_id=1, source_target_pairs={{0,6},{2,4},{4,2},{6,0},{8,14},{10,12},{12,10},{14,8},{16,22},{18,... | collective-permute-start | bytes 1044488 | tf_op jit(solution)/shard_map/ppermute | solution.py:416
  44.5 0.9 dispatch.4
  45.4 13.7 %collective-permute-done.12.refs_2_ = bf16[40,4352]{1,0:T(8,128)(2,1)S(1)} collective-permute-done((bf16[40,4352]{1,0:T(8,128)(2,1)S(1)}, bf16[40,4352]{1,0:T(8,128)(2,1)S(1)}, u32[]{:S(2)}, u32[]{:S(2)}) %collective-permute-start.12) | collective-permute-done | bytes 348192 | tf_op jit(solution)/shard_map/ppermute | solution.py:416
  59.0 1.5 collective-permute-start.19
  60.8 7.5 %collective-permute-done.19.refs_1_ = bf16[40,4352]{1,0:T(8,128)(2,1)S(1)} collective-permute-done((bf16[40,4352]{1,0:T(8,128)(2,1)S(1)}, bf16[40,4352]{1,0:T(8,128)(2,1)S(1)}, u32[]{:S(2)}, u32[]{:S(2)}) %collective-permute-start.19) | collective-permute-done | bytes 348192 | tf_op jit(solution)/shard_map/ppermute | solution.py:416
  68.8 4.8 %collective-permute-done.26.base_ref.meta_ref = bf16[64,4224]{1,0:T(8,128)(2,1)S(1)} collective-permute-done((bf16[64,4224]{1,0:T(8,128)(2,1)S(1)}, bf16[64,4224]{1,0:T(8,128)(2,1)S(1)}, u32[]{:S(2)}, u32[]{:S(2)}) %collective-permute-start.26) | collective-permute-done | bytes 540704 | tf_op jit(solution)/shard_map/ppermute | solution.py:416
  74.1 0.9 dispatch.5
  75.0 14.2 %collective-permute-done.20.refs_2_ = bf16[40,4352]{1,0:T(8,128)(2,1)S(1)} collective-permute-done((bf16[40,4352]{1,0:T(8,128)(2,1)S(1)}, bf16[40,4352]{1,0:T(8,128)(2,1)S(1)}, u32[]{:S(2)}, u32[]{:S(2)}) %collective-permute-start.20) | collective-permute-done | bytes 348192 | tf_op jit(solution)/shard_map/ppermute | solution.py:416
  89.7 3.4 %collective-permute-start.2 = (bf16[40,4352]{1,0:T(8,128)(2,1)}, bf16[40,4352]{1,0:T(8,128)(2,1)S(1)}, u32[]{:S(2)}, u32[]{:S(2)}) collective-permute-start(bf16[40,4352]{1,0:T(8,128)(2,1)} %get-tuple-element.43), channel_id=1, source_target_pairs={{0,6},{2,4},{4,2},{6,0},{8,14},{10,12},{12,10},{14,8},{16,22},{18,... | collective-permute-start | bytes 1044488 | tf_op jit(solution)/shard_map/ppermute | solution.py:416
  93.1 0.6 collective-permute-start.28
  93.8 1.9 copy-done
  95.7 1.9 copy-done.2
  97.5 1.9 copy-done.3
  99.4 8.0 %ffn.5 = (bf16[40,4352]{1,0:T(8,128)(2,1)S(1)}, bf16[40,4352]{1,0:T(8,128)(2,1)S(1)}, bf16[40,4352]{1,0:T(8,128)(2,1)S(1)}, bf16[40,4352]{1,0:T(8,128)(2,1)S(1)}) custom-call(bf16[40,4352]{1,0:T(8,128)(2,1)S(1)} %get-tuple-element.49.refs_0_, bf16[40,4352]{1,0:T(8,128)(2,1)S(1)} %collective-permute-done.11.refs_1_, ...), custom_call_target="tpu_custom_call" | custom-call | flops 3623878656 | bytes 22020096 | tf_op jit(solution)/shard_map/ffn/pallas_call | solution.py:376
  107.5 2.9 %collective-permute-start.29 = (bf16[40,4352]{1,0:T(8,128)(2,1)S(1)}, bf16[40,4352]{1,0:T(8,128)(2,1)S(1)}, u32[]{:S(2)}, u32[]{:S(2)}) collective-permute-start(bf16[40,4352]{1,0:T(8,128)(2,1)S(1)} %get-tuple-element.68), channel_id=1, source_target_pairs={{0,6},{2,4},{4,2},{6,0},{8,14},{10,12},{12,10},{14,8},{16,22},{18,... | collective-permute-start | bytes 1044488 | tf_op jit(solution)/shard_map/ppermute | solution.py:416
  110.4 8.4 %ffn.6 = (bf16[40,4352]{1,0:T(8,128)(2,1)S(1)}, bf16[40,4352]{1,0:T(8,128)(2,1)S(1)}, bf16[40,4352]{1,0:T(8,128)(2,1)S(1)}, bf16[40,4352]{1,0:T(8,128)(2,1)S(1)}) custom-call(bf16[40,4352]{1,0:T(8,128)(2,1)S(1)} %get-tuple-element.57.refs_0_, bf16[40,4352]{1,0:T(8,128)(2,1)S(1)} %collective-permute-done.19.refs_1_, ...), custom_call_target="tpu_custom_call" | custom-call | flops 3623878656 | bytes 22020096 | tf_op jit(solution)/shard_map/ffn/pallas_call | solution.py:376
  119.0 0.6 collective-permute-start.15
  119.6 2.9 %collective-permute-start.16 = (bf16[40,4352]{1,0:T(8,128)(2,1)S(1)}, bf16[40,4352]{1,0:T(8,128)(2,1)S(1)}, u32[]{:S(2)}, u32[]{:S(2)}) collective-permute-start(bf16[40,4352]{1,0:T(8,128)(2,1)S(1)} %get-tuple-element.56), channel_id=1, source_target_pairs={{0,6},{2,4},{4,2},{6,0},{8,14},{10,12},{12,10},{14,8},{16,22},{18,... | collective-permute-start | bytes 1044488 | tf_op jit(solution)/shard_map/ppermute | solution.py:416
  122.4 4.1 %collective-permute-done.28.refs_2_ = bf16[40,4352]{1,0:T(8,128)(2,1)S(1)} collective-permute-done((bf16[40,4352]{1,0:T(8,128)(2,1)S(1)}, bf16[40,4352]{1,0:T(8,128)(2,1)S(1)}, u32[]{:S(2)}, u32[]{:S(2)}) %collective-permute-start.28) | collective-permute-done | bytes 348192 | tf_op jit(solution)/shard_map/ppermute | solution.py:416
  126.5 2.2 %collective-permute-start.22 = (bf16[40,4352]{1,0:T(8,128)(2,1)S(1)}, bf16[40,4352]{1,0:T(8,128)(2,1)S(1)}, u32[]{:S(2)}, u32[]{:S(2)}) collective-permute-start(bf16[40,4352]{1,0:T(8,128)(2,1)S(1)} %get-tuple-element.62), channel_id=1, source_target_pairs={{0,2},{2,0},{4,6},{6,4},{8,10},{10,8},{12,14},{14,12},{16,18},{18,... | collective-permute-start | bytes 1044488 | tf_op jit(solution)/shard_map/ppermute | solution.py:416
  128.8 8.1 %ffn.7 = (bf16[40,4352]{1,0:T(8,128)(2,1)S(1)}, bf16[40,4352]{1,0:T(8,128)(2,1)S(1)}, bf16[40,4352]{1,0:T(8,128)(2,1)S(1)}, bf16[40,4352]{1,0:T(8,128)(2,1)S(1)}) custom-call(bf16[40,4352]{1,0:T(8,128)(2,1)S(1)} %get-tuple-element.65.refs_0_, bf16[40,4352]{1,0:T(8,128)(2,1)S(1)} %collective-permute-done.27.refs_1_, ...), custom_call_target="tpu_custom_call" | custom-call | flops 3623878656 | bytes 22020096 | tf_op jit(solution)/shard_map/ffn/pallas_call | solution.py:376
  136.9 1.5 collective-permute-start.24
  138.4 3.1 %collective-permute-done.15.refs_2_ = bf16[40,4352]{1,0:T(8,128)(2,1)S(1)} collective-permute-done((bf16[40,4352]{1,0:T(8,128)(2,1)S(1)}, bf16[40,4352]{1,0:T(8,128)(2,1)S(1)}, u32[]{:S(2)}, u32[]{:S(2)}) %collective-permute-start.15) | collective-permute-done | bytes 348192 | tf_op jit(solution)/shard_map/ppermute | solution.py:416
  141.5 2.2 %collective-permute-start.30 = (bf16[40,4352]{1,0:T(8,128)(2,1)S(1)}, bf16[40,4352]{1,0:T(8,128)(2,1)S(1)}, u32[]{:S(2)}, u32[]{:S(2)}) collective-permute-start(bf16[40,4352]{1,0:T(8,128)(2,1)S(1)} %get-tuple-element.70), channel_id=1, source_target_pairs={{0,2},{2,0},{4,6},{6,4},{8,10},{10,8},{12,14},{14,12},{16,18},{18,... | collective-permute-start | bytes 1044488 | tf_op jit(solution)/shard_map/ppermute | solution.py:416
  143.7 1.2 collective-permute-done.22.refs_1_
  145.1 8.1 %ffn.4 = (bf16[40,4352]{1,0:T(8,128)(2,1)S(1)}, bf16[40,4352]{1,0:T(8,128)(2,1)S(1)}, bf16[40,4352]{1,0:T(8,128)(2,1)S(1)}, bf16[40,4352]{1,0:T(8,128)(2,1)S(1)}) custom-call(bf16[40,4352]{1,0:T(8,128)(2,1)S(1)} %copy-done.5, bf16[40,4352]{1,0:T(8,128)(2,1)S(1)} %collective-permute-done.refs_1_, bf16[40,4352]{1,0:T(8,128)(2,1)S(1)} %collective-permute-done.1.refs_2_, ...), custom_call_target="tpu_custom_call" | custom-call | flops 3623878656 | bytes 22020096 | tf_op jit(solution)/shard_map/ffn/pallas_call | solution.py:376
  153.2 2.1 %collective-permute-start.6 = (bf16[40,4352]{1,0:T(8,128)(2,1)S(1)}, bf16[40,4352]{1,0:T(8,128)(2,1)S(1)}, u32[]{:S(2)}, u32[]{:S(2)}) collective-permute-start(bf16[40,4352]{1,0:T(8,128)(2,1)S(1)} %get-tuple-element.45), channel_id=1, source_target_pairs={{0,2},{2,0},{4,6},{6,4},{8,10},{10,8},{12,14},{14,12},{16,18},{18,... | collective-permute-start | bytes 1044488 | tf_op jit(solution)/shard_map/ppermute | solution.py:416
  155.3 1.4 combine.5
  156.9 1.2 combine.6
  158.1 3.3 %collective-permute-start.25 = (bf16[64,4096]{1,0:T(8,128)(2,1)S(1)}, bf16[64,4096]{1,0:T(8,128)(2,1)S(1)}, u32[]{:S(2)}, u32[]{:S(2)}) collective-permute-start(bf16[64,4096]{1,0:T(8,128)(2,1)S(1)} %combine.6), channel_id=1, source_target_pairs={{0,16},{2,18},{4,20},{6,22},{8,24},{10,26},{12,28},{14,30},{16,0},... | collective-permute-start | bytes 1572872 | tf_op jit(solution)/shard_map/ppermute | solution.py:416
  161.4 1.2 combine.7
  162.7 0.6 collective-permute-start.33
  163.3 1.3 collective-permute-start.7
  164.8 5.1 %attend.2.refs_4_ = f32[64,2048]{1,0:T(8,128)S(1)} custom-call(bf16[64,4096]{1,0:T(8,128)(2,1)} %q_ref.3, bf16[64,256]{1,0:T(8,128)(2,1)} %keys_ref.3, bf16[64,256]{1,0:T(8,128)(2,1)} %values_ref.3, bf16[1024,256]{1,0:T(8,128)(2,1)} %pkeys_ref.3, bf16[1024,256]{1,0:T(8,128)(2,1)} %pvalues_ref.3, bf16[64,4096]{1,0:T(8,128)(2,1)} %tokens_ref.5), custom_call_target="tpu_custom_call" | custom-call | flops 570425344 | bytes 1048576 | tf_op jit(solution)/shard_map/attend/pallas_call | solution.py:53
  169.9 5.1 %attend.3.refs_5_ = f32[64,2048]{1,0:T(8,128)S(1)} custom-call(bf16[64,4096]{1,0:T(8,128)(2,1)} %q_ref.3, bf16[64,256]{1,0:T(8,128)(2,1)} %keys_ref.3, bf16[64,256]{1,0:T(8,128)(2,1)} %values_ref.3, bf16[1024,256]{1,0:T(8,128)(2,1)} %pkeys_ref.3, bf16[1024,256]{1,0:T(8,128)(2,1)} %pvalues_ref.3, bf16[64,4096]{1,0:T(8,128)(2,1)} %tokens_ref.5), custom_call_target="tpu_custom_call" | custom-call | flops 570425344 | bytes 1048576 | tf_op jit(solution)/shard_map/attend/pallas_call | solution.py:53
  175.0 3.2 %collective-permute-done.7.refs_2_ = bf16[40,4352]{1,0:T(8,128)(2,1)S(1)} collective-permute-done((bf16[40,4352]{1,0:T(8,128)(2,1)S(1)}, bf16[40,4352]{1,0:T(8,128)(2,1)S(1)}, u32[]{:S(2)}, u32[]{:S(2)}) %collective-permute-start.7) | collective-permute-done | bytes 348192 | tf_op jit(solution)/shard_map/ppermute | solution.py:416
  178.1 1.2 combine.4
  179.4 5.9 %collective-permute-done.25 = bf16[64,4096]{1,0:T(8,128)(2,1)S(1)} collective-permute-done((bf16[64,4096]{1,0:T(8,128)(2,1)S(1)}, bf16[64,4096]{1,0:T(8,128)(2,1)S(1)}, u32[]{:S(2)}, u32[]{:S(2)}) %collective-permute-start.25) | collective-permute-done | bytes 524320 | tf_op jit(solution)/shard_map/ppermute | solution.py:416
  185.2 9.7 %collective-permute-done.33 = bf16[64,4096]{1,0:T(8,128)(2,1)S(1)} collective-permute-done((bf16[64,4096]{1,0:T(8,128)(2,1)S(1)}, bf16[64,4096]{1,0:T(8,128)(2,1)S(1)}, u32[]{:S(2)}, u32[]{:S(2)}) %collective-permute-start.33) | collective-permute-done | bytes 524320 | tf_op jit(solution)/shard_map/ppermute | solution.py:416
  194.9 1.1 add_convert_fusion
  (49 shorter events, 5.0 us)
Async XLA Ops:
  0.0 89.7 %collective-permute-start.3 = (bf16[4096,384]{1,0:T(8,128)(2,1)}, bf16[4096,384]{1,0:T(8,128)(2,1)S(1)}, u32[]{:S(2)}, u32[]{:S(2)}) collective-permute-start(bf16[4096,384]{1,0:T(8,128)(2,1)} %bitcast.7), channel_id=1, source_target_pairs={{0,1},{1,0},{2,3},{3,2},{4,5},{5,4},{6,7},{7,6},{8,9},{9,8},{10,11... | collective-permute-start | bytes 9437192 | tf_op jit(solution)/shard_map/ppermute | solution.py:419
  0.0 93.1 %collective-permute-start.4 = (bf16[4096,384]{1,0:T(8,128)(2,1)}, bf16[4096,384]{1,0:T(8,128)(2,1)}, u32[]{:S(2)}, u32[]{:S(2)}) collective-permute-start(bf16[4096,384]{1,0:T(8,128)(2,1)} %bitcast.12), channel_id=1, source_target_pairs={{0,1},{1,0},{2,3},{3,2},{4,5},{5,4},{6,7},{7,6},{8,9},{9,8},{10,11... | collective-permute-start | bytes 9437192 | tf_op jit(solution)/shard_map/ppermute | solution.py:419
  0.5 92.6 %collective-permute-start.5 = (bf16[384,4096]{1,0:T(8,128)(2,1)}, bf16[384,4096]{1,0:T(8,128)(2,1)}, u32[]{:S(2)}, u32[]{:S(2)}) collective-permute-start(bf16[384,4096]{1,0:T(8,128)(2,1)} %bitcast.17), channel_id=1, source_target_pairs={{0,1},{1,0},{2,3},{3,2},{4,5},{5,4},{6,7},{7,6},{8,9},{9,8},{10,11... | collective-permute-start | bytes 9437192 | tf_op jit(solution)/shard_map/ppermute | solution.py:419
  0.5 15.4 %collective-permute-start.10 = (bf16[64,4096]{1,0:T(8,128)(2,1)}, bf16[64,4096]{1,0:T(8,128)(2,1)}, u32[]{:S(2)}, u32[]{:S(2)}) collective-permute-start(bf16[64,4096]{1,0:T(8,128)(2,1)} %tokens_ref.5), channel_id=1, source_target_pairs={{0,8},{2,10},{4,12},{6,14},{8,0},{10,2},{12,4},{14,6},{16,24},{18,... | collective-permute-start | bytes 1572872 | tf_op jit(solution)/shard_map/ppermute | solution.py:416
  4.2 11.2 %collective-permute-start.9 = (bf16[64,128]{1,0:T(8,128)(2,1)}, bf16[64,128]{1,0:T(8,128)(2,1)S(1)}, u32[]{:S(2)}, u32[]{:S(2)}) collective-permute-start(bf16[64,128]{1,0:T(8,128)(2,1)} %get-tuple-element.48), channel_id=1, source_target_pairs={{0,8},{2,10},{4,12},{6,14},{8,0},{10,2},{12,4},{14,6},{16,24},{18,... | collective-permute-start | bytes 49160 | tf_op jit(solution)/shard_map/ppermute | solution.py:416
  15.4 10.0 %collective-permute-start = (bf16[40,4352]{1,0:T(8,128)(2,1)}, bf16[40,4352]{1,0:T(8,128)(2,1)S(1)}, u32[]{:S(2)}, u32[]{:S(2)}) collective-permute-start(bf16[40,4352]{1,0:T(8,128)(2,1)} %get-tuple-element.41), channel_id=1, source_target_pairs={{0,2},{2,0},{4,6},{6,4},{8,10},{10,8},{12,14},{14,12},{16,18},{18,... | collective-permute-start | bytes 1044488 | tf_op jit(solution)/shard_map/ppermute | solution.py:416
  16.0 25.6 %collective-permute-start.18 = (bf16[64,4224]{1,0:T(8,128)(2,1)}, bf16[64,4224]{1,0:T(8,128)(2,1)S(1)}, u32[]{:S(2)}, u32[]{:S(2)}) collective-permute-start(bf16[64,4224]{1,0:T(8,128)(2,1)} %get-tuple-element.39.meta_ref), channel_id=1, source_target_pairs={{0,16},{2,18},{4,20},{6,22},{8,24},{10,26},{12,28},{14,30},{16,0},... | collective-permute-start | bytes 1622024 | tf_op jit(solution)/shard_map/ppermute | solution.py:416
  18.5 0.7 copy-start.6
  25.4 16.6 %collective-permute-start.11 = (bf16[40,4352]{1,0:T(8,128)(2,1)S(1)}, bf16[40,4352]{1,0:T(8,128)(2,1)S(1)}, u32[]{:S(2)}, u32[]{:S(2)}) collective-permute-start(bf16[40,4352]{1,0:T(8,128)(2,1)S(1)} %get-tuple-element.50), channel_id=1, source_target_pairs={{0,2},{2,0},{4,6},{6,4},{8,10},{10,8},{12,14},{14,12},{16,18},{18,... | collective-permute-start | bytes 1044488 | tf_op jit(solution)/shard_map/ppermute | solution.py:416
  41.5 17.5 %collective-permute-start.12 = (bf16[40,4352]{1,0:T(8,128)(2,1)S(1)}, bf16[40,4352]{1,0:T(8,128)(2,1)S(1)}, u32[]{:S(2)}, u32[]{:S(2)}) collective-permute-start(bf16[40,4352]{1,0:T(8,128)(2,1)S(1)} %get-tuple-element.51), channel_id=1, source_target_pairs={{0,4},{2,6},{4,0},{6,2},{8,12},{10,14},{12,8},{14,10},{16,20},{18,... | collective-permute-start | bytes 1044488 | tf_op jit(solution)/shard_map/ppermute | solution.py:416
  42.0 18.5 %collective-permute-start.13 = (bf16[40,4352]{1,0:T(8,128)(2,1)S(1)}, bf16[40,4352]{1,0:T(8,128)(2,1)S(1)}, u32[]{:S(2)}, u32[]{:S(2)}) collective-permute-start(bf16[40,4352]{1,0:T(8,128)(2,1)S(1)} %get-tuple-element.52), channel_id=1, source_target_pairs={{0,6},{2,4},{4,2},{6,0},{8,14},{10,12},{12,10},{14,8},{16,22},{18,... | collective-permute-start | bytes 1044488 | tf_op jit(solution)/shard_map/ppermute | solution.py:416
  59.0 9.2 %collective-permute-start.19 = (bf16[40,4352]{1,0:T(8,128)(2,1)S(1)}, bf16[40,4352]{1,0:T(8,128)(2,1)S(1)}, u32[]{:S(2)}, u32[]{:S(2)}) collective-permute-start(bf16[40,4352]{1,0:T(8,128)(2,1)S(1)} %get-tuple-element.58), channel_id=1, source_target_pairs={{0,2},{2,0},{4,6},{6,4},{8,10},{10,8},{12,14},{14,12},{16,18},{18,... | collective-permute-start | bytes 1044488 | tf_op jit(solution)/shard_map/ppermute | solution.py:416
  60.5 13.1 %collective-permute-start.26 = (bf16[64,4224]{1,0:T(8,128)(2,1)S(1)}, bf16[64,4224]{1,0:T(8,128)(2,1)S(1)}, u32[]{:S(2)}, u32[]{:S(2)}) collective-permute-start(bf16[64,4224]{1,0:T(8,128)(2,1)S(1)} %collective-permute-done.18.base_ref.meta_ref), channel_id=1, source_target_pairs={{0,8},{2,10},{4,12},{6,14},{8,0},{10,2},{12,4},{14,6},{16,24},{18,... | collective-permute-start | bytes 1622024 | tf_op jit(solution)/shard_map/ppermute | solution.py:416
  68.3 20.9 %collective-permute-start.20 = (bf16[40,4352]{1,0:T(8,128)(2,1)S(1)}, bf16[40,4352]{1,0:T(8,128)(2,1)S(1)}, u32[]{:S(2)}, u32[]{:S(2)}) collective-permute-start(bf16[40,4352]{1,0:T(8,128)(2,1)S(1)} %get-tuple-element.59), channel_id=1, source_target_pairs={{0,4},{2,6},{4,0},{6,2},{8,12},{10,14},{12,8},{14,10},{16,20},{18,... | collective-permute-start | bytes 1044488 | tf_op jit(solution)/shard_map/ppermute | solution.py:416
  73.6 33.9 %collective-permute-start.21 = (bf16[40,4352]{1,0:T(8,128)(2,1)S(1)}, bf16[40,4352]{1,0:T(8,128)(2,1)S(1)}, u32[]{:S(2)}, u32[]{:S(2)}) collective-permute-start(bf16[40,4352]{1,0:T(8,128)(2,1)S(1)} %get-tuple-element.60), channel_id=1, source_target_pairs={{0,6},{2,4},{4,2},{6,0},{8,14},{10,12},{12,10},{14,8},{16,22},{18,... | collective-permute-start | bytes 1044488 | tf_op jit(solution)/shard_map/ppermute | solution.py:416
  89.2 29.7 %collective-permute-start.1 = (bf16[40,4352]{1,0:T(8,128)(2,1)}, bf16[40,4352]{1,0:T(8,128)(2,1)S(1)}, u32[]{:S(2)}, u32[]{:S(2)}) collective-permute-start(bf16[40,4352]{1,0:T(8,128)(2,1)} %get-tuple-element.42), channel_id=1, source_target_pairs={{0,4},{2,6},{4,0},{6,2},{8,12},{10,14},{12,8},{14,10},{16,20},{18,... | collective-permute-start | bytes 1044488 | tf_op jit(solution)/shard_map/ppermute | solution.py:416
  89.7 29.3 %collective-permute-start.2 = (bf16[40,4352]{1,0:T(8,128)(2,1)}, bf16[40,4352]{1,0:T(8,128)(2,1)S(1)}, u32[]{:S(2)}, u32[]{:S(2)}) collective-permute-start(bf16[40,4352]{1,0:T(8,128)(2,1)} %get-tuple-element.43), channel_id=1, source_target_pairs={{0,6},{2,4},{4,2},{6,0},{8,14},{10,12},{12,10},{14,8},{16,22},{18,... | collective-permute-start | bytes 1044488 | tf_op jit(solution)/shard_map/ppermute | solution.py:416
  93.1 26.4 %collective-permute-start.27 = (bf16[40,4352]{1,0:T(8,128)(2,1)S(1)}, bf16[40,4352]{1,0:T(8,128)(2,1)S(1)}, u32[]{:S(2)}, u32[]{:S(2)}) collective-permute-start(bf16[40,4352]{1,0:T(8,128)(2,1)S(1)} %get-tuple-element.66), channel_id=1, source_target_pairs={{0,2},{2,0},{4,6},{6,4},{8,10},{10,8},{12,14},{14,12},{16,18},{18,... | collective-permute-start | bytes 1044488 | tf_op jit(solution)/shard_map/ppermute | solution.py:416
  93.1 33.4 %collective-permute-start.28 = (bf16[40,4352]{1,0:T(8,128)(2,1)S(1)}, bf16[40,4352]{1,0:T(8,128)(2,1)S(1)}, u32[]{:S(2)}, u32[]{:S(2)}) collective-permute-start(bf16[40,4352]{1,0:T(8,128)(2,1)S(1)} %get-tuple-element.67), channel_id=1, source_target_pairs={{0,4},{2,6},{4,0},{6,2},{8,12},{10,14},{12,8},{14,10},{16,20},{18,... | collective-permute-start | bytes 1044488 | tf_op jit(solution)/shard_map/ppermute | solution.py:416
  93.8 1.9 copy-start
  95.7 1.9 copy-start.2
  97.5 1.9 copy-start.3
  107.5 21.3 %collective-permute-start.29 = (bf16[40,4352]{1,0:T(8,128)(2,1)S(1)}, bf16[40,4352]{1,0:T(8,128)(2,1)S(1)}, u32[]{:S(2)}, u32[]{:S(2)}) collective-permute-start(bf16[40,4352]{1,0:T(8,128)(2,1)S(1)} %get-tuple-element.68), channel_id=1, source_target_pairs={{0,6},{2,4},{4,2},{6,0},{8,14},{10,12},{12,10},{14,8},{16,22},{18,... | collective-permute-start | bytes 1044488 | tf_op jit(solution)/shard_map/ppermute | solution.py:416
  110.4 18.4 %copy-start.1 = (bf16[1,4096,384]{2,1,0:T(8,128)(2,1)S(1)}, bf16[1,4096,384]{2,1,0:T(8,128)(2,1)}, u32[]{:S(2)}) copy-start(bf16[1,4096,384]{2,1,0:T(8,128)(2,1)} %param.22) | copy-start | bytes 9437188
  118.9 18.0 %collective-permute-start.14 = (bf16[40,4352]{1,0:T(8,128)(2,1)S(1)}, bf16[40,4352]{1,0:T(8,128)(2,1)S(1)}, u32[]{:S(2)}, u32[]{:S(2)}) collective-permute-start(bf16[40,4352]{1,0:T(8,128)(2,1)S(1)} %get-tuple-element.54), channel_id=1, source_target_pairs={{0,2},{2,0},{4,6},{6,4},{8,10},{10,8},{12,14},{14,12},{16,18},{18,... | collective-permute-start | bytes 1044488 | tf_op jit(solution)/shard_map/ppermute | solution.py:416
  119.0 22.5 %collective-permute-start.15 = (bf16[40,4352]{1,0:T(8,128)(2,1)S(1)}, bf16[40,4352]{1,0:T(8,128)(2,1)S(1)}, u32[]{:S(2)}, u32[]{:S(2)}) collective-permute-start(bf16[40,4352]{1,0:T(8,128)(2,1)S(1)} %get-tuple-element.55), channel_id=1, source_target_pairs={{0,4},{2,6},{4,0},{6,2},{8,12},{10,14},{12,8},{14,10},{16,20},{18,... | collective-permute-start | bytes 1044488 | tf_op jit(solution)/shard_map/ppermute | solution.py:416
  119.6 24.1 %collective-permute-start.16 = (bf16[40,4352]{1,0:T(8,128)(2,1)S(1)}, bf16[40,4352]{1,0:T(8,128)(2,1)S(1)}, u32[]{:S(2)}, u32[]{:S(2)}) collective-permute-start(bf16[40,4352]{1,0:T(8,128)(2,1)S(1)} %get-tuple-element.56), channel_id=1, source_target_pairs={{0,6},{2,4},{4,2},{6,0},{8,14},{10,12},{12,10},{14,8},{16,22},{18,... | collective-permute-start | bytes 1044488 | tf_op jit(solution)/shard_map/ppermute | solution.py:416
  126.5 18.4 %collective-permute-start.22 = (bf16[40,4352]{1,0:T(8,128)(2,1)S(1)}, bf16[40,4352]{1,0:T(8,128)(2,1)S(1)}, u32[]{:S(2)}, u32[]{:S(2)}) collective-permute-start(bf16[40,4352]{1,0:T(8,128)(2,1)S(1)} %get-tuple-element.62), channel_id=1, source_target_pairs={{0,2},{2,0},{4,6},{6,4},{8,10},{10,8},{12,14},{14,12},{16,18},{18,... | collective-permute-start | bytes 1044488 | tf_op jit(solution)/shard_map/ppermute | solution.py:416
  128.8 24.5 %collective-permute-start.23 = (bf16[40,4352]{1,0:T(8,128)(2,1)S(1)}, bf16[40,4352]{1,0:T(8,128)(2,1)S(1)}, u32[]{:S(2)}, u32[]{:S(2)}) collective-permute-start(bf16[40,4352]{1,0:T(8,128)(2,1)S(1)} %get-tuple-element.63), channel_id=1, source_target_pairs={{0,4},{2,6},{4,0},{6,2},{8,12},{10,14},{12,8},{14,10},{16,20},{18,... | collective-permute-start | bytes 1044488 | tf_op jit(solution)/shard_map/ppermute | solution.py:416
  128.8 16.4 %copy-start.5 = (bf16[40,4352]{1,0:T(8,128)(2,1)S(1)}, bf16[40,4352]{1,0:T(8,128)(2,1)}, u32[]{:S(2)}) copy-start(bf16[40,4352]{1,0:T(8,128)(2,1)} %get-tuple-element.40.refs_0_) | copy-start | bytes 1044484
  136.9 19.9 %collective-permute-start.24 = (bf16[40,4352]{1,0:T(8,128)(2,1)S(1)}, bf16[40,4352]{1,0:T(8,128)(2,1)S(1)}, u32[]{:S(2)}, u32[]{:S(2)}) collective-permute-start(bf16[40,4352]{1,0:T(8,128)(2,1)S(1)} %get-tuple-element.64), channel_id=1, source_target_pairs={{0,6},{2,4},{4,2},{6,0},{8,14},{10,12},{12,10},{14,8},{16,22},{18,... | collective-permute-start | bytes 1044488 | tf_op jit(solution)/shard_map/ppermute | solution.py:416
  141.5 16.6 %collective-permute-start.30 = (bf16[40,4352]{1,0:T(8,128)(2,1)S(1)}, bf16[40,4352]{1,0:T(8,128)(2,1)S(1)}, u32[]{:S(2)}, u32[]{:S(2)}) collective-permute-start(bf16[40,4352]{1,0:T(8,128)(2,1)S(1)} %get-tuple-element.70), channel_id=1, source_target_pairs={{0,2},{2,0},{4,6},{6,4},{8,10},{10,8},{12,14},{14,12},{16,18},{18,... | collective-permute-start | bytes 1044488 | tf_op jit(solution)/shard_map/ppermute | solution.py:416
  143.7 17.8 %collective-permute-start.31 = (bf16[40,4352]{1,0:T(8,128)(2,1)S(1)}, bf16[40,4352]{1,0:T(8,128)(2,1)S(1)}, u32[]{:S(2)}, u32[]{:S(2)}) collective-permute-start(bf16[40,4352]{1,0:T(8,128)(2,1)S(1)} %get-tuple-element.71), channel_id=1, source_target_pairs={{0,4},{2,6},{4,0},{6,2},{8,12},{10,14},{12,8},{14,10},{16,20},{18,... | collective-permute-start | bytes 1044488 | tf_op jit(solution)/shard_map/ppermute | solution.py:416
  144.9 16.5 %collective-permute-start.32 = (bf16[40,4352]{1,0:T(8,128)(2,1)S(1)}, bf16[40,4352]{1,0:T(8,128)(2,1)S(1)}, u32[]{:S(2)}, u32[]{:S(2)}) collective-permute-start(bf16[40,4352]{1,0:T(8,128)(2,1)S(1)} %get-tuple-element.72), channel_id=1, source_target_pairs={{0,6},{2,4},{4,2},{6,0},{8,14},{10,12},{12,10},{14,8},{16,22},{18,... | collective-permute-start | bytes 1044488 | tf_op jit(solution)/shard_map/ppermute | solution.py:416
  153.2 11.4 %collective-permute-start.6 = (bf16[40,4352]{1,0:T(8,128)(2,1)S(1)}, bf16[40,4352]{1,0:T(8,128)(2,1)S(1)}, u32[]{:S(2)}, u32[]{:S(2)}) collective-permute-start(bf16[40,4352]{1,0:T(8,128)(2,1)S(1)} %get-tuple-element.45), channel_id=1, source_target_pairs={{0,2},{2,0},{4,6},{6,4},{8,10},{10,8},{12,14},{14,12},{16,18},{18,... | collective-permute-start | bytes 1044488 | tf_op jit(solution)/shard_map/ppermute | solution.py:416
  156.8 22.6 %collective-permute-start.17 = (bf16[64,4096]{1,0:T(8,128)(2,1)S(1)}, bf16[64,4096]{1,0:T(8,128)(2,1)S(1)}, u32[]{:S(2)}, u32[]{:S(2)}) collective-permute-start(bf16[64,4096]{1,0:T(8,128)(2,1)S(1)} %combine.5), channel_id=1, source_target_pairs={{0,8},{2,10},{4,12},{6,14},{8,0},{10,2},{12,4},{14,6},{16,24},{18,... | collective-permute-start | bytes 1572872 | tf_op jit(solution)/shard_map/ppermute | solution.py:416
  158.1 27.1 %collective-permute-start.25 = (bf16[64,4096]{1,0:T(8,128)(2,1)S(1)}, bf16[64,4096]{1,0:T(8,128)(2,1)S(1)}, u32[]{:S(2)}, u32[]{:S(2)}) collective-permute-start(bf16[64,4096]{1,0:T(8,128)(2,1)S(1)} %combine.6), channel_id=1, source_target_pairs={{0,16},{2,18},{4,20},{6,22},{8,24},{10,26},{12,28},{14,30},{16,0},... | collective-permute-start | bytes 1572872 | tf_op jit(solution)/shard_map/ppermute | solution.py:416
  162.7 15.5 %copy-start.4 = (bf16[64,4224]{1,0:T(8,128)(2,1)S(1)}, bf16[64,4224]{1,0:T(8,128)(2,1)}, u32[]{:S(2)}) copy-start(bf16[64,4224]{1,0:T(8,128)(2,1)} %get-tuple-element.39.meta_ref) | copy-start | bytes 1622020
  162.7 32.2 %collective-permute-start.33 = (bf16[64,4096]{1,0:T(8,128)(2,1)S(1)}, bf16[64,4096]{1,0:T(8,128)(2,1)S(1)}, u32[]{:S(2)}, u32[]{:S(2)}) collective-permute-start(bf16[64,4096]{1,0:T(8,128)(2,1)S(1)} %combine.7), channel_id=1, source_target_pairs={{0,24},{2,26},{4,28},{6,30},{8,16},{10,18},{12,20},{14,22},{16,8},... | collective-permute-start | bytes 1572872 | tf_op jit(solution)/shard_map/ppermute | solution.py:416
  163.3 14.8 %collective-permute-start.7 = (bf16[40,4352]{1,0:T(8,128)(2,1)S(1)}, bf16[40,4352]{1,0:T(8,128)(2,1)S(1)}, u32[]{:S(2)}, u32[]{:S(2)}) collective-permute-start(bf16[40,4352]{1,0:T(8,128)(2,1)S(1)} %get-tuple-element.46), channel_id=1, source_target_pairs={{0,4},{2,6},{4,0},{6,2},{8,12},{10,14},{12,8},{14,10},{16,20},{18,... | collective-permute-start | bytes 1044488 | tf_op jit(solution)/shard_map/ppermute | solution.py:416
  164.6 13.5 %collective-permute-start.8 = (bf16[40,4352]{1,0:T(8,128)(2,1)S(1)}, bf16[40,4352]{1,0:T(8,128)(2,1)S(1)}, u32[]{:S(2)}, u32[]{:S(2)}) collective-permute-start(bf16[40,4352]{1,0:T(8,128)(2,1)S(1)} %get-tuple-element.47), channel_id=1, source_target_pairs={{0,6},{2,4},{4,2},{6,0},{8,14},{10,12},{12,10},{14,8},{16,22},{18,... | collective-permute-start | bytes 1044488 | tf_op jit(solution)/shard_map/ppermute | solution.py:416

commit v3 on v2

--- a/solution.py
+++ b/solution.py
@@ -455,17 +455,22 @@
             lanes = swap(meta, 4)
             gather(1, (swap(tokens, 4), lanes, norm_gain.reshape(1, -1)))
             bases[1] = lanes
-            gather(2, swap(payload, 8))
+            gather(3, swap(payload, 12))
+            gather(2, swap(bases[3], 4))
         else:
             gather(first, swap(payload, 4 * first))
             gather(first + 1, swap(payload, 4 * first + 4))
             gather(first + 2, swap(payload, 4 * first + 8))
-        gather(first + 3, swap(bases[first + 2], 4))
+            gather(first + 3, swap(bases[first + 2], 4))
     for k in range(columns):
         serve(k)
     sums = []
-    for k in range(1, columns):
-        sums.append(swap(collect(k), 4 * k))
+    for first in range(0, columns, 4):
+        passed = swap(collect(first + 3), 4)
+        sums.append(swap(collect(first + 2, (passed,)), 4 * first + 8))
+        sums.append(swap(collect(first + 1), 4 * first + 4))
+        if first:
+            sums.append(swap(collect(first), 4 * first))
     result = collect(0, result, f32)
     for part in sums:
         result = result + part.astype(f32)

time: 198 us -> 186 us (0.939)
  waiting for transfers between devices: 96.8 us -> 86.9 us
  starting transfers between devices: 36.6 us -> 34 us
    ppermute x31, waiting for transfers between devices: 96.8 us -> 86.9 us  [swap(): lax.ppermute(value, 'expert', [(i, i ^ offset) for i in range(owners)])]
    ppermute x31, starting transfers between devices: 36.1 us -> 33.5 us  [swap(): lax.ppermute(value, 'expert', [(i, i ^ offset) for i in range(owners)])]
    unnamed x14 -> x20, local copies, waits for them, and re-layouts: 6.4 us -> 6.41 us
  transfers between devices with their start and end apart: 34 -> 34, of which waited for: 13 -> 10; matrix products, arithmetic and copies ran while one was open for 0% -> 0% of each run, Pallas kernels for 28% -> 30%
where the time goes in v3:
time: 186 us; the launch traced here: 184 us
  waiting for transfers between devices  86.9 us (47%)
  Pallas kernels  55 us (30%)
  starting transfers between devices  34 us (18%)
  local copies, waits for them, and re-layouts  6.41 us (3%)
    ppermute x31, waiting for transfers between devices, swap(): lax.ppermute(value, 'expert', [(i, i ^ offset) for i in range(owners)])  86.9 us
    ppermute x31, starting transfers between devices, swap(): lax.ppermute(value, 'expert', [(i, i ^ offset) for i in range(owners)])  33.5 us
    pallas_call x4, Pallas kernels, run_ffn(): pl.pallas_call(functools.partial(ffn_kernel, count), out_shape=[packed_sh...  32.9 us
    pallas_call x2, Pallas kernels, attend(): pl.pallas_call(functools.partial(attend_kernel, heads), grid=(steps,), ou...  10.1 us
    unnamed x20, local copies, waits for them, and re-layouts  6.41 us
    pallas_call x4, Pallas kernels, combine(): pl.pallas_call(functools.partial(combine_kernel, len(terms), experts, cou...  4.91 us
    pallas_call x3, Pallas kernels, dispatch(): pl.pallas_call(functools.partial(raw_dispatch_kernel if raw else dispatch...  3.74 us
  transfers between devices with their start and end apart: 34, of which 10 were waited for; matrix products, arithmetic and copies ran while one was open for 0% of the time, Pallas kernels for 30%

profile of v3, /device:TPU:14, one launch (start us, length us, event | category | flops | bytes accessed | tf_op | source)
XLA Modules:
  0.0 183.5 jit_solution(12499301490005731338)
XLA Ops:
  1.0 3.3 %payload.1 = (bf16[64,4224]{1,0:T(8,128)(2,1)}, bf16[64,128]{1,0:T(8,128)(2,1)}, bf16[40,4352]{1,0:T(8,128)(2,1)}, bf16[40,4352]{1,0:T(8,128)(2,1)}, bf16[40,4352]{1,0:T(8,128)(2,1)}, /*index=5*/bf16[40,4352]{1,0:T(8,128)(2,1)}) custom-call(s32[1]{0:T(128)} %bitcast.slot_ref, s32[16]{0:T(128)} %holder_ref.1, bf16[64,4096]{1,0:T(8,128)(2,1)} %tokens_ref.5, ...), custom_call_target="tpu_custom_call" | custom-call | tf_op jit(solution)/shard_map/payload/pallas_call | solution.py:234
  4.3 1.6 collective-permute-start.25
  5.8 9.6 %collective-permute-done.25.meta_ref = bf16[64,128]{1,0:T(8,128)(2,1)S(1)} collective-permute-done((bf16[64,128]{1,0:T(8,128)(2,1)}, bf16[64,128]{1,0:T(8,128)(2,1)S(1)}, u32[]{:S(2)}, u32[]{:S(2)}) %collective-permute-start.25) | collective-permute-done | bytes 16416 | tf_op jit(solution)/shard_map/ppermute | solution.py:416
  15.4 1.6 collective-permute-start.9
  17.0 0.7 copy-done.6
  17.7 2.0 %dispatch.5 = (bf16[40,4352]{1,0:T(8,128)(2,1)S(1)}, bf16[40,4352]{1,0:T(8,128)(2,1)S(1)}, bf16[40,4352]{1,0:T(8,128)(2,1)S(1)}, bf16[40,4352]{1,0:T(8,128)(2,1)S(1)}) custom-call(s32[1]{0:T(128)} %bitcast.slot_ref, bf16[64,4096]{1,0:T(8,128)(2,1)} %collective-permute-done.26.tokens_ref, bf16[64,128]{1,0:T(8,128)(2,1)S(1)} %collective-permute-done.25.meta_ref, ...), custom_call_target="tpu_custom_call" | custom-call | flops 88080384 | bytes 1900544 | tf_op jit(solution)/shard_map/dispatch/pallas_call | solution.py:267
  19.7 0.6 collective-permute-start.27
  20.3 20.9 %collective-permute-done.9.base_ref.meta_ref = bf16[64,4224]{1,0:T(8,128)(2,1)S(1)} collective-permute-done((bf16[64,4224]{1,0:T(8,128)(2,1)}, bf16[64,4224]{1,0:T(8,128)(2,1)S(1)}, u32[]{:S(2)}, u32[]{:S(2)}) %collective-permute-start.9) | collective-permute-done | bytes 540704 | tf_op jit(solution)/shard_map/ppermute | solution.py:416
  41.1 0.9 dispatch.4
  42.0 0.6 collective-permute-start.17
  42.6 8.7 %collective-permute-done.17.refs_1_ = bf16[40,4352]{1,0:T(8,128)(2,1)S(1)} collective-permute-done((bf16[40,4352]{1,0:T(8,128)(2,1)S(1)}, bf16[40,4352]{1,0:T(8,128)(2,1)S(1)}, u32[]{:S(2)}, u32[]{:S(2)}) %collective-permute-start.17) | collective-permute-done | bytes 348192 | tf_op jit(solution)/shard_map/ppermute | solution.py:416
  51.8 2.6 %collective-permute-done.10.base_ref.meta_ref = bf16[64,4224]{1,0:T(8,128)(2,1)S(1)} collective-permute-done((bf16[64,4224]{1,0:T(8,128)(2,1)S(1)}, bf16[64,4224]{1,0:T(8,128)(2,1)S(1)}, u32[]{:S(2)}, u32[]{:S(2)}) %collective-permute-start.10) | collective-permute-done | bytes 540704 | tf_op jit(solution)/shard_map/ppermute | solution.py:416
  54.9 0.9 dispatch.3
  55.8 11.3 %collective-permute-done.18.refs_2_ = bf16[40,4352]{1,0:T(8,128)(2,1)S(1)} collective-permute-done((bf16[40,4352]{1,0:T(8,128)(2,1)S(1)}, bf16[40,4352]{1,0:T(8,128)(2,1)S(1)}, u32[]{:S(2)}, u32[]{:S(2)}) %collective-permute-start.18) | collective-permute-done | bytes 348192 | tf_op jit(solution)/shard_map/ppermute | solution.py:416
  67.2 0.5 collective-permute-start.11
  68.1 2.5 %collective-permute-start.13 = (bf16[40,4352]{1,0:T(8,128)(2,1)S(1)}, bf16[40,4352]{1,0:T(8,128)(2,1)S(1)}, u32[]{:S(2)}, u32[]{:S(2)}) collective-permute-start(bf16[40,4352]{1,0:T(8,128)(2,1)S(1)} %get-tuple-element.51), channel_id=1, source_target_pairs={{0,6},{2,4},{4,2},{6,0},{8,14},{10,12},{12,10},{14,8},{16,22},{18,... | collective-permute-start | bytes 1044488 | tf_op jit(solution)/shard_map/ppermute | solution.py:416
  71.2 1.5 collective-permute-start.29
  72.7 1.9 %copy-done = bf16[1,4096,384]{2,1,0:T(8,128)(2,1)S(1)} copy-done((bf16[1,4096,384]{2,1,0:T(8,128)(2,1)S(1)}, bf16[1,4096,384]{2,1,0:T(8,128)(2,1)}, u32[]{:S(2)}) %copy-start) | copy-done | bytes 3145752
  74.6 1.9 %copy-done.2 = bf16[1,4096,384]{2,1,0:T(8,128)(2,1)S(1)} copy-done((bf16[1,4096,384]{2,1,0:T(8,128)(2,1)S(1)}, bf16[1,4096,384]{2,1,0:T(8,128)(2,1)}, u32[]{:S(2)}) %copy-start.2) | copy-done | bytes 3145752
  76.5 1.9 %copy-done.3 = bf16[1,384,4096]{2,1,0:T(8,128)(2,1)S(1)} copy-done((bf16[1,384,4096]{2,1,0:T(8,128)(2,1)S(1)}, bf16[1,384,4096]{2,1,0:T(8,128)(2,1)}, u32[]{:S(2)}) %copy-start.3) | copy-done | bytes 3145752
  78.3 8.0 %ffn.6 = (bf16[40,4352]{1,0:T(8,128)(2,1)S(1)}, bf16[40,4352]{1,0:T(8,128)(2,1)S(1)}, bf16[40,4352]{1,0:T(8,128)(2,1)S(1)}, bf16[40,4352]{1,0:T(8,128)(2,1)S(1)}) custom-call(bf16[40,4352]{1,0:T(8,128)(2,1)S(1)} %get-tuple-element.56.refs_0_, bf16[40,4352]{1,0:T(8,128)(2,1)S(1)} %collective-permute-done.17.refs_1_, ...), custom_call_target="tpu_custom_call" | custom-call | flops 3623878656 | bytes 22020096 | tf_op jit(solution)/shard_map/ffn/pallas_call | solution.py:376
  86.4 1.6 collective-permute-start.20
  88.0 5.6 %collective-permute-done.12.refs_2_ = bf16[40,4352]{1,0:T(8,128)(2,1)S(1)} collective-permute-done((bf16[40,4352]{1,0:T(8,128)(2,1)S(1)}, bf16[40,4352]{1,0:T(8,128)(2,1)S(1)}, u32[]{:S(2)}, u32[]{:S(2)}) %collective-permute-start.12) | collective-permute-done | bytes 348192 | tf_op jit(solution)/shard_map/ppermute | solution.py:416
  93.6 2.8 %collective-permute-start.22 = (bf16[40,4352]{1,0:T(8,128)(2,1)S(1)}, bf16[40,4352]{1,0:T(8,128)(2,1)S(1)}, u32[]{:S(2)}, u32[]{:S(2)}) collective-permute-start(bf16[40,4352]{1,0:T(8,128)(2,1)S(1)} %get-tuple-element.63), channel_id=1, source_target_pairs={{0,6},{2,4},{4,2},{6,0},{8,14},{10,12},{12,10},{14,8},{16,22},{18,... | collective-permute-start | bytes 1044488 | tf_op jit(solution)/shard_map/ppermute | solution.py:416
  96.4 8.4 %ffn.5 = (bf16[40,4352]{1,0:T(8,128)(2,1)S(1)}, bf16[40,4352]{1,0:T(8,128)(2,1)S(1)}, bf16[40,4352]{1,0:T(8,128)(2,1)S(1)}, bf16[40,4352]{1,0:T(8,128)(2,1)S(1)}) custom-call(bf16[40,4352]{1,0:T(8,128)(2,1)S(1)} %get-tuple-element.48.refs_0_, bf16[40,4352]{1,0:T(8,128)(2,1)S(1)} %collective-permute-done.11.refs_1_, ...), custom_call_target="tpu_custom_call" | custom-call | flops 3623878656 | bytes 22020096 | tf_op jit(solution)/shard_map/ffn/pallas_call | solution.py:376
  104.8 3.6 %collective-permute-done.28.refs_2_ = bf16[40,4352]{1,0:T(8,128)(2,1)S(1)} collective-permute-done((bf16[40,4352]{1,0:T(8,128)(2,1)S(1)}, bf16[40,4352]{1,0:T(8,128)(2,1)S(1)}, u32[]{:S(2)}, u32[]{:S(2)}) %collective-permute-start.28) | collective-permute-done | bytes 348192 | tf_op jit(solution)/shard_map/ppermute | solution.py:416
  108.5 0.9 collective-permute-start.14
  109.4 1.1 collective-permute-start.15
  110.5 8.1 %ffn.7 = (bf16[40,4352]{1,0:T(8,128)(2,1)S(1)}, bf16[40,4352]{1,0:T(8,128)(2,1)S(1)}, bf16[40,4352]{1,0:T(8,128)(2,1)S(1)}, bf16[40,4352]{1,0:T(8,128)(2,1)S(1)}) custom-call(bf16[40,4352]{1,0:T(8,128)(2,1)S(1)} %get-tuple-element.65.refs_0_, bf16[40,4352]{1,0:T(8,128)(2,1)S(1)} %collective-permute-done.27.refs_1_, ...), custom_call_target="tpu_custom_call" | custom-call | flops 3623878656 | bytes 22020096 | tf_op jit(solution)/shard_map/ffn/pallas_call | solution.py:376
  118.8 2.0 %collective-permute-start.31 = (bf16[40,4352]{1,0:T(8,128)(2,1)S(1)}, bf16[40,4352]{1,0:T(8,128)(2,1)S(1)}, u32[]{:S(2)}, u32[]{:S(2)}) collective-permute-start(bf16[40,4352]{1,0:T(8,128)(2,1)S(1)} %get-tuple-element.71), channel_id=1, source_target_pairs={{0,4},{2,6},{4,0},{6,2},{8,12},{10,14},{12,8},{14,10},{16,20},{18,... | collective-permute-start | bytes 1044488 | tf_op jit(solution)/shard_map/ppermute | solution.py:416
  120.8 1.5 collective-permute-start.32
  122.3 1.2 combine.5
  123.5 1.3 collective-permute-start.23
  124.8 6.8 %collective-permute-done.15.refs_2_ = bf16[40,4352]{1,0:T(8,128)(2,1)S(1)} collective-permute-done((bf16[40,4352]{1,0:T(8,128)(2,1)S(1)}, bf16[40,4352]{1,0:T(8,128)(2,1)S(1)}, u32[]{:S(2)}, u32[]{:S(2)}) %collective-permute-start.15) | collective-permute-done | bytes 348192 | tf_op jit(solution)/shard_map/ppermute | solution.py:416
  131.6 3.3 %collective-permute-start.16 = (bf16[40,4352]{1,0:T(8,128)(2,1)S(1)}, bf16[40,4352]{1,0:T(8,128)(2,1)S(1)}, u32[]{:S(2)}, u32[]{:S(2)}) collective-permute-start(bf16[40,4352]{1,0:T(8,128)(2,1)S(1)} %get-tuple-element.55), channel_id=1, source_target_pairs={{0,6},{2,4},{4,2},{6,0},{8,14},{10,12},{12,10},{14,8},{16,22},{18,... | collective-permute-start | bytes 1044488 | tf_op jit(solution)/shard_map/ppermute | solution.py:416
  134.9 13.3 %collective-permute-done.31.refs_2_ = bf16[40,4352]{1,0:T(8,128)(2,1)S(1)} collective-permute-done((bf16[40,4352]{1,0:T(8,128)(2,1)S(1)}, bf16[40,4352]{1,0:T(8,128)(2,1)S(1)}, u32[]{:S(2)}, u32[]{:S(2)}) %collective-permute-start.31) | collective-permute-done | bytes 348192 | tf_op jit(solution)/shard_map/ppermute | solution.py:416
  148.4 1.6 collective-permute-start.2
  150.0 1.2 combine.7
  151.2 1.1 collective-permute-start.33
  152.3 1.3 combine.6
  153.6 1.3 collective-permute-start.24
  154.9 4.3 %collective-permute-done.1.refs_2_ = bf16[40,4352]{1,0:T(8,128)(2,1)S(1)} collective-permute-done((bf16[40,4352]{1,0:T(8,128)(2,1)S(1)}, bf16[40,4352]{1,0:T(8,128)(2,1)S(1)}, u32[]{:S(2)}, u32[]{:S(2)}) %collective-permute-start.1) | collective-permute-done | bytes 348192 | tf_op jit(solution)/shard_map/ppermute | solution.py:416
  159.2 8.3 %ffn.4 = (bf16[40,4352]{1,0:T(8,128)(2,1)S(1)}, bf16[40,4352]{1,0:T(8,128)(2,1)S(1)}, bf16[40,4352]{1,0:T(8,128)(2,1)S(1)}, bf16[40,4352]{1,0:T(8,128)(2,1)S(1)}) custom-call(bf16[40,4352]{1,0:T(8,128)(2,1)S(1)} %copy-done.5, bf16[40,4352]{1,0:T(8,128)(2,1)S(1)} %collective-permute-done.refs_1_, bf16[40,4352]{1,0:T(8,128)(2,1)S(1)} %collective-permute-done.1.refs_2_, ...), custom_call_target="tpu_custom_call" | custom-call | flops 3623878656 | bytes 22020096 | tf_op jit(solution)/shard_map/ffn/pallas_call | solution.py:376
  168.3 2.8 %collective-permute-start.8 = (bf16[40,4352]{1,0:T(8,128)(2,1)S(1)}, bf16[40,4352]{1,0:T(8,128)(2,1)S(1)}, u32[]{:S(2)}, u32[]{:S(2)}) collective-permute-start(bf16[40,4352]{1,0:T(8,128)(2,1)S(1)} %get-tuple-element.47), channel_id=1, source_target_pairs={{0,6},{2,4},{4,2},{6,0},{8,14},{10,12},{12,10},{14,8},{16,22},{18,... | collective-permute-start | bytes 1044488 | tf_op jit(solution)/shard_map/ppermute | solution.py:416
  171.1 5.1 %attend.2.refs_4_ = f32[64,2048]{1,0:T(8,128)S(1)} custom-call(bf16[64,4096]{1,0:T(8,128)(2,1)} %q_ref.3, bf16[64,256]{1,0:T(8,128)(2,1)} %keys_ref.3, bf16[64,256]{1,0:T(8,128)(2,1)} %values_ref.3, bf16[1024,256]{1,0:T(8,128)(2,1)} %pkeys_ref.3, bf16[1024,256]{1,0:T(8,128)(2,1)} %pvalues_ref.3, bf16[64,4096]{1,0:T(8,128)(2,1)} %tokens_ref.5), custom_call_target="tpu_custom_call" | custom-call | flops 570425344 | bytes 1048576 | tf_op jit(solution)/shard_map/attend/pallas_call | solution.py:53
  176.2 5.1 %attend.3.refs_5_ = f32[64,2048]{1,0:T(8,128)S(1)} custom-call(bf16[64,4096]{1,0:T(8,128)(2,1)} %q_ref.3, bf16[64,256]{1,0:T(8,128)(2,1)} %keys_ref.3, bf16[64,256]{1,0:T(8,128)(2,1)} %values_ref.3, bf16[1024,256]{1,0:T(8,128)(2,1)} %pkeys_ref.3, bf16[1024,256]{1,0:T(8,128)(2,1)} %pvalues_ref.3, bf16[64,4096]{1,0:T(8,128)(2,1)} %tokens_ref.5), custom_call_target="tpu_custom_call" | custom-call | flops 570425344 | bytes 1048576 | tf_op jit(solution)/shard_map/attend/pallas_call | solution.py:53
  181.3 1.2 combine.4
  182.6 1.0 add_convert_fusion
  (55 shorter events, 4.0 us)
Async XLA Ops:
  0.0 68.1 %collective-permute-start.3 = (bf16[4096,384]{1,0:T(8,128)(2,1)}, bf16[4096,384]{1,0:T(8,128)(2,1)S(1)}, u32[]{:S(2)}, u32[]{:S(2)}) collective-permute-start(bf16[4096,384]{1,0:T(8,128)(2,1)} %bitcast.7), channel_id=1, source_target_pairs={{0,1},{1,0},{2,3},{3,2},{4,5},{5,4},{6,7},{7,6},{8,9},{9,8},{10,11... | collective-permute-start | bytes 9437192 | tf_op jit(solution)/shard_map/ppermute | solution.py:419
  0.0 70.7 %collective-permute-start.4 = (bf16[4096,384]{1,0:T(8,128)(2,1)}, bf16[4096,384]{1,0:T(8,128)(2,1)}, u32[]{:S(2)}, u32[]{:S(2)}) collective-permute-start(bf16[4096,384]{1,0:T(8,128)(2,1)} %bitcast.12), channel_id=1, source_target_pairs={{0,1},{1,0},{2,3},{3,2},{4,5},{5,4},{6,7},{7,6},{8,9},{9,8},{10,11... | collective-permute-start | bytes 9437192 | tf_op jit(solution)/shard_map/ppermute | solution.py:419
  0.5 70.7 %collective-permute-start.5 = (bf16[384,4096]{1,0:T(8,128)(2,1)}, bf16[384,4096]{1,0:T(8,128)(2,1)}, u32[]{:S(2)}, u32[]{:S(2)}) collective-permute-start(bf16[384,4096]{1,0:T(8,128)(2,1)} %bitcast.17), channel_id=1, source_target_pairs={{0,1},{1,0},{2,3},{3,2},{4,5},{5,4},{6,7},{7,6},{8,9},{9,8},{10,11... | collective-permute-start | bytes 9437192 | tf_op jit(solution)/shard_map/ppermute | solution.py:419
  0.5 16.5 %collective-permute-start.26 = (bf16[64,4096]{1,0:T(8,128)(2,1)}, bf16[64,4096]{1,0:T(8,128)(2,1)}, u32[]{:S(2)}, u32[]{:S(2)}) collective-permute-start(bf16[64,4096]{1,0:T(8,128)(2,1)} %tokens_ref.5), channel_id=1, source_target_pairs={{0,8},{2,10},{4,12},{6,14},{8,0},{10,2},{12,4},{14,6},{16,24},{18,... | collective-permute-start | bytes 1572872 | tf_op jit(solution)/shard_map/ppermute | solution.py:416
  4.3 11.2 %collective-permute-start.25 = (bf16[64,128]{1,0:T(8,128)(2,1)}, bf16[64,128]{1,0:T(8,128)(2,1)S(1)}, u32[]{:S(2)}, u32[]{:S(2)}) collective-permute-start(bf16[64,128]{1,0:T(8,128)(2,1)} %get-tuple-element.64), channel_id=1, source_target_pairs={{0,8},{2,10},{4,12},{6,14},{8,0},{10,2},{12,4},{14,6},{16,24},{18,... | collective-permute-start | bytes 49160 | tf_op jit(solution)/shard_map/ppermute | solution.py:416
  15.4 25.7 %collective-permute-start.9 = (bf16[64,4224]{1,0:T(8,128)(2,1)}, bf16[64,4224]{1,0:T(8,128)(2,1)S(1)}, u32[]{:S(2)}, u32[]{:S(2)}) collective-permute-start(bf16[64,4224]{1,0:T(8,128)(2,1)} %get-tuple-element.39.meta_ref), channel_id=1, source_target_pairs={{0,24},{2,26},{4,28},{6,30},{8,16},{10,18},{12,20},{14,22},{16,8},... | collective-permute-start | bytes 1622024 | tf_op jit(solution)/shard_map/ppermute | solution.py:416
  17.0 0.7 copy-start.6
  19.7 22.3 %collective-permute-start.27 = (bf16[40,4352]{1,0:T(8,128)(2,1)S(1)}, bf16[40,4352]{1,0:T(8,128)(2,1)S(1)}, u32[]{:S(2)}, u32[]{:S(2)}) collective-permute-start(bf16[40,4352]{1,0:T(8,128)(2,1)S(1)} %get-tuple-element.66), channel_id=1, source_target_pairs={{0,2},{2,0},{4,6},{6,4},{8,10},{10,8},{12,14},{14,12},{16,18},{18,... | collective-permute-start | bytes 1044488 | tf_op jit(solution)/shard_map/ppermute | solution.py:416
  41.1 13.3 %collective-permute-start.10 = (bf16[64,4224]{1,0:T(8,128)(2,1)S(1)}, bf16[64,4224]{1,0:T(8,128)(2,1)S(1)}, u32[]{:S(2)}, u32[]{:S(2)}) collective-permute-start(bf16[64,4224]{1,0:T(8,128)(2,1)S(1)} %collective-permute-done.9.base_ref.meta_ref), channel_id=1, source_target_pairs={{0,8},{2,10},{4,12},{6,14},{8,0},{10,2},{12,4},{14,6},{16,24},{18,... | collective-permute-start | bytes 1622024 | tf_op jit(solution)/shard_map/ppermute | solution.py:416
  42.0 9.3 %collective-permute-start.17 = (bf16[40,4352]{1,0:T(8,128)(2,1)S(1)}, bf16[40,4352]{1,0:T(8,128)(2,1)S(1)}, u32[]{:S(2)}, u32[]{:S(2)}) collective-permute-start(bf16[40,4352]{1,0:T(8,128)(2,1)S(1)} %get-tuple-element.57), channel_id=1, source_target_pairs={{0,2},{2,0},{4,6},{6,4},{8,10},{10,8},{12,14},{14,12},{16,18},{18,... | collective-permute-start | bytes 1044488 | tf_op jit(solution)/shard_map/ppermute | solution.py:416
  51.3 15.8 %collective-permute-start.18 = (bf16[40,4352]{1,0:T(8,128)(2,1)S(1)}, bf16[40,4352]{1,0:T(8,128)(2,1)S(1)}, u32[]{:S(2)}, u32[]{:S(2)}) collective-permute-start(bf16[40,4352]{1,0:T(8,128)(2,1)S(1)} %get-tuple-element.58), channel_id=1, source_target_pairs={{0,4},{2,6},{4,0},{6,2},{8,12},{10,14},{12,8},{14,10},{16,20},{18,... | collective-permute-start | bytes 1044488 | tf_op jit(solution)/shard_map/ppermute | solution.py:416
  54.5 13.2 %collective-permute-start.19 = (bf16[40,4352]{1,0:T(8,128)(2,1)S(1)}, bf16[40,4352]{1,0:T(8,128)(2,1)S(1)}, u32[]{:S(2)}, u32[]{:S(2)}) collective-permute-start(bf16[40,4352]{1,0:T(8,128)(2,1)S(1)} %get-tuple-element.59), channel_id=1, source_target_pairs={{0,6},{2,4},{4,2},{6,0},{8,14},{10,12},{12,10},{14,8},{16,22},{18,... | collective-permute-start | bytes 1044488 | tf_op jit(solution)/shard_map/ppermute | solution.py:416
  67.2 19.2 %collective-permute-start.11 = (bf16[40,4352]{1,0:T(8,128)(2,1)S(1)}, bf16[40,4352]{1,0:T(8,128)(2,1)S(1)}, u32[]{:S(2)}, u32[]{:S(2)}) collective-permute-start(bf16[40,4352]{1,0:T(8,128)(2,1)S(1)} %get-tuple-element.49), channel_id=1, source_target_pairs={{0,2},{2,0},{4,6},{6,4},{8,10},{10,8},{12,14},{14,12},{16,18},{18,... | collective-permute-start | bytes 1044488 | tf_op jit(solution)/shard_map/ppermute | solution.py:416
  67.7 25.9 %collective-permute-start.12 = (bf16[40,4352]{1,0:T(8,128)(2,1)S(1)}, bf16[40,4352]{1,0:T(8,128)(2,1)S(1)}, u32[]{:S(2)}, u32[]{:S(2)}) collective-permute-start(bf16[40,4352]{1,0:T(8,128)(2,1)S(1)} %get-tuple-element.50), channel_id=1, source_target_pairs={{0,4},{2,6},{4,0},{6,2},{8,12},{10,14},{12,8},{14,10},{16,20},{18,... | collective-permute-start | bytes 1044488 | tf_op jit(solution)/shard_map/ppermute | solution.py:416
  68.1 25.5 %collective-permute-start.13 = (bf16[40,4352]{1,0:T(8,128)(2,1)S(1)}, bf16[40,4352]{1,0:T(8,128)(2,1)S(1)}, u32[]{:S(2)}, u32[]{:S(2)}) collective-permute-start(bf16[40,4352]{1,0:T(8,128)(2,1)S(1)} %get-tuple-element.51), channel_id=1, source_target_pairs={{0,6},{2,4},{4,2},{6,0},{8,14},{10,12},{12,10},{14,8},{16,22},{18,... | collective-permute-start | bytes 1044488 | tf_op jit(solution)/shard_map/ppermute | solution.py:416
  70.7 37.8 %collective-permute-start.28 = (bf16[40,4352]{1,0:T(8,128)(2,1)S(1)}, bf16[40,4352]{1,0:T(8,128)(2,1)S(1)}, u32[]{:S(2)}, u32[]{:S(2)}) collective-permute-start(bf16[40,4352]{1,0:T(8,128)(2,1)S(1)} %get-tuple-element.67), channel_id=1, source_target_pairs={{0,4},{2,6},{4,0},{6,2},{8,12},{10,14},{12,8},{14,10},{16,20},{18,... | collective-permute-start | bytes 1044488 | tf_op jit(solution)/shard_map/ppermute | solution.py:416
  71.2 38.2 %collective-permute-start.29 = (bf16[40,4352]{1,0:T(8,128)(2,1)S(1)}, bf16[40,4352]{1,0:T(8,128)(2,1)S(1)}, u32[]{:S(2)}, u32[]{:S(2)}) collective-permute-start(bf16[40,4352]{1,0:T(8,128)(2,1)S(1)} %get-tuple-element.68), channel_id=1, source_target_pairs={{0,6},{2,4},{4,2},{6,0},{8,14},{10,12},{12,10},{14,8},{16,22},{18,... | collective-permute-start | bytes 1044488 | tf_op jit(solution)/shard_map/ppermute | solution.py:416
  72.7 1.9 %copy-start = (bf16[1,4096,384]{2,1,0:T(8,128)(2,1)S(1)}, bf16[1,4096,384]{2,1,0:T(8,128)(2,1)}, u32[]{:S(2)}) copy-start(bf16[1,4096,384]{2,1,0:T(8,128)(2,1)} %param.22) | copy-start | bytes 9437188
  74.6 1.9 %copy-start.2 = (bf16[1,4096,384]{2,1,0:T(8,128)(2,1)S(1)}, bf16[1,4096,384]{2,1,0:T(8,128)(2,1)}, u32[]{:S(2)}) copy-start(bf16[1,4096,384]{2,1,0:T(8,128)(2,1)} %param.23) | copy-start | bytes 9437188
  76.5 1.9 %copy-start.3 = (bf16[1,384,4096]{2,1,0:T(8,128)(2,1)S(1)}, bf16[1,384,4096]{2,1,0:T(8,128)(2,1)}, u32[]{:S(2)}) copy-start(bf16[1,384,4096]{2,1,0:T(8,128)(2,1)} %param.24) | copy-start | bytes 9437188
  86.4 32.3 %collective-permute-start.20 = (bf16[40,4352]{1,0:T(8,128)(2,1)S(1)}, bf16[40,4352]{1,0:T(8,128)(2,1)S(1)}, u32[]{:S(2)}, u32[]{:S(2)}) collective-permute-start(bf16[40,4352]{1,0:T(8,128)(2,1)S(1)} %get-tuple-element.61), channel_id=1, source_target_pairs={{0,2},{2,0},{4,6},{6,4},{8,10},{10,8},{12,14},{14,12},{16,18},{18,... | collective-permute-start | bytes 1044488 | tf_op jit(solution)/shard_map/ppermute | solution.py:416
  93.6 25.2 %collective-permute-start.21 = (bf16[40,4352]{1,0:T(8,128)(2,1)S(1)}, bf16[40,4352]{1,0:T(8,128)(2,1)S(1)}, u32[]{:S(2)}, u32[]{:S(2)}) collective-permute-start(bf16[40,4352]{1,0:T(8,128)(2,1)S(1)} %get-tuple-element.62), channel_id=1, source_target_pairs={{0,4},{2,6},{4,0},{6,2},{8,12},{10,14},{12,8},{14,10},{16,20},{18,... | collective-permute-start | bytes 1044488 | tf_op jit(solution)/shard_map/ppermute | solution.py:416
  93.6 27.2 %collective-permute-start.22 = (bf16[40,4352]{1,0:T(8,128)(2,1)S(1)}, bf16[40,4352]{1,0:T(8,128)(2,1)S(1)}, u32[]{:S(2)}, u32[]{:S(2)}) collective-permute-start(bf16[40,4352]{1,0:T(8,128)(2,1)S(1)} %get-tuple-element.63), channel_id=1, source_target_pairs={{0,6},{2,4},{4,2},{6,0},{8,14},{10,12},{12,10},{14,8},{16,22},{18,... | collective-permute-start | bytes 1044488 | tf_op jit(solution)/shard_map/ppermute | solution.py:416
  96.4 14.1 %copy-start.1 = (bf16[1,4096,384]{2,1,0:T(8,128)(2,1)S(1)}, bf16[1,4096,384]{2,1,0:T(8,128)(2,1)}, u32[]{:S(2)}) copy-start(bf16[1,4096,384]{2,1,0:T(8,128)(2,1)} %param.22) | copy-start | bytes 9437188
  108.5 15.0 %collective-permute-start.14 = (bf16[40,4352]{1,0:T(8,128)(2,1)S(1)}, bf16[40,4352]{1,0:T(8,128)(2,1)S(1)}, u32[]{:S(2)}, u32[]{:S(2)}) collective-permute-start(bf16[40,4352]{1,0:T(8,128)(2,1)S(1)} %get-tuple-element.53), channel_id=1, source_target_pairs={{0,2},{2,0},{4,6},{6,4},{8,10},{10,8},{12,14},{14,12},{16,18},{18,... | collective-permute-start | bytes 1044488 | tf_op jit(solution)/shard_map/ppermute | solution.py:416
  109.4 22.2 %collective-permute-start.15 = (bf16[40,4352]{1,0:T(8,128)(2,1)S(1)}, bf16[40,4352]{1,0:T(8,128)(2,1)S(1)}, u32[]{:S(2)}, u32[]{:S(2)}) collective-permute-start(bf16[40,4352]{1,0:T(8,128)(2,1)S(1)} %get-tuple-element.54), channel_id=1, source_target_pairs={{0,4},{2,6},{4,0},{6,2},{8,12},{10,14},{12,8},{14,10},{16,20},{18,... | collective-permute-start | bytes 1044488 | tf_op jit(solution)/shard_map/ppermute | solution.py:416
  110.5 24.4 %copy-start.9 = (bf16[40,4352]{1,0:T(8,128)(2,1)S(1)}, bf16[40,4352]{1,0:T(8,128)(2,1)}, u32[]{:S(2)}) copy-start(bf16[40,4352]{1,0:T(8,128)(2,1)} %get-tuple-element.41) | copy-start | bytes 1044484
  110.5 37.7 %copy-start.8 = (bf16[40,4352]{1,0:T(8,128)(2,1)S(1)}, bf16[40,4352]{1,0:T(8,128)(2,1)}, u32[]{:S(2)}) copy-start(bf16[40,4352]{1,0:T(8,128)(2,1)} %get-tuple-element.42) | copy-start | bytes 1044484
  110.5 37.9 %copy-start.7 = (bf16[40,4352]{1,0:T(8,128)(2,1)S(1)}, bf16[40,4352]{1,0:T(8,128)(2,1)}, u32[]{:S(2)}) copy-start(bf16[40,4352]{1,0:T(8,128)(2,1)} %get-tuple-element.43) | copy-start | bytes 1044484
  118.7 16.2 %collective-permute-start.30 = (bf16[40,4352]{1,0:T(8,128)(2,1)S(1)}, bf16[40,4352]{1,0:T(8,128)(2,1)S(1)}, u32[]{:S(2)}, u32[]{:S(2)}) collective-permute-start(bf16[40,4352]{1,0:T(8,128)(2,1)S(1)} %get-tuple-element.70), channel_id=1, source_target_pairs={{0,2},{2,0},{4,6},{6,4},{8,10},{10,8},{12,14},{14,12},{16,18},{18,... | collective-permute-start | bytes 1044488 | tf_op jit(solution)/shard_map/ppermute | solution.py:416
  118.8 29.4 %collective-permute-start.31 = (bf16[40,4352]{1,0:T(8,128)(2,1)S(1)}, bf16[40,4352]{1,0:T(8,128)(2,1)S(1)}, u32[]{:S(2)}, u32[]{:S(2)}) collective-permute-start(bf16[40,4352]{1,0:T(8,128)(2,1)S(1)} %get-tuple-element.71), channel_id=1, source_target_pairs={{0,4},{2,6},{4,0},{6,2},{8,12},{10,14},{12,8},{14,10},{16,20},{18,... | collective-permute-start | bytes 1044488 | tf_op jit(solution)/shard_map/ppermute | solution.py:416
  120.8 27.6 %collective-permute-start.32 = (bf16[40,4352]{1,0:T(8,128)(2,1)S(1)}, bf16[40,4352]{1,0:T(8,128)(2,1)S(1)}, u32[]{:S(2)}, u32[]{:S(2)}) collective-permute-start(bf16[40,4352]{1,0:T(8,128)(2,1)S(1)} %get-tuple-element.72), channel_id=1, source_target_pairs={{0,6},{2,4},{4,2},{6,0},{8,14},{10,12},{12,10},{14,8},{16,22},{18,... | collective-permute-start | bytes 1044488 | tf_op jit(solution)/shard_map/ppermute | solution.py:416
  122.3 37.0 %copy-start.5 = (bf16[40,4352]{1,0:T(8,128)(2,1)S(1)}, bf16[40,4352]{1,0:T(8,128)(2,1)}, u32[]{:S(2)}) copy-start(bf16[40,4352]{1,0:T(8,128)(2,1)} %get-tuple-element.40.refs_0_) | copy-start | bytes 1044484
  123.5 28.9 %collective-permute-start.23 = (bf16[64,4096]{1,0:T(8,128)(2,1)S(1)}, bf16[64,4096]{1,0:T(8,128)(2,1)S(1)}, u32[]{:S(2)}, u32[]{:S(2)}) collective-permute-start(bf16[64,4096]{1,0:T(8,128)(2,1)S(1)} %combine.5), channel_id=1, source_target_pairs={{0,8},{2,10},{4,12},{6,14},{8,0},{10,2},{12,4},{14,6},{16,24},{18,... | collective-permute-start | bytes 1572872 | tf_op jit(solution)/shard_map/ppermute | solution.py:416
  131.6 19.6 %collective-permute-start.16 = (bf16[40,4352]{1,0:T(8,128)(2,1)S(1)}, bf16[40,4352]{1,0:T(8,128)(2,1)S(1)}, u32[]{:S(2)}, u32[]{:S(2)}) collective-permute-start(bf16[40,4352]{1,0:T(8,128)(2,1)S(1)} %get-tuple-element.55), channel_id=1, source_target_pairs={{0,6},{2,4},{4,2},{6,0},{8,14},{10,12},{12,10},{14,8},{16,22},{18,... | collective-permute-start | bytes 1044488 | tf_op jit(solution)/shard_map/ppermute | solution.py:416
  134.9 20.0 %collective-permute-start = (bf16[40,4352]{1,0:T(8,128)(2,1)S(1)}, bf16[40,4352]{1,0:T(8,128)(2,1)S(1)}, u32[]{:S(2)}, u32[]{:S(2)}) collective-permute-start(bf16[40,4352]{1,0:T(8,128)(2,1)S(1)} %copy-done.9), channel_id=1, source_target_pairs={{0,2},{2,0},{4,6},{6,4},{8,10},{10,8},{12,14},{14,12},{16,18},{18,... | collective-permute-start | bytes 1044488 | tf_op jit(solution)/shard_map/ppermute | solution.py:416
  148.2 11.0 %collective-permute-start.1 = (bf16[40,4352]{1,0:T(8,128)(2,1)S(1)}, bf16[40,4352]{1,0:T(8,128)(2,1)S(1)}, u32[]{:S(2)}, u32[]{:S(2)}) collective-permute-start(bf16[40,4352]{1,0:T(8,128)(2,1)S(1)} %copy-done.8), channel_id=1, source_target_pairs={{0,4},{2,6},{4,0},{6,2},{8,12},{10,14},{12,8},{14,10},{16,20},{18,... | collective-permute-start | bytes 1044488 | tf_op jit(solution)/shard_map/ppermute | solution.py:416
  148.4 10.8 %collective-permute-start.2 = (bf16[40,4352]{1,0:T(8,128)(2,1)S(1)}, bf16[40,4352]{1,0:T(8,128)(2,1)S(1)}, u32[]{:S(2)}, u32[]{:S(2)}) collective-permute-start(bf16[40,4352]{1,0:T(8,128)(2,1)S(1)} %copy-done.7), channel_id=1, source_target_pairs={{0,6},{2,4},{4,2},{6,0},{8,14},{10,12},{12,10},{14,8},{16,22},{18,... | collective-permute-start | bytes 1044488 | tf_op jit(solution)/shard_map/ppermute | solution.py:416
  151.2 31.3 %collective-permute-start.33 = (bf16[64,4096]{1,0:T(8,128)(2,1)S(1)}, bf16[64,4096]{1,0:T(8,128)(2,1)S(1)}, u32[]{:S(2)}, u32[]{:S(2)}) collective-permute-start(bf16[64,4096]{1,0:T(8,128)(2,1)S(1)} %combine.7), channel_id=1, source_target_pairs={{0,8},{2,10},{4,12},{6,14},{8,0},{10,2},{12,4},{14,6},{16,24},{18,... | collective-permute-start | bytes 1572872 | tf_op jit(solution)/shard_map/ppermute | solution.py:416
  153.6 28.9 %collective-permute-start.24 = (bf16[64,4096]{1,0:T(8,128)(2,1)S(1)}, bf16[64,4096]{1,0:T(8,128)(2,1)S(1)}, u32[]{:S(2)}, u32[]{:S(2)}) collective-permute-start(bf16[64,4096]{1,0:T(8,128)(2,1)S(1)} %combine.6), channel_id=1, source_target_pairs={{0,16},{2,18},{4,20},{6,22},{8,24},{10,26},{12,28},{14,30},{16,0},... | collective-permute-start | bytes 1572872 | tf_op jit(solution)/shard_map/ppermute | solution.py:416
  167.5 13.8 %copy-start.4 = (bf16[64,4224]{1,0:T(8,128)(2,1)S(1)}, bf16[64,4224]{1,0:T(8,128)(2,1)}, u32[]{:S(2)}) copy-start(bf16[64,4224]{1,0:T(8,128)(2,1)} %get-tuple-element.39.meta_ref) | copy-start | bytes 1622020
  167.6 13.7 %collective-permute-start.6 = (bf16[40,4352]{1,0:T(8,128)(2,1)S(1)}, bf16[40,4352]{1,0:T(8,128)(2,1)S(1)}, u32[]{:S(2)}, u32[]{:S(2)}) collective-permute-start(bf16[40,4352]{1,0:T(8,128)(2,1)S(1)} %get-tuple-element.45), channel_id=1, source_target_pairs={{0,2},{2,0},{4,6},{6,4},{8,10},{10,8},{12,14},{14,12},{16,18},{18,... | collective-permute-start | bytes 1044488 | tf_op jit(solution)/shard_map/ppermute | solution.py:416
  167.9 13.3 %collective-permute-start.7 = (bf16[40,4352]{1,0:T(8,128)(2,1)S(1)}, bf16[40,4352]{1,0:T(8,128)(2,1)S(1)}, u32[]{:S(2)}, u32[]{:S(2)}) collective-permute-start(bf16[40,4352]{1,0:T(8,128)(2,1)S(1)} %get-tuple-element.46), channel_id=1, source_target_pairs={{0,4},{2,6},{4,0},{6,2},{8,12},{10,14},{12,8},{14,10},{16,20},{18,... | collective-permute-start | bytes 1044488 | tf_op jit(solution)/shard_map/ppermute | solution.py:416
  168.3 13.0 %collective-permute-start.8 = (bf16[40,4352]{1,0:T(8,128)(2,1)S(1)}, bf16[40,4352]{1,0:T(8,128)(2,1)S(1)}, u32[]{:S(2)}, u32[]{:S(2)}) collective-permute-start(bf16[40,4352]{1,0:T(8,128)(2,1)S(1)} %get-tuple-element.47), channel_id=1, source_target_pairs={{0,6},{2,4},{4,2},{6,0},{8,14},{10,12},{12,10},{14,8},{16,22},{18,... | collective-permute-start | bytes 1044488 | tf_op jit(solution)/shard_map/ppermute | solution.py:416
